TPU v7x, 32 devices: a whole 2x2x4 slice. The times are simulated.
32 devices in a mesh: section: 2 (over y), seq: 4 (over z), dp: 4 (over x, core).
Axes of the slice: x: 2, y: 2, z: 4, core: 2. Of those that a mesh axis runs over, the one named last changes fastest.
Arguments:
- ends_in: bfloat16 [2, 8, 256, 1024], P('section', 'dp', 'seq'), may hold values from -40 to 40
- segments: int32 [8, 256], P('dp', 'seq'), may hold values from 0 to 7, never falling along the last dimension, each value on 1 to 64 neighbouring positions
- qkv_weight: bfloat16 [2, 1024, 3072], P('section', 'dp'), may hold values from -2 to 2
- out_weight: bfloat16 [2, 1024, 1024], P('section', 'dp'), may hold values from -1 to 1
- up_weight: bfloat16 [2, 1024, 4096], P('section', 'dp'), may hold values from -0.1875 to 0.1875
- down_weight: bfloat16 [2, 4096, 1024], P('section', 'dp'), may hold values from -0.09375 to 0.09375
- gains: bfloat16 [2, 2, 1024], P('section', None, 'dp'), may hold values from 0.5 to 1.5
- shifts: bfloat16 [2, 6, 1024], P('section', None, 'dp'), may hold values from -3 to 3
- up_bias: bfloat16 [2, 4096], P('section', 'dp'), may hold values from -3 to 3
Outputs:
- ends_out: float32 [2, 8, 256, 1024], P('section', 'dp', 'seq')
- qkv_grad: float32 [2, 1024, 3072], P('section', 'dp')
- out_grad: float32 [2, 1024, 1024], P('section', 'dp')
- up_grad: float32 [2, 1024, 4096], P('section', 'dp')
- down_grad: float32 [2, 4096, 1024], P('section', 'dp')
- gains_grad: float32 [2, 2, 1024], P('section', None, 'dp')
- shifts_grad: float32 [2, 6, 1024], P('section', None, 'dp')
- up_bias_grad: float32 [2, 4096], P('section', 'dp')
Inputs may be any that keep to these rules, and one draw needn't show every extreme that they name: `segments`: segment numbers never fall along a sequence; every segment is 1 to 64 tokens long, one of them exactly that long.
All inputs are finite; a program needn't handle non-finite values.
Results may differ from a plain program's by a relative error of at most 0.019.
Values may be sent and summed in bfloat16 or wider, within the bound.
A program may use at most 256 MiB of HBM per device.

v0:
```python
import jax
import jax.numpy as jnp
from jax import lax
from jax.experimental import pallas as pl
from jax.experimental.pallas import tpu as pltpu
from jax.sharding import PartitionSpec as P

DH = 64


EPSILON = 1e-05
MASKED = -1e30


def passed_along(array, axis, by):
    count = lax.axis_size(axis)
    pairs = [(i, i + by) for i in range(count) if 0 <= i + by < count]
    return lax.ppermute(array, axis, pairs)


def layer_norm(row_values, gain_vec, shift_vec):
    center = row_values - jnp.mean(row_values, axis=-1, keepdims=True)
    spread = jnp.mean(center * center, axis=-1, keepdims=True)
    return center * lax.rsqrt(spread + EPSILON) * gain_vec + shift_vec


def smooth_gate(upper_act):
    return jax.nn.gelu(upper_act, approximate=True)


def masked_scores(query_heads, key_heads, full_segments):
    raw_scores = jnp.einsum(
        "sqhd,skhd->shqk", query_heads, key_heads, preferred_element_type=jnp.float32
    ) * DH ** (-0.5)
    positions = lax.iota(jnp.int32, key_heads.shape[1])
    causal = (positions[None, :] <= positions[:, None])[None, None]
    same_doc = full_segments[:, None, :, None] == full_segments[:, None, None, :]
    return jnp.where(causal & same_doc, raw_scores, MASKED)


def split_heads(head_view):
    seq_count, length = head_view.shape[:2]
    local_view = head_view.reshape(seq_count, length, 3, -1, DH)
    return (local_view[:, :, 0], local_view[:, :, 1], local_view[:, :, 2])


def attend(head_view, full_segments):
    seq_count, length = head_view.shape[:2]
    query_heads, key_heads, value_heads = split_heads(head_view)
    scores = masked_scores(query_heads, key_heads, full_segments)
    row_max = jnp.max(scores, axis=-1, keepdims=True)
    log_total = jnp.log(jnp.sum(jnp.exp(scores - row_max), axis=-1, keepdims=True)) + row_max
    weights = jnp.exp(scores - log_total).astype(jnp.bfloat16)
    attended = jnp.einsum(
        "shqk,skhd->sqhd", weights, value_heads, preferred_element_type=jnp.float32
    ).astype(jnp.bfloat16)
    return (attended.reshape(seq_count, length, 1, -1), log_total)


def attend_grad(head_view, attended, log_total, heads_grad, full_segments):
    seq_count, length = head_view.shape[:2]
    query_heads, key_heads, value_heads = split_heads(head_view)
    out_heads = attended.reshape(seq_count, length, -1, DH)
    grads_in = heads_grad.reshape(seq_count, length, -1, DH)
    row_delta = jnp.moveaxis(
        jnp.sum(grads_in.astype(jnp.float32) * out_heads.astype(jnp.float32), axis=-1), 1, 2
    )[..., None]
    score_scale = DH ** (-0.5)
    scores = masked_scores(query_heads, key_heads, full_segments)
    weights = jnp.exp(scores - log_total)
    values_grad = jnp.einsum(
        "shqk,sqhd->skhd",
        weights.astype(jnp.bfloat16),
        grads_in,
        preferred_element_type=jnp.float32,
    )
    weights_grad = jnp.einsum(
        "sqhd,skhd->shqk", grads_in, value_heads, preferred_element_type=jnp.float32
    )
    scores_grad = (weights * (weights_grad - row_delta)).astype(jnp.bfloat16)
    query_grad = (
        jnp.einsum("shqk,skhd->sqhd", scores_grad, key_heads, preferred_element_type=jnp.float32)
        * score_scale
    )
    keys_grad = (
        jnp.einsum("shqk,sqhd->skhd", scores_grad, query_heads, preferred_element_type=jnp.float32)
        * score_scale
    )
    joined = jnp.stack([query_grad, keys_grad, values_grad], axis=2).astype(jnp.bfloat16)
    return joined.reshape(seq_count, length, 1, -1)


def to_heads(rows):
    return lax.all_to_all(rows, "seq", split_axis=2, concat_axis=1, tiled=True)


def to_tokens(heads):
    return lax.all_to_all(heads, "seq", split_axis=1, concat_axis=2, tiled=True)


def forward(entry_rows, params, full_segments):
    qkv_w, out_w, up_w, down_w, gain_vecs, vectors, up_vec = params
    seq_count, tok_count, width = entry_rows.shape
    groups = lax.axis_size("seq")
    row_values = entry_rows.reshape(-1, width).astype(jnp.float32)
    normed = layer_norm(row_values, gain_vecs[0], vectors[0]).astype(jnp.bfloat16)
    qkv_bias = jnp.concatenate([vectors[1], jnp.zeros_like(vectors[1]), vectors[2]])
    projected = (jnp.dot(normed, qkv_w, preferred_element_type=jnp.float32) + qkv_bias).astype(
        jnp.bfloat16
    )
    grouped = projected.reshape(seq_count, tok_count, 3, groups, width // groups)
    grouped = grouped.transpose(0, 1, 3, 2, 4).reshape(seq_count, tok_count, groups, -1)
    head_view = to_heads(grouped)
    attended, log_total = attend(head_view, full_segments)
    mixed = to_tokens(attended).reshape(-1, width)
    residual = row_values + jnp.dot(mixed, out_w, preferred_element_type=jnp.float32) + vectors[3]
    normed_two = layer_norm(residual, gain_vecs[1], vectors[4]).astype(jnp.bfloat16)
    upper_act = jnp.dot(normed_two, up_w, preferred_element_type=jnp.float32) + up_vec
    hidden = smooth_gate(upper_act).astype(jnp.bfloat16)
    output = residual + jnp.dot(hidden, down_w, preferred_element_type=jnp.float32) + vectors[5]
    return (output, (normed, head_view, attended, log_total, mixed, residual, normed_two, upper_act))


def backward(incoming, entry_rows, params, saved, full_segments, beside=None):
    qkv_w, out_w, up_w, down_w, gain_vecs, vectors, up_vec = params
    normed, head_view, attended, log_total, mixed, residual, normed_two, upper_act = saved
    seq_count, tok_count, width = entry_rows.shape
    groups = lax.axis_size("seq")
    grad_rows = incoming.reshape(-1, width)
    upstream = grad_rows.astype(jnp.float32)
    down_bias_g = jnp.sum(upstream, axis=0)
    hidden_g = jnp.einsum("rd,fd->rf", grad_rows, down_w, preferred_element_type=jnp.float32)
    upper_g = jax.vjp(smooth_gate, upper_act)[1](hidden_g)[0]
    up_bias_g = jnp.sum(upper_g, axis=0)
    normed_two_g = jnp.einsum(
        "rf,df->rd", upper_g.astype(jnp.bfloat16), up_w, preferred_element_type=jnp.float32
    )
    norm_back = jax.vjp(layer_norm, residual, gain_vecs[1], vectors[4])[1]
    residual_part, gain_two_g, shift_two_g = norm_back(normed_two_g)
    residual_g = upstream + residual_part
    residual_round = residual_g.astype(jnp.bfloat16)
    out_bias_g = jnp.sum(residual_g, axis=0)
    mixed_g = jnp.einsum(
        "re,de->rd", residual_round, out_w, preferred_element_type=jnp.float32
    ).astype(jnp.bfloat16)
    heads_grad = to_heads(mixed_g.reshape(seq_count, tok_count, groups, width // groups))
    joined_heads = attend_grad(head_view, attended, log_total, heads_grad, full_segments)
    if beside is not None:
        joined_heads, beside = lax.optimization_barrier((joined_heads, beside))
    token_grads = to_tokens(joined_heads)
    joined = token_grads.reshape(seq_count, tok_count, groups, 3, width // groups)
    joined = joined.transpose(0, 1, 3, 2, 4).reshape(-1, 3 * width)
    column_sums = jnp.sum(joined.astype(jnp.float32), axis=0)
    normed_g = jnp.einsum("re,de->rd", joined, qkv_w, preferred_element_type=jnp.float32)
    row_values = entry_rows.reshape(-1, width).astype(jnp.float32)
    entry_back = jax.vjp(layer_norm, row_values, gain_vecs[0], vectors[0])[1]
    entry_part, gain_one_g, shift_one_g = entry_back(normed_g)
    vector_grads = (
        jnp.stack([gain_one_g, gain_two_g]),
        jnp.stack(
            [
                shift_one_g,
                column_sums[:width],
                column_sums[2 * width :],
                out_bias_g,
                shift_two_g,
                down_bias_g,
            ]
        ),
        up_bias_g[None],
    )
    return (residual_g + entry_part, residual_round, joined_heads, vector_grads, beside)


def rounded_blocks(partial):
    owners = lax.axis_size("dp")
    return partial.reshape(owners, -1, partial.shape[1]).astype(jnp.bfloat16)


def summed_blocks(blocks):
    return lax.psum_scatter(
        blocks.reshape(-1, blocks.shape[2]), "dp", scatter_dimension=0, tiled=True
    )


def gathered_parts(own):
    return lax.all_gather(own, "seq", axis=0, tiled=False)


def own_columns(array, outer, inner):
    index = lax.axis_index("seq")
    rows = array.shape[0]
    parts = array.reshape(rows, outer, inner, -1)
    return lax.dynamic_index_in_dim(parts, index, 2, keepdims=False).reshape(rows, -1)


def own_rows(array, outer, inner):
    index = lax.axis_index("seq")
    columns = array.shape[1]
    parts = array.reshape(outer, inner, -1, columns)
    return lax.dynamic_index_in_dim(parts, index, 1, keepdims=False).reshape(-1, columns)


def feed_forward_grads(normed_two, incoming, params):
    up_w, down_w, up_vec = params[2], params[3], params[6]
    outer, inner = lax.axis_size("dp"), lax.axis_size("seq")
    up_part = own_columns(up_w, outer, inner)
    down_part = own_rows(down_w, outer, inner)
    bias_part = own_columns(up_vec[None], outer, inner)[0]
    upper_act = jnp.dot(normed_two, up_part, preferred_element_type=jnp.float32) + bias_part
    hidden_f, gate_back = jax.vjp(smooth_gate, upper_act)
    hidden = hidden_f.astype(jnp.bfloat16)
    hidden_g = jnp.einsum("rd,fd->rf", incoming, down_part, preferred_element_type=jnp.float32)
    upper_round = gate_back(hidden_g)[0].astype(jnp.bfloat16)
    down_g = jnp.einsum("rf,rd->fd", hidden, incoming, preferred_element_type=jnp.float32)
    up_g = jnp.einsum("rd,rf->df", normed_two, upper_round, preferred_element_type=jnp.float32)
    return (up_g, down_g)


def joined_columns(parts, outer_columns):
    inner, rows, columns = parts.shape
    ordered = parts.reshape(inner, rows, outer_columns, -1).transpose(1, 2, 0, 3)
    return ordered.reshape(rows, inner * columns).astype(jnp.float32)


def gathered_rows(values):
    return lax.all_gather(values, "seq", axis=0, tiled=True)


def by_owner(array, owners):
    rows, columns = array.shape
    return array.reshape(rows, owners, -1).transpose(1, 0, 2).reshape(owners, -1)


def piece_plan(shapes):
    return [
        (which, part * (rows // (2 * pieces)), rows // (2 * pieces), rows // 2)
        for which, (rows, columns) in enumerate(shapes)
        for pieces in (2 if rows * columns > 512 * 1024 else 1,)
        for part in range(pieces)
    ]


def gather_kernel(plan, count, *refs):
    own, full = refs[:count], refs[count : 2 * count]
    (local_sem, own_send, own_recv, far_send, far_recv) = refs[2 * count : 2 * count + 5]
    (side_send, side_recv, near_send, near_recv, last_send, last_recv) = refs[2 * count + 5 :]
    me, place = lax.axis_index("dp"), lax.axis_index("seq")
    far = lax.rem(me + 2, 4)
    near = me + 1 - 2 * lax.rem(me, 2)
    half = lax.rem(place, 2)
    side = place + 1 - 2 * half
    barrier = pltpu.get_barrier_semaphore()
    for target in ({"dp": far}, {"dp": near}, {"seq": side}):
        pl.semaphore_signal(
            barrier, inc=1, device_id=target, device_id_type=pl.DeviceIdType.MESH
        )
    pl.semaphore_wait(barrier, 3)

    def rows_at(which_half, first, rows, half_rows):
        return pl.ds(pl.multiple_of(which_half * half_rows + first, rows), rows)

    def remote(source, target, send, recv, device):
        return pltpu.make_async_remote_copy(
            src_ref=source,
            dst_ref=target,
            send_sem=send,
            recv_sem=recv,
            device_id=device,
            device_id_type=pl.DeviceIdType.MESH,
        )

    far_copies, side_copies, near_copies, last_copies = [], [], [], []
    for index, (which, first, rows, half_rows) in enumerate(plan):
        span = rows_at(half, first, rows, half_rows)
        copy = remote(
            own[which].at[span],
            full[which].at[me, span],
            far_send.at[index],
            far_recv.at[index],
            {"dp": far},
        )
        copy.start()
        far_copies.append(copy)
    own_copies, local_copies = [], []
    for which in range(count):
        copy = remote(
            own[which], full[which].at[me], own_send.at[which], own_recv.at[which], {"dp": near}
        )
        copy.start()
        own_copies.append(copy)
        copy = pltpu.make_async_copy(own[which], full[which].at[me], local_sem.at[which])
        copy.start()
        local_copies.append(copy)

    def last_step(index):
        which, first, rows, half_rows = plan[index]
        side_copies[index].wait_recv()
        block = full[which].at[far, rows_at(1 - half, first, rows, half_rows)]
        copy = remote(block, block, last_send.at[index], last_recv.at[index], {"dp": near})
        copy.start()
        last_copies.append(copy)

    for index, (which, first, rows, half_rows) in enumerate(plan):
        far_copies[index].wait_recv()
        block = full[which].at[far, rows_at(half, first, rows, half_rows)]
        copy = remote(block, block, side_send.at[index], side_recv.at[index], {"seq": side})
        copy.start()
        side_copies.append(copy)
        copy = remote(block, block, near_send.at[index], near_recv.at[index], {"dp": near})
        copy.start()
        near_copies.append(copy)
        if index > 0:
            last_step(index - 1)
    last_step(len(plan) - 1)
    for copy in near_copies + last_copies + own_copies:
        copy.wait_recv()
    for copy in far_copies + side_copies + near_copies + last_copies + own_copies:
        copy.wait_send()
    for copy in local_copies:
        copy.wait()


def gathered_weights(weights):
    owners, places = lax.axis_size("dp"), lax.axis_size("seq")
    if owners != 4 or places % 2:
        return [lax.all_gather(weight, "dp", axis=0, tiled=True) for weight in weights]
    plan = piece_plan([weight.shape for weight in weights])
    count, pieces = len(weights), len(plan)
    dma = pltpu.SemaphoreType.DMA
    full = pl.pallas_call(
        lambda *refs: gather_kernel(plan, count, *refs),
        out_shape=[jax.ShapeDtypeStruct((owners,) + w.shape, w.dtype) for w in weights],
        in_specs=[pl.BlockSpec(memory_space=pltpu.VMEM)] * count,
        out_specs=[pl.BlockSpec(memory_space=pl.ANY)] * count,
        scratch_shapes=[dma((count,))] * 3 + [dma((pieces,))] * 8,
        compiler_params=pltpu.CompilerParams(collective_id=0, has_side_effects=True),
        name="gather_weights",
    )(*weights)
    return [whole.reshape(-1, whole.shape[2]) for whole in full]


def shards(
    ends_in, segments, qkv_weight, out_weight, up_weight, down_weight, gains, shifts, up_bias
):
    section_index = lax.axis_index("section")
    leading = section_index == 0
    outer, inner = lax.axis_size("dp"), lax.axis_size("seq")
    own_slot = ends_in[0]
    seq_count, tok_count, width = own_slot.shape
    share = width // outer
    packed = jnp.concatenate([gains[0].reshape(-1), shifts[0].reshape(-1), up_bias[0]])
    packed = lax.all_gather(packed, "dp", axis=0, tiled=False).astype(jnp.float32)
    gain_count, shift_count = gains.shape[1], shifts.shape[1]

    def rows_of(first, count):
        part = packed[:, first * share : (first + count) * share]
        return part.reshape(outer, count, share).transpose(1, 0, 2).reshape(count, width)

    params = (
        *gathered_weights((qkv_weight[0], out_weight[0], up_weight[0], down_weight[0])),
        rows_of(0, gain_count),
        rows_of(gain_count, shift_count),
        packed[:, (gain_count + shift_count) * share :].reshape(-1),
    )
    full_segments = lax.all_gather(segments, "seq", axis=1, tiled=True)

    first_output = forward(own_slot, params, full_segments)[0]
    received = passed_along(
        first_output.astype(jnp.bfloat16).reshape(own_slot.shape), "section", 1
    )
    entry_rows = jnp.where(leading, own_slot, received)
    last_output, saved = forward(entry_rows, params, full_segments)
    normed, head_view, attended, log_total, mixed, residual, normed_two, upper_act = saved
    tokens_in = gathered_rows(jnp.concatenate([normed, normed_two, mixed], axis=1))
    early_entry = backward(own_slot, entry_rows, params, saved, full_segments)[0]
    early_entry, tokens_in = lax.optimization_barrier((early_entry, tokens_in))
    all_normed = tokens_in[:, :width]
    all_normed_two = tokens_in[:, width : 2 * width]
    all_mixed = tokens_in[:, 2 * width :]
    returned = passed_along(
        early_entry.astype(jnp.bfloat16).reshape(own_slot.shape), "section", -1
    )
    incoming = jnp.where(leading, returned, own_slot)
    all_incoming = gathered_rows(incoming.reshape(-1, width))
    up_g, down_g = feed_forward_grads(all_normed_two, all_incoming, params)
    up_columns = up_g.shape[1]
    gate_blocks = jnp.concatenate(
        [rounded_blocks(up_g), rounded_blocks(down_g.reshape(width, -1))], axis=2
    )
    entry_g, residual_round, joined_heads, vector_grads, gate_blocks = backward(
        incoming, entry_rows, params, saved, full_segments, gate_blocks
    )
    gate_own = summed_blocks(gate_blocks)
    residual_part = lax.all_to_all(
        residual_round.reshape(-1, inner, width // inner),
        "seq",
        split_axis=1,
        concat_axis=0,
        tiled=True,
    ).reshape(-1, width // inner)
    out_g = jnp.einsum("rd,re->de", all_mixed, residual_part, preferred_element_type=jnp.float32)
    joined_part = joined_heads.reshape(seq_count, inner, tok_count, -1).transpose(1, 0, 2, 3)
    joined_part = joined_part.reshape(seq_count * inner * tok_count, -1)
    qkv_g = jnp.einsum("rd,re->de", all_normed, joined_part, preferred_element_type=jnp.float32)
    matrix_part = jnp.concatenate([rounded_blocks(qkv_g), rounded_blocks(out_g)], axis=2)
    vectors_g = jnp.concatenate([by_owner(part, outer) for part in vector_grads], axis=1)
    columns, vector_size = matrix_part.shape[2], vectors_g.shape[1]
    vector_rows = -(-vector_size // (16 * columns)) * 16
    vectors_g = jnp.pad(vectors_g, ((0, 0), (0, vector_rows * columns - vector_size)))
    vectors_g = rounded_blocks(vectors_g.reshape(-1, columns))
    last_blocks = jnp.concatenate([matrix_part, vectors_g], axis=1)
    last_blocks, gate_own = lax.optimization_barrier((last_blocks, gate_own))
    gate_parts = gathered_parts(gate_own)
    last_own, gate_parts = lax.optimization_barrier((summed_blocks(last_blocks), gate_parts))
    up_total = joined_columns(gate_parts[:, :, :up_columns], outer)
    down_total = gate_parts[:, :, up_columns:].reshape(-1, width).astype(jnp.float32)
    parts = gathered_parts(last_own)
    qkv_columns = qkv_g.shape[1]
    qkv_total = joined_columns(parts[:, :share, :qkv_columns], 3)
    out_total = joined_columns(parts[:, :share, qkv_columns:], 1)
    own_vectors = jnp.sum(parts[:, share:].astype(jnp.float32), axis=0).reshape(-1)
    gains_total = own_vectors[: gain_count * share].reshape(gain_count, share)
    shifts_total = own_vectors[gain_count * share : (gain_count + shift_count) * share]
    shifts_total = shifts_total.reshape(shift_count, share)
    up_bias_total = own_vectors[(gain_count + shift_count) * share : vector_size]

    ends_out = jnp.where(leading, entry_g, last_output).reshape(own_slot.shape)[None]
    return (
        ends_out,
        qkv_total[None],
        out_total[None],
        up_total[None],
        down_total[None],
        gains_total[None],
        shifts_total[None],
        up_bias_total[None],
    )


def solution(mesh):
    in_specs = (
        P("section", "dp", "seq", None),
        P("dp", "seq"),
        P("section", "dp", None),
        P("section", "dp", None),
        P("section", "dp", None),
        P("section", "dp", None),
        P("section", None, "dp"),
        P("section", None, "dp"),
        P("section", "dp"),
    )
    out_specs = (
        P("section", "dp", "seq", None),
        P("section", "dp", None),
        P("section", "dp", None),
        P("section", "dp", None),
        P("section", "dp", None),
        P("section", None, "dp"),
        P("section", None, "dp"),
        P("section", "dp"),
    )
    return jax.shard_map(shards, mesh=mesh, in_specs=in_specs, out_specs=out_specs, check_vma=False)
```

profile of v0, /device:TPU:0, one launch (start us, length us, event | category | flops | bytes accessed | tf_op | source)
XLA Modules:
  0.0 699.1 jit_solution(360932382943544068)
XLA Ops:
  9.3 6.2 all-gather
  19.1 89.8 %gather_weights.1 = (bf16[4,256,3072]{2,1,0:T(8,128)(2,1)}, bf16[4,256,1024]{2,1,0:T(8,128)(2,1)}, bf16[4,256,4096]{2,1,0:T(8,128)(2,1)}, bf16[4,1024,1024]{2,1,0:T(8,128)(2,1)}) custom-call(bf16[256,3072]{1,0:T(8,128)(2,1)} %bitcast.392, bf16[256,1024]{1,0:T(8,128)(2,1)} %bitcast.404, bf16[256,4096]{1,0:T(8,128)(2,1)} %bitcast.384, bf16[1024,1024]{1,0:T(8,128)(2,1)} %bitcast.385), custom_call_target="tpu_custom_call" | custom-call | tf_op jit(solution)/shard_map/gather_weights/pallas_call | solution.py:331
  120.3 19.3 %all-gather.3 = s32[4,64,2]{1,2,0:T(2,128)S(1)} all-gather(s32[1,64,2]{1,2,0:T(2,128)S(1)} %bitcast.453), channel_id=1, replica_groups=mesh['section'=2,'seq'=4,'dp'=4] {'seq'}, dimensions={0}, use_global_device_ids=true | all-gather | bytes 2560 | tf_op jit(solution)/shard_map/all_gather | solution.py:366
  150.9 6.7 all-to-all-done.1
  158.7 10.5 %fusion.28 = bf16[128,1024]{1,0:T(8,128)(2,1)S(1)} fusion(f32[128,1024]{1,0:T(8,128)S(1)} %get-tuple-element.117, bf16[4096,1024]{1,0:T(8,128)(2,1)} %bitcast.341, bf16[1024,4096]{1,0:T(8,128)(2,1)} %bitcast.337, f32[4096]{0:T(1024)S(1)} %bitcast.430, f32[1024]{0:T(1024)S(1)} %bitcast.443, f32[1024]{0:T(1024)S(1)} %bitcast.445, f32[1024]{0:T(1024)S(1)} %bitcast.425, ...), kind=kOutput, calls=%fused_computation.71 | convolution fusion | flops 2153775104 | bytes 17593344 | tf_op jit(solution)/shard_map/dot_general | solution.py:120
  183.0 19.3 %all_to_all.135 = bf16[2,64,4,768]{3,1,0,2:T(8,128)(2,1)S(1)} all-to-all(bf16[2,64,4,768]{3,1,0,2:T(8,128)(2,1)S(1)} %copy.207), channel_id=1, replica_groups=mesh['section'=2,'seq'=4,'dp'=4] {'seq'}, dimensions={2} | all-to-all | bytes 1572864 | tf_op jit(solution)/shard_map/all_to_all | solution.py:94
  211.2 10.8 %all_to_all.136 = bf16[2,256,1,256]{3,0,2,1:T(2,128)(2,1)S(1)} all-to-all(bf16[2,256,1,256]{3,0,2,1:T(2,128)(2,1)} %copy.213), channel_id=1, replica_groups=mesh['section'=2,'seq'=4,'dp'=4] {'seq'}, dimensions={1} | all-to-all | bytes 524288 | tf_op jit(solution)/shard_map/all_to_all | solution.py:98
  224.2 7.9 %convolution_add_fusion = f32[128,4096]{0,1:T(8,128)} fusion(bf16[128,1024]{1,0:T(8,128)(2,1)S(1)} %add_convert_fusion.2, bf16[1024,4096]{1,0:T(8,128)(2,1)} %bitcast.338, f32[4096]{0:T(1024)S(1)} %bitcast.431), kind=kOutput, calls=%fused_computation.1 | convolution fusion | flops 1074266112 | bytes 10764288 | tf_op jit(solution)/shard_map/dot_general | solution.py:118
  232.0 15.8 %multiply_reduce_fusion.5 = (f32[128]{0:T(128)S(1)}, f32[128,1024]{1,0:T(8,128)}) fusion(f32[128,1024]{1,0:T(8,128)S(1)} %get-tuple-element.121, f32[128]{0:T(128)S(1)} %broadcast_multiply_fusion.2, f32[1024]{0:T(1024)S(1)} %bitcast.427, bf16[1024,4096]{1,0:T(8,128)(2,1)} %bitcast.339, f32[128,4096]{0,1:T(8,128)} %convolution_add_fusion, ...), kind=kOutput, calls=%fused_computation.145 | convolution fusion | flops 2158493696 | bytes 20190208 | tf_op jit(solution)/shard_map/rf,df->rd/dot_general | solution.py:135
  256.0 10.6 %all_to_all.137 = bf16[2,64,4,256]{3,1,0,2:T(8,128)(2,1)} all-to-all(bf16[2,64,4,256]{3,1,0,2:T(8,128)(2,1)S(1)} %copy.217), channel_id=1, replica_groups=mesh['section'=2,'seq'=4,'dp'=4] {'seq'}, dimensions={2} | all-to-all | bytes 524288 | tf_op jit(solution)/shard_map/all_to_all | solution.py:94
  283.6 15.9 %all-to-all-done.5 = bf16[2,256,1,768]{3,0,2,1:T(2,128)(2,1)} async-done(((bf16[2,256,1,768]{3,0,2,1:T(2,128)(2,1)}), bf16[2,256,1,768]{3,0,2,1:T(2,128)(2,1)}, u32[]{:S(2)}, u32[]{:S(2)}) %all-to-all-start.5) | async-done | bytes 786464 | tf_op jit(solution)/shard_map/all_to_all | solution.py:98
  318.1 14.7 %reshape_reshape.8 = bf16[1024,4,4,256]{3,2,1,0:T(4,128)(2,1)} reshape(bf16[4,256,4096]{2,1,0:T(8,128)(2,1)} %get-tuple-element.23) | data formatting | bytes 16777216 | tf_op jit(solution)/shard_map/reshape;reshape | solution.py:193
  334.3 45.6 %all-gather.9.cloned.1.call-done = bf16[512,3072]{1,0:T(8,128)(2,1)} async-done(((bf16[128,3072]{1,0:T(8,128)(2,1)}), bf16[512,3072]{1,0:T(8,128)(2,1)}) %all-gather.9.cloned.1.call-update) | async-done | bytes 3145744 | tf_op jit(solution)/shard_map/all_gather | solution.py:227
  381.4 9.7 %constant_dynamic-slice_fusion.1 = bf16[1024,4,1,256]{3,2,1,0:T(2,128)(2,1)} fusion(bf16[1024,4,4,256]{3,2,1,0:T(4,128)(2,1)} %reshape_reshape.8, s32[]{:T(128)S(6)} %select_n.43), kind=kLoop, calls=%fused_computation.193 | loop fusion | bytes 4194308 | tf_op jit(solution)/shard_map/jit(dynamic_index_in_dim)/dynamic_slice | solution.py:194
  395.4 8.1 %fusion.127 = (bf16[4096]{0:T(1024)(128)(2,1)S(1)}, bf16[128,4096]{0,1:T(8,128)(2,1)}) fusion(f32[128,4096]{0,1:T(8,128)} %convolution_add_fusion, bf16[128,1024]{1,0:T(8,128)(2,1)S(1)} %bitcast.377, bf16[4096,1024]{1,0:T(8,128)(2,1)} %bitcast.344), kind=kOutput, calls=%fused_computation.243 | convolution fusion | flops 1084747776 | bytes 11804672 | tf_op jit(solution)/shard_map/rd,fd->rf/dot_general | solution.py:132
  403.5 6.7 multiply_reduce_fusion
  421.4 10.5 %copy.290 = bf16[1024,4,1,256]{0,3,1,2:T(8,128)(2,1)} copy(bf16[1024,4,1,256]{3,2,1,0:T(2,128)(2,1)} %constant_dynamic-slice_fusion.1) | data formatting | bytes 4194304
  450.8 7.2 %convolution_convert_fusion.1 = bf16[1024,1024]{1,0:T(8,128)(2,1)} fusion(f32[512,1024]{1,0:T(8,128)} %fusion.59, f32[1024]{0:T(1024)S(1)} %bitcast.451, bf16[512,3072]{1,0:T(8,128)(2,1)} %all-gather.9.cloned.1.call-done, bf16[512,1024]{1,0:T(8,128)(2,1)S(1)} %copy-done.30, bf16[1024,1024]{1,0:T(8,128)(2,1)} %bitcast.387), kind=kOutput, calls=%fused_computation.51 | convolution fusion | flops 2159542272 | bytes 8392704 | tf_op jit(solution)/shard_map/rd,rf->df/dot_general | solution.py:216
  470.8 6.6 all-to-all-done.8
  514.7 31.0 %reduce-scatter.5.cloned.1.call-done = bf16[272,1024]{1,0:T(8,128)(2,1)} async-done(((bf16[1088,1024]{1,0:T(8,128)(2,1)}), bf16[272,1024]{1,0:T(8,128)(2,1)}) %reduce-scatter.5.cloned.1.call-update) | async-done | bytes 557072 | tf_op jit(solution)/shard_map/reduce_scatter | solution.py:181
  545.6 82.2 %all-gather.13.cloned.1.call-done = bf16[1024,2048]{1,0:T(8,128)(2,1)} async-done(((bf16[256,2048]{1,0:T(8,128)(2,1)}), bf16[1024,2048]{1,0:T(8,128)(2,1)}) %all-gather.13.cloned.1.call-update) | async-done | bytes 4194320 | tf_op jit(solution)/shard_map/all_gather | solution.py:187
  627.9 6.2 add_select_fusion
  642.4 6.9 copy.305
  657.6 18.0 %all-gather.15.cloned.1.call-done = bf16[1088,1024]{1,0:T(8,128)(2,1)} async-done(((bf16[272,1024]{1,0:T(8,128)(2,1)}), bf16[1088,1024]{1,0:T(8,128)(2,1)}) %all-gather.15.cloned.1.call-update) | async-done | bytes 2228240 | tf_op jit(solution)/shard_map/all_gather | solution.py:187
  (268 shorter events, 217.3 us)
Async XLA Ops:
  113.7 6.7 copy-start.29
  115.6 25.5 %all-to-all-start = ((bf16[2,64,4,768]{3,1,0,2:T(8,128)(2,1)}), bf16[2,64,4,768]{3,1,0,2:T(8,128)(2,1)S(1)}, u32[]{:S(2)}, u32[]{:S(2)}) async-start(bf16[2,64,4,768]{3,1,0,2:T(8,128)(2,1)} %copy.195), calls=%async_computation | async-start | bytes 1572864 | tf_op jit(solution)/shard_map/all_to_all | solution.py:94
  144.2 13.7 %copy-start = (bf16[4,256,1024]{2,1,0:T(8,128)(2,1)S(1)}, bf16[4,256,1024]{2,1,0:T(8,128)(2,1)}, u32[]{:S(2)}) copy-start(bf16[4,256,1024]{2,1,0:T(8,128)(2,1)} %get-tuple-element.22) | copy-start | bytes 6291460
  144.2 13.7 %copy-start.3 = (bf16[1,2,64,1024]{3,2,1,0:T(8,128)(2,1)S(1)}, bf16[1,2,64,1024]{3,2,1,0:T(8,128)(2,1)}, u32[]{:S(2)}) copy-start(bf16[1,2,64,1024]{3,2,1,0:T(8,128)(2,1)} %param.9) | copy-start | bytes 786436
  145.6 12.1 %all-to-all-start.1 = ((bf16[2,256,1,256]{3,0,2,1:T(2,128)(2,1)}), bf16[2,256,1,256]{3,0,2,1:T(2,128)(2,1)S(1)}, u32[]{:S(2)}, u32[]{:S(2)}) async-start(bf16[2,256,1,256]{3,0,2,1:T(2,128)(2,1)} %copy.202), calls=%async_computation.1 | async-start | bytes 524288 | tf_op jit(solution)/shard_map/all_to_all | solution.py:98
  169.2 7.3 %collective-permute-start = (bf16[2,64,1024]{2,1,0:T(8,128)(2,1)S(1)}, bf16[2,64,1024]{2,1,0:T(8,128)(2,1)S(1)}, u32[]{:S(2)}, u32[]{:S(2)}) collective-permute-start(bf16[2,64,1024]{2,1,0:T(8,128)(2,1)S(1)} %bitcast.455), channel_id=1, source_target_pairs={{0,16},{1,17},{2,18},{3,19},{4,20},{5,21},{6,22},{7,23},{8,24},{9,... | collective-permute-start | bytes 786440 | tf_op jit(solution)/shard_map/ppermute | solution.py:18
  208.7 64.9 %copy-start.7 = (bf16[2,256,1,4,64]{1,4,3,0,2:T(8,128)(2,1)}, bf16[2,256,1,4,64]{1,4,3,0,2:T(8,128)(2,1)S(1)}, u32[]{:S(2)}) copy-start(bf16[2,256,1,4,64]{1,4,3,0,2:T(8,128)(2,1)S(1)} %copy.287) | copy-start | bytes 786436
  210.4 12.0 %copy-start.12 = (bf16[2,4,64,256]{3,2,1,0:T(8,128)(2,1)}, bf16[2,4,64,256]{3,2,1,0:T(8,128)(2,1)S(1)}, u32[]{:S(2)}) copy-start(bf16[2,4,64,256]{3,2,1,0:T(8,128)(2,1)S(1)} %convolution_convert_fusion.8) | copy-start | bytes 786436
  211.2 11.2 %copy-start.1 = (bf16[4,256,1024]{2,1,0:T(8,128)(2,1)S(1)}, bf16[4,256,1024]{2,1,0:T(8,128)(2,1)}, u32[]{:S(2)}) copy-start(bf16[4,256,1024]{2,1,0:T(8,128)(2,1)} %get-tuple-element.22) | copy-start | bytes 6291460
  279.2 20.3 %all-to-all-start.5 = ((bf16[2,256,1,768]{3,0,2,1:T(2,128)(2,1)}), bf16[2,256,1,768]{3,0,2,1:T(2,128)(2,1)}, u32[]{:S(2)}, u32[]{:S(2)}) async-start(bf16[2,256,1,768]{3,0,2,1:T(2,128)(2,1)} %copy.227), calls=%async_computation.5 | async-start | bytes 1572864 | tf_op jit(solution)/shard_map/all_to_all | solution.py:98
  283.4 96.6 %all-gather.9.cloned.1.call-start = ((), (), s32[]{:S(2)}) async-start(), calls=%async_computation.11 | async-start | bytes 3932160 | tf_op jit(solution)/shard_map/all_gather | solution.py:227
  310.6 6.5 copy-start.26
  318.1 127.8 %all-gather.11.cloned.1.call-start = ((), (), s32[]{:S(2)}) async-start(), calls=%async_computation.12 | async-start | bytes 1310720 | tf_op jit(solution)/shard_map/all_gather | solution.py:227
  380.0 14.3 %collective-permute-start.1 = (bf16[2,64,1024]{2,1,0:T(8,128)(2,1)S(1)}, bf16[2,64,1024]{2,1,0:T(8,128)(2,1)}, u32[]{:S(2)}, u32[]{:S(2)}) collective-permute-start(bf16[2,64,1024]{2,1,0:T(8,128)(2,1)S(1)} %bitcast.408), channel_id=1, source_target_pairs={{16,0},{17,1},{18,2},{19,3},{20,4},{21,5},{22,6},{23,7},{24,8},{25... | collective-permute-start | bytes 786440 | tf_op jit(solution)/shard_map/ppermute | solution.py:18
  395.4 8.1 %copy-start.21 = (bf16[2,64,1024]{2,1,0:T(8,128)(2,1)}, bf16[2,64,1024]{2,1,0:T(8,128)(2,1)S(1)}, u32[]{:S(2)}) copy-start(bf16[2,64,1024]{2,1,0:T(8,128)(2,1)S(1)} %get-tuple-element.71) | copy-start | bytes 786436
  403.5 7.1 %copy-start.22 = (bf16[2,64,1024]{2,1,0:T(8,128)(2,1)S(1)}, bf16[2,64,1024]{2,1,0:T(8,128)(2,1)}, u32[]{:S(2)}) copy-start(bf16[2,64,1024]{2,1,0:T(8,128)(2,1)} %copy-done.21) | copy-start | bytes 786436
  417.1 19.8 %all-to-all-start.6 = ((bf16[2,64,4,256]{3,1,0,2:T(8,128)(2,1)}), bf16[2,64,4,256]{3,1,0,2:T(8,128)(2,1)}, u32[]{:S(2)}, u32[]{:S(2)}) async-start(bf16[2,64,4,256]{3,1,0,2:T(8,128)(2,1)} %copy.232), calls=%async_computation.6 | async-start | bytes 524288 | tf_op jit(solution)/shard_map/all_to_all | solution.py:94
  421.1 92.7 %reduce-scatter.3.cloned.1.call-start = ((), (), s32[]{:S(2)}) async-start(), calls=%async_computation.13 | async-start | bytes 5242880 | tf_op jit(solution)/shard_map/reduce_scatter | solution.py:181
  464.4 13.0 %all-to-all-start.8 = ((bf16[128,4,256]{2,0,1:T(8,128)(2,1)}), bf16[128,4,256]{2,0,1:T(8,128)(2,1)S(1)}, u32[]{:S(2)}, u32[]{:S(2)}) async-start(bf16[128,4,256]{2,0,1:T(8,128)(2,1)} %bitcast.323), calls=%async_computation.8 | async-start | bytes 524288 | tf_op jit(solution)/shard_map/all_to_all | solution.py:395
  477.4 22.2 %all-to-all-start.7 = ((bf16[2,256,1,768]{3,0,2,1:T(2,128)(2,1)}), bf16[2,256,1,768]{3,0,2,1:T(2,128)(2,1)}, u32[]{:S(2)}, u32[]{:S(2)}) async-start(bf16[2,256,1,768]{3,0,2,1:T(2,128)(2,1)} %copy.243), calls=%async_computation.7 | async-start | bytes 1572864 | tf_op jit(solution)/shard_map/all_to_all | solution.py:98
  481.6 64.1 %reduce-scatter.5.cloned.1.call-start = ((), (), s32[]{:S(2)}) async-start(), calls=%async_computation.14 | async-start | bytes 2785280 | tf_op jit(solution)/shard_map/reduce_scatter | solution.py:181
  513.8 114.0 %copy-start.4 = (f32[128,4096]{0,1:T(8,128)S(1)}, f32[128,4096]{0,1:T(8,128)}, u32[]{:S(2)}) copy-start(f32[128,4096]{0,1:T(8,128)} %convolution_add_fusion) | copy-start | bytes 6291460
  513.9 114.0 %all-gather.13.cloned.1.call-start = ((), (), s32[]{:S(2)}) async-start(), calls=%async_computation.15 | async-start | bytes 5242880 | tf_op jit(solution)/shard_map/all_gather | solution.py:187
  514.5 161.1 %all-gather.15.cloned.1.call-start = ((), (), s32[]{:S(2)}) async-start(), calls=%async_computation.16 | async-start | bytes 2785280 | tf_op jit(solution)/shard_map/all_gather | solution.py:187
  (21 other events, 43.2 us)
Sparse Core Ops, SparseCore 0:
  318.2 61.7 all-gather.8
  403.6 33.5 all-gather.10
  462.8 46.3 reduce-scatter.2
  514.0 31.6 reduce-scatter.4
  547.1 80.7 all-gather.12
  629.2 46.2 all-gather.14
where the time goes:
time: 708 us; the launch traced here: 699 us
  waiting for transfers between devices  217 us (31%)
  local copies, waits for them, and re-layouts  132 us (19%)
  matrix products  110 us (16%)
  Pallas kernels  89.8 us (13%)
  blocking collectives  66.3 us (9%)
  other arithmetic  34.8 us (5%)
  starting transfers between devices  33.1 us (5%)
  between operations  15.3 us (2%)
    all_gather x2, waiting for transfers between devices, gathered_parts(): return lax.all_gather(own, 'seq', axis=0, tiled=False)  100 us
    pallas_call x1, Pallas kernels, gathered_weights(): pl.pallas_call(lambda *refs: gather_kernel(plan, count, *refs), out_shape...  89.8 us
    all_gather x2, waiting for transfers between devices, gathered_rows(): return lax.all_gather(values, 'seq', axis=0, tiled=True)  45.7 us
    reduce_scatter x2, waiting for transfers between devices, summed_blocks(): lax.psum_scatter(blocks.reshape(-1, blocks.shape[2]), 'dp', scatter_dimen...  31 us
    all_to_all x2, blocking collectives, to_heads(): return lax.all_to_all(rows, 'seq', split_axis=2, concat_axis=1, tiled=True)  29.9 us
    all_to_all x3, waiting for transfers between devices, to_tokens(): return lax.all_to_all(heads, 'seq', split_axis=1, concat_axis=2, tiled=True)  28 us
    convert_element_type x6, local copies, waits for them, and re-layouts, joined_columns(): return ordered.reshape(rows, inner * columns).astype(jnp.float32)  24.5 us
    dot_general x2, matrix products, backward(): jnp.einsum('rf,df->rd', upper_g.astype(jnp.bfloat16), up_w, preferred_ele...  22.6 us
  transfers between devices with their start and end apart: 14, of which 11 were waited for; matrix products, arithmetic and copies ran while one was open for 18% of the time, Pallas kernels for 0%

commit v1 on v0

--- a/solution.py
+++ b/solution.py
@@ -28,104 +28,175 @@
     return jax.nn.gelu(upper_act, approximate=True)
 
 
-def masked_scores(query_heads, key_heads, full_segments):
-    raw_scores = jnp.einsum(
-        "sqhd,skhd->shqk", query_heads, key_heads, preferred_element_type=jnp.float32
-    ) * DH ** (-0.5)
-    positions = lax.iota(jnp.int32, key_heads.shape[1])
-    causal = (positions[None, :] <= positions[:, None])[None, None]
-    same_doc = full_segments[:, None, :, None] == full_segments[:, None, None, :]
-    return jnp.where(causal & same_doc, raw_scores, MASKED)
-
-
-def split_heads(head_view):
-    seq_count, length = head_view.shape[:2]
-    local_view = head_view.reshape(seq_count, length, 3, -1, DH)
-    return (local_view[:, :, 0], local_view[:, :, 1], local_view[:, :, 2])
-
-
-def attend(head_view, full_segments):
-    seq_count, length = head_view.shape[:2]
-    query_heads, key_heads, value_heads = split_heads(head_view)
-    scores = masked_scores(query_heads, key_heads, full_segments)
+def halo_chunks():
+    return max(1, lax.axis_size("seq") // 4)
+
+
+def from_before(array):
+    return jnp.stack([passed_along(array, "seq", by) for by in range(halo_chunks(), 0, -1)])
+
+
+def score_bias(segments):
+    chunks = halo_chunks()
+    tok_count = segments.shape[1]
+    place = lax.axis_index("seq")
+    before = from_before(segments)
+    window = [
+        jnp.where(place >= chunks - chunk, before[chunk], -1) for chunk in range(chunks)
+    ] + [segments]
+    keys = jnp.concatenate(window, axis=1)
+    query_pos = lax.iota(jnp.int32, tok_count) + chunks * tok_count
+    key_pos = lax.iota(jnp.int32, keys.shape[1])
+    allowed = (key_pos[None, :] <= query_pos[:, None])[None]
+    allowed = allowed & (keys[:, None, :] == segments[:, :, None])
+    return jnp.where(allowed, 0.0, MASKED).astype(jnp.float32)
+
+
+def halves_of(pair):
+    lane = lax.broadcasted_iota(jnp.int32, pair.shape, 1)
+    low = jnp.where(lane < DH, pair, jnp.zeros_like(pair))
+    high = jnp.where(lane < DH, jnp.zeros_like(pair), pair)
+    return jnp.concatenate([low, high], axis=0)
+
+
+def joined_halves(stacked):
+    tok_count = stacked.shape[0] // 2
+    low, high = stacked[:tok_count], stacked[tok_count:]
+    return jnp.where(lax.broadcasted_iota(jnp.int32, low.shape, 1) < DH, low, high)
+
+
+def dot_last(left, right):
+    return lax.dot_general(
+        left, right, (((1,), (1,)), ((), ())), preferred_element_type=jnp.float32
+    )
+
+
+def dot_first(left, right):
+    return lax.dot_general(
+        left, right, (((0,), (0,)), ((), ())), preferred_element_type=jnp.float32
+    )
+
+
+def pair_scores(query_pair, key_pair, bias):
+    scores = dot_last(halves_of(query_pair), key_pair) * DH ** (-0.5)
+    scores = scores + jnp.concatenate([bias, bias], axis=0)
     row_max = jnp.max(scores, axis=-1, keepdims=True)
     log_total = jnp.log(jnp.sum(jnp.exp(scores - row_max), axis=-1, keepdims=True)) + row_max
-    weights = jnp.exp(scores - log_total).astype(jnp.bfloat16)
-    attended = jnp.einsum(
-        "shqk,skhd->sqhd", weights, value_heads, preferred_element_type=jnp.float32
-    ).astype(jnp.bfloat16)
-    return (attended.reshape(seq_count, length, 1, -1), log_total)
-
-
-def attend_grad(head_view, attended, log_total, heads_grad, full_segments):
-    seq_count, length = head_view.shape[:2]
-    query_heads, key_heads, value_heads = split_heads(head_view)
-    out_heads = attended.reshape(seq_count, length, -1, DH)
-    grads_in = heads_grad.reshape(seq_count, length, -1, DH)
-    row_delta = jnp.moveaxis(
-        jnp.sum(grads_in.astype(jnp.float32) * out_heads.astype(jnp.float32), axis=-1), 1, 2
-    )[..., None]
-    score_scale = DH ** (-0.5)
-    scores = masked_scores(query_heads, key_heads, full_segments)
-    weights = jnp.exp(scores - log_total)
-    values_grad = jnp.einsum(
-        "shqk,sqhd->skhd",
-        weights.astype(jnp.bfloat16),
-        grads_in,
-        preferred_element_type=jnp.float32,
-    )
-    weights_grad = jnp.einsum(
-        "sqhd,skhd->shqk", grads_in, value_heads, preferred_element_type=jnp.float32
-    )
-    scores_grad = (weights * (weights_grad - row_delta)).astype(jnp.bfloat16)
-    query_grad = (
-        jnp.einsum("shqk,skhd->sqhd", scores_grad, key_heads, preferred_element_type=jnp.float32)
-        * score_scale
-    )
-    keys_grad = (
-        jnp.einsum("shqk,sqhd->skhd", scores_grad, query_heads, preferred_element_type=jnp.float32)
-        * score_scale
-    )
-    joined = jnp.stack([query_grad, keys_grad, values_grad], axis=2).astype(jnp.bfloat16)
-    return joined.reshape(seq_count, length, 1, -1)
-
-
-def to_heads(rows):
-    return lax.all_to_all(rows, "seq", split_axis=2, concat_axis=1, tiled=True)
-
-
-def to_tokens(heads):
-    return lax.all_to_all(heads, "seq", split_axis=1, concat_axis=2, tiled=True)
-
-
-def forward(entry_rows, params, full_segments):
+    return jnp.exp(scores - log_total)
+
+
+def window_pair(halo_ref, own_ref, rows, first):
+    columns = pl.ds(first, 2 * DH)
+    parts = [halo_ref[chunk, rows, columns] for chunk in range(halo_ref.shape[0])]
+    return jnp.concatenate(parts + [own_ref[rows, columns]], axis=0)
+
+
+def attend_kernel(query_ref, own_ref, halo_ref, bias_ref, out_ref):
+    tok_count, width = bias_ref.shape[1], query_ref.shape[1]
+    for sequence in range(bias_ref.shape[0]):
+        rows = pl.ds(sequence * tok_count, tok_count)
+        bias = bias_ref[sequence]
+        for first in range(0, width, 2 * DH):
+            weights = pair_scores(
+                query_ref[rows, pl.ds(first, 2 * DH)],
+                window_pair(halo_ref, own_ref, rows, first),
+                bias,
+            )
+            values = window_pair(halo_ref, own_ref, rows, width + first)
+            attended = jnp.dot(
+                weights.astype(jnp.bfloat16), values, preferred_element_type=jnp.float32
+            )
+            out_ref[rows, pl.ds(first, 2 * DH)] = joined_halves(attended).astype(jnp.bfloat16)
+
+
+def attend_grad_kernel(
+    query_ref, own_ref, halo_ref, bias_ref, out_ref, grad_ref, query_g_ref, own_g_ref, halo_g_ref
+):
+    tok_count, width = bias_ref.shape[1], query_ref.shape[1]
+    chunks = halo_ref.shape[0]
+    for sequence in range(bias_ref.shape[0]):
+        rows = pl.ds(sequence * tok_count, tok_count)
+        bias = bias_ref[sequence]
+        for first in range(0, width, 2 * DH):
+            columns = pl.ds(first, 2 * DH)
+            query_pair, grad_pair = query_ref[rows, columns], grad_ref[rows, columns]
+            keys = window_pair(halo_ref, own_ref, rows, first)
+            values = window_pair(halo_ref, own_ref, rows, width + first)
+            weights = pair_scores(query_pair, keys, bias)
+            queries_two, grads_two = halves_of(query_pair), halves_of(grad_pair)
+            products = grads_two.astype(jnp.float32) * halves_of(out_ref[rows, columns]).astype(
+                jnp.float32
+            )
+            row_delta = jnp.sum(products, axis=-1, keepdims=True)
+            scores_g = (weights * (dot_last(grads_two, values) - row_delta)).astype(jnp.bfloat16)
+            query_g = jnp.dot(scores_g, keys, preferred_element_type=jnp.float32)
+            query_g_ref[rows, columns] = (joined_halves(query_g) * DH ** (-0.5)).astype(
+                jnp.bfloat16
+            )
+            keys_g = dot_first(scores_g, queries_two) * DH ** (-0.5)
+            values_g = dot_first(weights.astype(jnp.bfloat16), grads_two)
+            for grad, start in ((keys_g, first), (values_g, width + first)):
+                for chunk in range(chunks):
+                    halo_g_ref[chunk, rows, pl.ds(start, 2 * DH)] = grad[
+                        chunk * tok_count : (chunk + 1) * tok_count
+                    ].astype(jnp.bfloat16)
+                own_g_ref[rows, pl.ds(start, 2 * DH)] = grad[chunks * tok_count :]
+
+
+def in_vmem(count):
+    return [pl.BlockSpec(memory_space=pltpu.VMEM)] * count
+
+
+def attend(query, own, halo, bias):
+    return pl.pallas_call(
+        attend_kernel,
+        out_shape=jax.ShapeDtypeStruct(query.shape, jnp.bfloat16),
+        in_specs=in_vmem(4),
+        out_specs=pl.BlockSpec(memory_space=pltpu.VMEM),
+        cost_estimate=pl.CostEstimate(flops=10**9, bytes_accessed=10**7, transcendentals=0),
+        name="attend",
+    )(query, own, halo, bias)
+
+
+def attend_grad(query, own, halo, bias, attended, heads_grad):
+    return pl.pallas_call(
+        attend_grad_kernel,
+        out_shape=(
+            jax.ShapeDtypeStruct(query.shape, jnp.bfloat16),
+            jax.ShapeDtypeStruct(own.shape, jnp.float32),
+            jax.ShapeDtypeStruct(halo.shape, jnp.bfloat16),
+        ),
+        in_specs=in_vmem(6),
+        out_specs=tuple(in_vmem(3)),
+        cost_estimate=pl.CostEstimate(flops=10**9, bytes_accessed=10**7, transcendentals=0),
+        name="attend_grad",
+    )(query, own, halo, bias, attended, heads_grad)
+
+
+def forward(entry_rows, params, bias):
     qkv_w, out_w, up_w, down_w, gain_vecs, vectors, up_vec = params
-    seq_count, tok_count, width = entry_rows.shape
-    groups = lax.axis_size("seq")
+    width = entry_rows.shape[-1]
     row_values = entry_rows.reshape(-1, width).astype(jnp.float32)
     normed = layer_norm(row_values, gain_vecs[0], vectors[0]).astype(jnp.bfloat16)
-    qkv_bias = jnp.concatenate([vectors[1], jnp.zeros_like(vectors[1]), vectors[2]])
-    projected = (jnp.dot(normed, qkv_w, preferred_element_type=jnp.float32) + qkv_bias).astype(
-        jnp.bfloat16
-    )
-    grouped = projected.reshape(seq_count, tok_count, 3, groups, width // groups)
-    grouped = grouped.transpose(0, 1, 3, 2, 4).reshape(seq_count, tok_count, groups, -1)
-    head_view = to_heads(grouped)
-    attended, log_total = attend(head_view, full_segments)
-    mixed = to_tokens(attended).reshape(-1, width)
+    own_bias = jnp.concatenate([jnp.zeros_like(vectors[2]), vectors[2]])
+    own = jnp.dot(normed, qkv_w[:, width:], preferred_element_type=jnp.float32) + own_bias
+    own = own.astype(jnp.bfloat16)
+    halo = from_before(own)
+    query = jnp.dot(normed, qkv_w[:, :width], preferred_element_type=jnp.float32) + vectors[1]
+    query = query.astype(jnp.bfloat16)
+    mixed = attend(query, own, halo, bias)
     residual = row_values + jnp.dot(mixed, out_w, preferred_element_type=jnp.float32) + vectors[3]
     normed_two = layer_norm(residual, gain_vecs[1], vectors[4]).astype(jnp.bfloat16)
     upper_act = jnp.dot(normed_two, up_w, preferred_element_type=jnp.float32) + up_vec
     hidden = smooth_gate(upper_act).astype(jnp.bfloat16)
     output = residual + jnp.dot(hidden, down_w, preferred_element_type=jnp.float32) + vectors[5]
-    return (output, (normed, head_view, attended, log_total, mixed, residual, normed_two, upper_act))
-
-
-def backward(incoming, entry_rows, params, saved, full_segments, beside=None):
+    return (output, (normed, query, own, halo, mixed, residual, normed_two, upper_act))
+
+
+def backward(incoming, entry_rows, params, saved, bias, beside=None):
     qkv_w, out_w, up_w, down_w, gain_vecs, vectors, up_vec = params
-    normed, head_view, attended, log_total, mixed, residual, normed_two, upper_act = saved
-    seq_count, tok_count, width = entry_rows.shape
-    groups = lax.axis_size("seq")
+    normed, query, own, halo, mixed, residual, normed_two, upper_act = saved
+    width = entry_rows.shape[-1]
     grad_rows = incoming.reshape(-1, width)
     upstream = grad_rows.astype(jnp.float32)
     down_bias_g = jnp.sum(upstream, axis=0)
@@ -143,33 +214,30 @@
     mixed_g = jnp.einsum(
         "re,de->rd", residual_round, out_w, preferred_element_type=jnp.float32
     ).astype(jnp.bfloat16)
-    heads_grad = to_heads(mixed_g.reshape(seq_count, tok_count, groups, width // groups))
-    joined_heads = attend_grad(head_view, attended, log_total, heads_grad, full_segments)
+    query_g, own_g, halo_g = attend_grad(query, own, halo, bias, mixed, mixed_g)
     if beside is not None:
-        joined_heads, beside = lax.optimization_barrier((joined_heads, beside))
-    token_grads = to_tokens(joined_heads)
-    joined = token_grads.reshape(seq_count, tok_count, groups, 3, width // groups)
-    joined = joined.transpose(0, 1, 3, 2, 4).reshape(-1, 3 * width)
-    column_sums = jnp.sum(joined.astype(jnp.float32), axis=0)
-    normed_g = jnp.einsum("re,de->rd", joined, qkv_w, preferred_element_type=jnp.float32)
+        query_g, halo_g, beside = lax.optimization_barrier((query_g, halo_g, beside))
+    chunks = halo_g.shape[0]
+    for chunk in range(chunks):
+        own_g = own_g + passed_along(halo_g[chunk], "seq", chunk - chunks).astype(jnp.float32)
+    own_g = own_g.astype(jnp.bfloat16)
+    column_sums = jnp.sum(query_g.astype(jnp.float32), axis=0)
+    value_sums = jnp.sum(own_g[:, width:].astype(jnp.float32), axis=0)
+    normed_g = jnp.einsum(
+        "re,de->rd", query_g, qkv_w[:, :width], preferred_element_type=jnp.float32
+    ) + jnp.einsum("re,de->rd", own_g, qkv_w[:, width:], preferred_element_type=jnp.float32)
     row_values = entry_rows.reshape(-1, width).astype(jnp.float32)
     entry_back = jax.vjp(layer_norm, row_values, gain_vecs[0], vectors[0])[1]
     entry_part, gain_one_g, shift_one_g = entry_back(normed_g)
     vector_grads = (
         jnp.stack([gain_one_g, gain_two_g]),
         jnp.stack(
-            [
-                shift_one_g,
-                column_sums[:width],
-                column_sums[2 * width :],
-                out_bias_g,
-                shift_two_g,
-                down_bias_g,
-            ]
+            [shift_one_g, column_sums, value_sums, out_bias_g, shift_two_g, down_bias_g]
         ),
         up_bias_g[None],
     )
-    return (residual_g + entry_part, residual_round, joined_heads, vector_grads, beside)
+    joined = jnp.concatenate([query_g, own_g], axis=1)
+    return (residual_g + entry_part, residual_round, joined, vector_grads, beside)
 
 
 def rounded_blocks(partial):
@@ -363,17 +431,17 @@
         rows_of(gain_count, shift_count),
         packed[:, (gain_count + shift_count) * share :].reshape(-1),
     )
-    full_segments = lax.all_gather(segments, "seq", axis=1, tiled=True)
-
-    first_output = forward(own_slot, params, full_segments)[0]
+    bias = score_bias(segments)
+
+    first_output = forward(own_slot, params, bias)[0]
     received = passed_along(
         first_output.astype(jnp.bfloat16).reshape(own_slot.shape), "section", 1
     )
     entry_rows = jnp.where(leading, own_slot, received)
-    last_output, saved = forward(entry_rows, params, full_segments)
-    normed, head_view, attended, log_total, mixed, residual, normed_two, upper_act = saved
+    last_output, saved = forward(entry_rows, params, bias)
+    normed, query, own, halo, mixed, residual, normed_two, upper_act = saved
     tokens_in = gathered_rows(jnp.concatenate([normed, normed_two, mixed], axis=1))
-    early_entry = backward(own_slot, entry_rows, params, saved, full_segments)[0]
+    early_entry = backward(own_slot, entry_rows, params, saved, bias)[0]
     early_entry, tokens_in = lax.optimization_barrier((early_entry, tokens_in))
     all_normed = tokens_in[:, :width]
     all_normed_two = tokens_in[:, width : 2 * width]
@@ -389,19 +457,20 @@
         [rounded_blocks(up_g), rounded_blocks(down_g.reshape(width, -1))], axis=2
     )
     entry_g, residual_round, joined_heads, vector_grads, gate_blocks = backward(
-        incoming, entry_rows, params, saved, full_segments, gate_blocks
+        incoming, entry_rows, params, saved, bias, gate_blocks
     )
     gate_own = summed_blocks(gate_blocks)
-    residual_part = lax.all_to_all(
-        residual_round.reshape(-1, inner, width // inner),
-        "seq",
-        split_axis=1,
-        concat_axis=0,
-        tiled=True,
-    ).reshape(-1, width // inner)
+    sent = jnp.concatenate(
+        [
+            joined_heads.reshape(-1, inner, 3 * width // inner),
+            residual_round.reshape(-1, inner, width // inner),
+        ],
+        axis=2,
+    )
+    sent = lax.all_to_all(sent, "seq", split_axis=1, concat_axis=0, tiled=True)
+    sent = sent.reshape(-1, sent.shape[2])
+    joined_part, residual_part = sent[:, : 3 * width // inner], sent[:, 3 * width // inner :]
     out_g = jnp.einsum("rd,re->de", all_mixed, residual_part, preferred_element_type=jnp.float32)
-    joined_part = joined_heads.reshape(seq_count, inner, tok_count, -1).transpose(1, 0, 2, 3)
-    joined_part = joined_part.reshape(seq_count * inner * tok_count, -1)
     qkv_g = jnp.einsum("rd,re->de", all_normed, joined_part, preferred_element_type=jnp.float32)
     matrix_part = jnp.concatenate([rounded_blocks(qkv_g), rounded_blocks(out_g)], axis=2)
     vectors_g = jnp.concatenate([by_owner(part, outer) for part in vector_grads], axis=1)
@@ -417,7 +486,7 @@
     down_total = gate_parts[:, :, up_columns:].reshape(-1, width).astype(jnp.float32)
     parts = gathered_parts(last_own)
     qkv_columns = qkv_g.shape[1]
-    qkv_total = joined_columns(parts[:, :share, :qkv_columns], 3)
+    qkv_total = joined_columns(parts[:, :share, :qkv_columns], 1)
     out_total = joined_columns(parts[:, :share, qkv_columns:], 1)
     own_vectors = jnp.sum(parts[:, share:].astype(jnp.float32), axis=0).reshape(-1)
     gains_total = own_vectors[: gain_count * share].reshape(gain_count, share)

time: 708 us -> 588 us (0.83)
  blocking collectives: 66.3 us -> 6.25 us
  local copies, waits for them, and re-layouts: 132 us -> 72.4 us
  Pallas kernels: 89.8 us -> 122 us
  waiting for transfers between devices: 217 us -> 200 us
  starting transfers between devices: 33.1 us -> 24.7 us
    all_to_all x3 -> x0, blocking collectives: 40.8 us -> none  [the longest x2 29.9 us: to_heads(): return lax.all_to_all(rows, 'seq', split_axis=2, concat_axis=1, tiled=True)]
    all_gather x2, waiting for transfers between devices: 45.7 us -> 6.91 us  [gathered_rows(): return lax.all_gather(values, 'seq', axis=0, tiled=True)]
    ppermute x2 -> x7, waiting for transfers between devices: 3.85 us -> 38.9 us  [passed_along(): return lax.ppermute(array, axis, pairs)]
    pallas_call x0 -> x4, Pallas kernels: none -> 32.7 us  [the longest x2 17.9 us: attend_grad(): pl.pallas_call(attend_grad_kernel, out_shape=(jax.ShapeDtypeStruct(query....]
    reshape x24 -> x1, local copies, waits for them, and re-layouts: 30.7 us -> 0.05 us  [shards(): joined_heads.reshape(-1, inner, 3 * width // inner)]
    all_to_all x6 -> x1, starting transfers between devices: 27.1 us -> 3.52 us  [shards(): sent = lax.all_to_all(sent, 'seq', split_axis=1, concat_axis=0, tiled=True)]
    all_gather x1 -> x0, blocking collectives: 19.3 us -> none  [shards(): full_segments = lax.all_gather(segments, 'seq', axis=1, tiled=True)]
    ppermute x2 -> x7, starting transfers between devices: 4.89 us -> 20.3 us  [passed_along(): return lax.ppermute(array, axis, pairs)]
  transfers between devices with their start and end apart: 14 -> 14, of which waited for: 11 -> 10; matrix products, arithmetic and copies ran while one was open for 18% -> 23% of each run, Pallas kernels for 0% -> 3%
where the time goes in v1:
time: 588 us; the launch traced here: 579 us
  waiting for transfers between devices  200 us (34%)
  Pallas kernels  122 us (21%)
  matrix products  108 us (18%)
  local copies, waits for them, and re-layouts  72.4 us (12%)
  other arithmetic  30.4 us (5%)
  starting transfers between devices  24.7 us (4%)
  between operations  15.1 us (3%)
  blocking collectives  6.25 us (1%)
    all_gather x2, waiting for transfers between devices, gathered_parts(): return lax.all_gather(own, 'seq', axis=0, tiled=False)  98.9 us
    pallas_call x1, Pallas kernels, gathered_weights(): pl.pallas_call(lambda *refs: gather_kernel(plan, count, *refs), out_shape...  89.8 us
    ppermute x7, waiting for transfers between devices, passed_along(): return lax.ppermute(array, axis, pairs)  38.9 us
    reduce_scatter x2, waiting for transfers between devices, summed_blocks(): lax.psum_scatter(blocks.reshape(-1, blocks.shape[2]), 'dp', scatter_dimen...  30.6 us
    all_to_all x1, waiting for transfers between devices, shards(): sent = lax.all_to_all(sent, 'seq', split_axis=1, concat_axis=0, tiled=True)  23.8 us
    dot_general x2, matrix products, backward(): jnp.einsum('rf,df->rd', upper_g.astype(jnp.bfloat16), up_w, preferred_ele...  22.8 us
    convert_element_type x5, local copies, waits for them, and re-layouts, joined_columns(): return ordered.reshape(rows, inner * columns).astype(jnp.float32)  22.2 us
    ppermute x7, starting transfers between devices, passed_along(): return lax.ppermute(array, axis, pairs)  20.3 us
  transfers between devices with their start and end apart: 14, of which 10 were waited for; matrix products, arithmetic and copies ran while one was open for 23% of the time, Pallas kernels for 3%

profile of v1, /device:TPU:0, one launch (start us, length us, event | category | flops | bytes accessed | tf_op | source)
XLA Modules:
  0.0 578.7 jit_solution(12689743225147529822)
XLA Ops:
  9.3 6.2 %all-gather = bf16[12288]{0:T(1024)(128)(2,1)S(1)} all-gather(bf16[3072]{0:T(1024)(128)(2,1)S(1)} %pad_maximum_fusion.5), channel_id=2, replica_groups=mesh['section'=2,'seq'=4,'dp'=4] {'dp'}, dimensions={0}, use_global_device_ids=true | all-gather | bytes 30720 | tf_op jit(solution)/shard_map/all_gather | solution.py:421
  19.3 89.8 %gather_weights.1 = (bf16[4,256,3072]{2,1,0:T(8,128)(2,1)}, bf16[4,256,1024]{2,1,0:T(8,128)(2,1)}, bf16[4,256,4096]{2,1,0:T(8,128)(2,1)}, bf16[4,1024,1024]{2,1,0:T(8,128)(2,1)}) custom-call(bf16[256,3072]{1,0:T(8,128)(2,1)} %bitcast.202, bf16[256,1024]{1,0:T(8,128)(2,1)} %bitcast.207, bf16[256,4096]{1,0:T(8,128)(2,1)} %bitcast.195, bf16[1024,1024]{1,0:T(8,128)(2,1)} %bitcast.196), custom_call_target="tpu_custom_call" | custom-call | tf_op jit(solution)/shard_map/gather_weights/pallas_call | solution.py:399
  128.0 7.4 %attend.2 = bf16[128,1024]{1,0:T(8,128)(2,1)} custom-call(bf16[128,1024]{1,0:T(8,128)(2,1)} %fusion.72.query_ref, bf16[128,2048]{1,0:T(8,128)(2,1)} %copy-done.17, bf16[1,128,2048]{2,1,0:T(8,128)(2,1)} %bitcast.15.halo_ref, f32[2,64,128]{2,1,0:T(8,128)} %and_select_fusion.bias_ref), custom_call_target="tpu_custom_call" | custom-call | flops 1000000000 | bytes 10000000 | tf_op jit(solution)/shard_map/attend/pallas_call | solution.py:151
  137.1 10.5 %fusion.68 = bf16[128,1024]{1,0:T(8,128)(2,1)S(1)} fusion(f32[128,1024]{1,0:T(8,128)S(1)} %get-tuple-element.99, bf16[4096,1024]{1,0:T(8,128)(2,1)} %bitcast.167, bf16[1024,4096]{1,0:T(8,128)(2,1)} %bitcast.163, f32[4096]{0:T(1024)S(1)} %bitcast.225, f32[1024]{0:T(1024)S(1)} %bitcast.233, f32[1024]{0:T(1024)S(1)} %bitcast.235, f32[1024]{0:T(1024)S(1)} %bitcast.220, ...), kind=kOutput, calls=%fused_computation.79 | convolution fusion | flops 2153775104 | bytes 17593344 | tf_op jit(solution)/shard_map/dot_general | solution.py:192
  165.5 14.5 %reshape_reshape.8 = bf16[1024,4,4,256]{3,2,1,0:T(4,128)(2,1)} reshape(bf16[4,256,4096]{2,1,0:T(8,128)(2,1)} %get-tuple-element.30) | data formatting | bytes 16777216 | tf_op jit(solution)/shard_map/reshape;reshape | solution.py:261
  182.7 7.4 %attend.3.out_ref = bf16[128,1024]{1,0:T(8,128)(2,1)} custom-call(bf16[128,1024]{1,0:T(8,128)(2,1)} %fusion.69.query_ref, bf16[128,2048]{1,0:T(8,128)(2,1)} %copy-done.16, bf16[1,128,2048]{2,1,0:T(8,128)(2,1)} %bitcast.24.halo_ref, f32[2,64,128]{2,1,0:T(8,128)} %and_select_fusion.bias_ref), custom_call_target="tpu_custom_call" | custom-call | flops 1000000000 | bytes 10000000 | tf_op jit(solution)/shard_map/attend/pallas_call | solution.py:151
  192.0 7.9 %convolution_add_fusion = f32[128,4096]{0,1:T(8,128)} fusion(bf16[128,1024]{1,0:T(8,128)(2,1)S(1)} %add_convert_fusion.4, bf16[1024,4096]{1,0:T(8,128)(2,1)} %bitcast.164, f32[4096]{0:T(1024)S(1)} %bitcast.226), kind=kOutput, calls=%fused_computation.1 | convolution fusion | flops 1074266112 | bytes 10764288 | tf_op jit(solution)/shard_map/dot_general | solution.py:190
  201.4 16.1 %multiply_reduce_fusion.5 = (f32[128]{0:T(128)S(1)}, f32[128,1024]{1,0:T(8,128)}) fusion(f32[128,1024]{1,0:T(8,128)S(1)} %get-tuple-element.101, f32[128]{0:T(128)S(1)} %broadcast_multiply_fusion.2, f32[1024]{0:T(1024)S(1)} %bitcast.222, bf16[1024,4096]{1,0:T(8,128)(2,1)} %bitcast.165, f32[128,4096]{0,1:T(8,128)} %convolution_add_fusion, ...), kind=kOutput, calls=%fused_computation.138 | convolution fusion | flops 2158493696 | bytes 20190208 | tf_op jit(solution)/shard_map/rf,df->rd/dot_general | solution.py:206
  221.1 8.9 %attend_grad.2 = (bf16[128,1024]{1,0:T(8,128)(2,1)}, f32[128,2048]{1,0:T(8,128)}, bf16[1,128,2048]{2,1,0:T(8,128)(2,1)}) custom-call(bf16[128,1024]{1,0:T(8,128)(2,1)} %fusion.69.query_ref, bf16[128,2048]{1,0:T(8,128)(2,1)} %copy-done.16, bf16[1,128,2048]{2,1,0:T(8,128)(2,1)} %bitcast.24.halo_ref, f32[2,64,128]{2,1,0:T(8,128)} %and_select_fusion.bias_ref, ...), custom_call_target="tpu_custom_call" | custom-call | flops 1000000000 | bytes 10000000 | tf_op jit(solution)/shard_map/attend_grad/pallas_call | solution.py:162
  231.5 9.8 %constant_dynamic-slice_fusion.1 = bf16[1024,4,1,256]{3,2,1,0:T(2,128)(2,1)} fusion(bf16[1024,4,4,256]{3,2,1,0:T(4,128)(2,1)} %reshape_reshape.8, s32[]{:T(128)S(6)} %select_n.47), kind=kLoop, calls=%fused_computation.181 | loop fusion | bytes 4194308 | tf_op jit(solution)/shard_map/jit(dynamic_index_in_dim)/dynamic_slice | solution.py:262
  241.3 10.5 %copy.57 = bf16[1024,4,1,256]{0,3,1,2:T(8,128)(2,1)} copy(bf16[1024,4,1,256]{3,2,1,0:T(2,128)(2,1)} %constant_dynamic-slice_fusion.1) | data formatting | bytes 4194304
  255.0 13.8 %collective-permute-done.4 = bf16[128,2048]{1,0:T(8,128)(2,1)} collective-permute-done((bf16[128,2048]{1,0:T(8,128)(2,1)}, bf16[128,2048]{1,0:T(8,128)(2,1)}, u32[]{:S(2)}, u32[]{:S(2)}) %collective-permute-start.4) | collective-permute-done | bytes 524320 | tf_op jit(solution)/shard_map/ppermute | solution.py:18
  285.3 8.1 %fusion.150 = (bf16[4096]{0:T(1024)(128)(2,1)S(1)}, bf16[128,4096]{0,1:T(8,128)(2,1)}) fusion(f32[128,4096]{0,1:T(8,128)} %convolution_add_fusion, bf16[128,1024]{1,0:T(8,128)(2,1)S(1)} %bitcast.190, bf16[4096,1024]{1,0:T(8,128)(2,1)} %bitcast.170), kind=kOutput, calls=%fused_computation.229 | convolution fusion | flops 1084747776 | bytes 11804672 | tf_op jit(solution)/shard_map/rd,fd->rf/dot_general | solution.py:203
  293.7 6.8 %multiply_reduce_fusion = (bf16[1024]{0:T(1024)(128)(2,1)S(1)}, f32[128]{0:T(128)S(1)}, bf16[1024]{0:T(1024)(128)(2,1)S(1)}, f32[128,1024]{1,0:T(8,128)S(1)}) fusion(f32[128,1024]{1,0:T(8,128)S(1)} %get-tuple-element.101, f32[128]{0:T(128)S(1)} %fusion.122, f32[128]{0:T(128)S(1)} %broadcast_multiply_fusion.2, f32[1024]{0:T(1024)S(1)} %bitcast.223, ...), kind=kOutput, calls=%fused_computation.130 | convolution fusion | flops 1074788224 | bytes 10495488 | tf_op jit(solution)/shard_map/rf,df->rd/dot_general | solution.py:206
  303.3 9.0 %attend_grad.3 = (bf16[128,1024]{1,0:T(8,128)(2,1)}, f32[128,2048]{1,0:T(8,128)}, bf16[1,128,2048]{2,1,0:T(8,128)(2,1)}) custom-call(bf16[128,1024]{1,0:T(8,128)(2,1)} %fusion.69.query_ref, bf16[128,2048]{1,0:T(8,128)(2,1)} %copy-done.16, bf16[1,128,2048]{2,1,0:T(8,128)(2,1)} %bitcast.24.halo_ref, f32[2,64,128]{2,1,0:T(8,128)} %and_select_fusion.bias_ref, ...), custom_call_target="tpu_custom_call" | custom-call | flops 1000000000 | bytes 10000000 | tf_op jit(solution)/shard_map/attend_grad/pallas_call | solution.py:162
  312.3 6.9 %all-gather.10.cloned.1.call-done = bf16[512,1024]{1,0:T(8,128)(2,1)} async-done(((bf16[128,1024]{1,0:T(8,128)(2,1)}), bf16[512,1024]{1,0:T(8,128)(2,1)}) %all-gather.10.cloned.1.call-update) | async-done | bytes 1048592 | tf_op jit(solution)/shard_map/all_gather | solution.py:295
  324.1 7.0 %convolution_convert_fusion.1 = bf16[1024,1024]{1,0:T(8,128)(2,1)} fusion(f32[512,1024]{1,0:T(8,128)} %fusion.96, f32[1024]{0:T(1024)S(1)} %bitcast.242, bf16[512,3072]{1,0:T(8,128)(2,1)} %all-gather.8.cloned.1.call-done, bf16[512,1024]{1,0:T(8,128)(2,1)} %all-gather.10.cloned.1.call-done, bf16[1024,1024]{1,0:T(8,128)(2,1)S(1)} %bitcast.198), kind=kOutput, calls=%fused_computation.52 | convolution fusion | flops 2159542272 | bytes 8392704 | tf_op jit(solution)/shard_map/rd,rf->df/dot_general | solution.py:284
  340.2 11.1 %collective-permute-done.6 = bf16[128,2048]{1,0:T(8,128)(2,1)S(1)} collective-permute-done((bf16[128,2048]{1,0:T(8,128)(2,1)}, bf16[128,2048]{1,0:T(8,128)(2,1)S(1)}, u32[]{:S(2)}, u32[]{:S(2)}) %collective-permute-start.6) | collective-permute-done | bytes 524320 | tf_op jit(solution)/shard_map/ppermute | solution.py:18
  363.5 23.8 %all-to-all-done = bf16[128,4,1024]{2,0,1:T(8,128)(2,1)S(1)} async-done(((bf16[128,4,1024]{2,0,1:T(8,128)(2,1)}), bf16[128,4,1024]{2,0,1:T(8,128)(2,1)S(1)}, u32[]{:S(2)}, u32[]{:S(2)}) %all-to-all-start) | async-done | bytes 1048608 | tf_op jit(solution)/shard_map/all_to_all | solution.py:470
  394.8 30.6 %reduce-scatter.5.cloned.1.call-done = bf16[272,1024]{1,0:T(8,128)(2,1)} async-done(((bf16[1088,1024]{1,0:T(8,128)(2,1)}), bf16[272,1024]{1,0:T(8,128)(2,1)}) %reduce-scatter.5.cloned.1.call-update) | async-done | bytes 557072 | tf_op jit(solution)/shard_map/reduce_scatter | solution.py:249
  425.4 82.2 %all-gather.12.cloned.1.call-done = bf16[1024,2048]{1,0:T(8,128)(2,1)} async-done(((bf16[256,2048]{1,0:T(8,128)(2,1)}), bf16[1024,2048]{1,0:T(8,128)(2,1)}) %all-gather.12.cloned.1.call-update) | async-done | bytes 4194320 | tf_op jit(solution)/shard_map/all_gather | solution.py:255
  508.9 6.2 %add_select_fusion = f32[128,1024]{1,0:T(8,128)} fusion(f32[128,1024]{1,0:T(8,128)} %copy-done.3, f32[128,1024]{1,0:T(8,128)S(1)} %get-tuple-element.75, f32[128]{0:T(128)S(1)} %negate_multiply_fusion, f32[1024]{0:T(1024)S(1)} %bitcast.234, f32[128,1024]{1,0:T(8,128)S(1)} %get-tuple-element.101, bf16[4096,1024]{1,0:T(8,128)(2,1)} %bitcast.171, ...), kind=kOutput, calls=%fused_computation.132 | convolution fusion | flops 1079115776 | bytes 12587521 | tf_op jit(solution)/shard_map/dot_general | solution.py:192
  523.5 6.9 %copy.69 = f32[4,256,4,256]{3,0,2,1:T(4,128)} copy(f32[4,256,4,256]{3,2,1,0:T(4,128)} %reshape.402) | data formatting | bytes 8388608 | tf_op jit(solution)/shard_map/convert_element_type | solution.py:291
  538.6 16.7 %all-gather.14.cloned.1.call-done = bf16[1088,1024]{1,0:T(8,128)(2,1)} async-done(((bf16[272,1024]{1,0:T(8,128)(2,1)}), bf16[1088,1024]{1,0:T(8,128)(2,1)}) %all-gather.14.cloned.1.call-update) | async-done | bytes 2228240 | tf_op jit(solution)/shard_map/all_gather | solution.py:255
  (188 shorter events, 145.6 us)
Async XLA Ops:
  7.2 268.8 %all-gather.8.cloned.1.call-start = ((), (), s32[]{:S(2)}) async-start(), calls=%async_computation.3 | async-start | bytes 3932160 | tf_op jit(solution)/shard_map/all_gather | solution.py:295
  109.1 7.1 %copy-start.15 = (s32[2,64]{1,0:T(2,128)S(1)}, s32[2,64]{1,0:T(2,128)}, u32[]{:S(2)}) copy-start(s32[2,64]{1,0:T(2,128)} %param.10) | copy-start | bytes 1540
  112.0 16.0 %copy-start.17 = (bf16[128,2048]{1,0:T(8,128)(2,1)}, bf16[128,2048]{1,0:T(8,128)(2,1)S(1)}, u32[]{:S(2)}) copy-start(bf16[128,2048]{1,0:T(8,128)(2,1)S(1)} %fusion.17.own_ref) | copy-start | bytes 1572868
  112.0 16.0 %collective-permute-start = (bf16[128,2048]{1,0:T(8,128)(2,1)S(1)}, bf16[128,2048]{1,0:T(8,128)(2,1)}, u32[]{:S(2)}, u32[]{:S(2)}) collective-permute-start(bf16[128,2048]{1,0:T(8,128)(2,1)S(1)} %fusion.17.own_ref), channel_id=1, source_target_pairs={{0,4},{4,8},{8,12},{1,5},{5,9},{9,13},{2,6},{6,10},{10,14},{3,7},{... | collective-permute-start | bytes 1572872 | tf_op jit(solution)/shard_map/ppermute | solution.py:18
  116.2 11.0 %collective-permute-start.1 = (s32[2,64]{1,0:T(2,128)S(1)}, s32[2,64]{1,0:T(2,128)S(1)}, u32[]{:S(2)}, u32[]{:S(2)}) collective-permute-start(s32[2,64]{1,0:T(2,128)S(1)} %copy-done.15), channel_id=1, source_target_pairs={{0,4},{4,8},{8,12},{1,5},{5,9},{9,13},{2,6},{6,10},{10,14},{3,7},{... | collective-permute-start | bytes 1544 | tf_op jit(solution)/shard_map/ppermute | solution.py:18
  121.8 13.6 %copy-start = (bf16[4,256,1024]{2,1,0:T(8,128)(2,1)S(1)}, bf16[4,256,1024]{2,1,0:T(8,128)(2,1)}, u32[]{:S(2)}) copy-start(bf16[4,256,1024]{2,1,0:T(8,128)(2,1)} %get-tuple-element.29) | copy-start | bytes 6291460
  121.8 13.6 %copy-start.1 = (bf16[1,2,64,1024]{3,2,1,0:T(8,128)(2,1)S(1)}, bf16[1,2,64,1024]{3,2,1,0:T(8,128)(2,1)}, u32[]{:S(2)}) copy-start(bf16[1,2,64,1024]{3,2,1,0:T(8,128)(2,1)} %param.9) | copy-start | bytes 786436
  147.6 8.7 %collective-permute-start.2 = (bf16[2,64,1024]{2,1,0:T(8,128)(2,1)S(1)}, bf16[2,64,1024]{2,1,0:T(8,128)(2,1)S(1)}, u32[]{:S(2)}, u32[]{:S(2)}) collective-permute-start(bf16[2,64,1024]{2,1,0:T(8,128)(2,1)S(1)} %bitcast.255), channel_id=1, source_target_pairs={{0,16},{1,17},{2,18},{3,19},{4,20},{5,21},{6,22},{7,23},{8,24},{9,... | collective-permute-start | bytes 786440 | tf_op jit(solution)/shard_map/ppermute | solution.py:18
  160.0 20.0 %copy-start.16 = (bf16[128,2048]{1,0:T(8,128)(2,1)}, bf16[128,2048]{1,0:T(8,128)(2,1)S(1)}, u32[]{:S(2)}) copy-start(bf16[128,2048]{1,0:T(8,128)(2,1)S(1)} %fusion.14.own_ref) | copy-start | bytes 1572868
  160.0 22.7 %collective-permute-start.3 = (bf16[128,2048]{1,0:T(8,128)(2,1)S(1)}, bf16[128,2048]{1,0:T(8,128)(2,1)}, u32[]{:S(2)}, u32[]{:S(2)}) collective-permute-start(bf16[128,2048]{1,0:T(8,128)(2,1)S(1)} %fusion.14.own_ref), channel_id=1, source_target_pairs={{0,4},{4,8},{8,12},{1,5},{5,9},{9,13},{2,6},{6,10},{10,14},{3,7},{... | collective-permute-start | bytes 1572872 | tf_op jit(solution)/shard_map/ppermute | solution.py:18
  192.0 7.9 %copy-start.13 = (bf16[128,1024]{1,0:T(8,128)(2,1)S(1)}, bf16[128,1024]{1,0:T(8,128)(2,1)}, u32[]{:S(2)}) copy-start(bf16[128,1024]{1,0:T(8,128)(2,1)} %attend.3.out_ref) | copy-start | bytes 786436
  200.9 118.2 %all-gather.10.cloned.1.call-start = ((), (), s32[]{:S(2)}) async-start(), calls=%async_computation.4 | async-start | bytes 1310720 | tf_op jit(solution)/shard_map/all_gather | solution.py:295
  230.0 38.8 %collective-permute-start.4 = (bf16[128,2048]{1,0:T(8,128)(2,1)}, bf16[128,2048]{1,0:T(8,128)(2,1)}, u32[]{:S(2)}, u32[]{:S(2)}) collective-permute-start(bf16[128,2048]{1,0:T(8,128)(2,1)} %bitcast.254), channel_id=1, source_target_pairs={{4,0},{8,4},{12,8},{5,1},{9,5},{13,9},{6,2},{10,6},{14,10},{7,3},{... | collective-permute-start | bytes 1572872 | tf_op jit(solution)/shard_map/ppermute | solution.py:18
  251.8 17.0 %copy-start.18 = (f32[128,2048]{1,0:T(8,128)S(1)}, f32[128,2048]{1,0:T(8,128)}, u32[]{:S(2)}) copy-start(f32[128,2048]{1,0:T(8,128)} %get-tuple-element.32) | copy-start | bytes 3145732
  276.0 9.2 %collective-permute-start.5 = (bf16[2,64,1024]{2,1,0:T(8,128)(2,1)S(1)}, bf16[2,64,1024]{2,1,0:T(8,128)(2,1)S(1)}, u32[]{:S(2)}, u32[]{:S(2)}) collective-permute-start(bf16[2,64,1024]{2,1,0:T(8,128)(2,1)S(1)} %bitcast.212), channel_id=1, source_target_pairs={{16,0},{17,1},{18,2},{19,3},{20,4},{21,5},{22,6},{23,7},{24,8},{25... | collective-permute-start | bytes 786440 | tf_op jit(solution)/shard_map/ppermute | solution.py:18
  285.3 8.1 %copy-start.7 = (bf16[2,64,1024]{2,1,0:T(8,128)(2,1)}, bf16[2,64,1024]{2,1,0:T(8,128)(2,1)S(1)}, u32[]{:S(2)}) copy-start(bf16[2,64,1024]{2,1,0:T(8,128)(2,1)S(1)} %get-tuple-element.69) | copy-start | bytes 786436
  293.4 100.7 %reduce-scatter.3.cloned.1.call-start = ((), (), s32[]{:S(2)}) async-start(), calls=%async_computation.5 | async-start | bytes 5242880 | tf_op jit(solution)/shard_map/reduce_scatter | solution.py:249
  335.9 16.2 %copy-start.10 = (f32[128,2048]{1,0:T(8,128)S(1)}, f32[128,2048]{1,0:T(8,128)}, u32[]{:S(2)}) copy-start(f32[128,2048]{1,0:T(8,128)} %get-tuple-element.39) | copy-start | bytes 3145732
  335.9 15.4 %collective-permute-start.6 = (bf16[128,2048]{1,0:T(8,128)(2,1)}, bf16[128,2048]{1,0:T(8,128)(2,1)S(1)}, u32[]{:S(2)}, u32[]{:S(2)}) collective-permute-start(bf16[128,2048]{1,0:T(8,128)(2,1)} %bitcast.253), channel_id=1, source_target_pairs={{4,0},{8,4},{12,8},{5,1},{9,5},{13,9},{6,2},{10,6},{14,10},{7,3},{... | collective-permute-start | bytes 1572872 | tf_op jit(solution)/shard_map/ppermute | solution.py:18
  359.8 27.6 %all-to-all-start = ((bf16[128,4,1024]{2,0,1:T(8,128)(2,1)}), bf16[128,4,1024]{2,0,1:T(8,128)(2,1)S(1)}, u32[]{:S(2)}, u32[]{:S(2)}) async-start(bf16[128,4,1024]{2,0,1:T(8,128)(2,1)} %pad_maximum_fusion.2), calls=%async_computation | async-start | bytes 2097152 | tf_op jit(solution)/shard_map/all_to_all | solution.py:470
  363.3 62.1 %reduce-scatter.5.cloned.1.call-start = ((), (), s32[]{:S(2)}) async-start(), calls=%async_computation.6 | async-start | bytes 2785280 | tf_op jit(solution)/shard_map/reduce_scatter | solution.py:249
  394.1 114.8 %copy-start.2 = (f32[128,4096]{0,1:T(8,128)S(1)}, f32[128,4096]{0,1:T(8,128)}, u32[]{:S(2)}) copy-start(f32[128,4096]{0,1:T(8,128)} %convolution_add_fusion) | copy-start | bytes 6291460
  394.2 113.4 %all-gather.12.cloned.1.call-start = ((), (), s32[]{:S(2)}) async-start(), calls=%async_computation.7 | async-start | bytes 5242880 | tf_op jit(solution)/shard_map/all_gather | solution.py:255
  394.8 160.6 %all-gather.14.cloned.1.call-start = ((), (), s32[]{:S(2)}) async-start(), calls=%async_computation.8 | async-start | bytes 2785280 | tf_op jit(solution)/shard_map/all_gather | solution.py:255
  (10 other events, 30.3 us)
Sparse Core Ops, SparseCore 0:
  201.0 73.8 all-gather.7
  293.5 25.5 all-gather.9
  336.0 43.9 reduce-scatter.2
  394.3 31.0 reduce-scatter.4
  426.8 80.7 all-gather.11
  509.0 46.2 all-gather.13

commit v2 on v1

--- a/solution.py
+++ b/solution.py
@@ -193,7 +193,7 @@
     return (output, (normed, query, own, halo, mixed, residual, normed_two, upper_act))
 
 
-def backward(incoming, entry_rows, params, saved, bias, beside=None):
+def backward(incoming, entry_rows, params, saved, bias):
     qkv_w, out_w, up_w, down_w, gain_vecs, vectors, up_vec = params
     normed, query, own, halo, mixed, residual, normed_two, upper_act = saved
     width = entry_rows.shape[-1]
@@ -215,8 +215,6 @@
         "re,de->rd", residual_round, out_w, preferred_element_type=jnp.float32
     ).astype(jnp.bfloat16)
     query_g, own_g, halo_g = attend_grad(query, own, halo, bias, mixed, mixed_g)
-    if beside is not None:
-        query_g, halo_g, beside = lax.optimization_barrier((query_g, halo_g, beside))
     chunks = halo_g.shape[0]
     for chunk in range(chunks):
         own_g = own_g + passed_along(halo_g[chunk], "seq", chunk - chunks).astype(jnp.float32)
@@ -236,68 +234,82 @@
         ),
         up_bias_g[None],
     )
-    joined = jnp.concatenate([query_g, own_g], axis=1)
-    return (residual_g + entry_part, residual_round, joined, vector_grads, beside)
-
-
-def rounded_blocks(partial):
-    owners = lax.axis_size("dp")
-    return partial.reshape(owners, -1, partial.shape[1]).astype(jnp.bfloat16)
-
-
-def summed_blocks(blocks):
-    return lax.psum_scatter(
-        blocks.reshape(-1, blocks.shape[2]), "dp", scatter_dimension=0, tiled=True
-    )
-
-
-def gathered_parts(own):
-    return lax.all_gather(own, "seq", axis=0, tiled=False)
-
-
-def own_columns(array, outer, inner):
-    index = lax.axis_index("seq")
-    rows = array.shape[0]
-    parts = array.reshape(rows, outer, inner, -1)
-    return lax.dynamic_index_in_dim(parts, index, 2, keepdims=False).reshape(rows, -1)
-
-
-def own_rows(array, outer, inner):
-    index = lax.axis_index("seq")
-    columns = array.shape[1]
-    parts = array.reshape(outer, inner, -1, columns)
-    return lax.dynamic_index_in_dim(parts, index, 1, keepdims=False).reshape(-1, columns)
-
-
-def feed_forward_grads(normed_two, incoming, params):
+    return (residual_g + entry_part, residual_round, query_g, own_g, vector_grads)
+
+
+def partner(array, by):
+    return lax.ppermute(array, "dp", [(i, i ^ by) for i in range(lax.axis_size("dp"))])
+
+
+def gathered_rows(values, axis=0):
+    return lax.all_gather(values, "seq", axis=axis, tiled=True)
+
+
+def gathered_tokens(rows):
+    line = gathered_rows(rows)
+    both = jnp.concatenate([line, partner(line, 2)])
+    return jnp.concatenate([both, partner(both, 1)])
+
+
+def blocks_of(array, by, axis=1):
+    index = lax.axis_index("dp")
+    size = array.shape[axis] // lax.axis_size("dp")
+    blocks = [
+        lax.dynamic_slice_in_dim(array, (index ^ which) * size, size, axis) for which in by
+    ]
+    return blocks[0] if len(blocks) == 1 else jnp.concatenate(blocks, axis=axis)
+
+
+def feed_forward_grads(all_normed_two, all_incoming, params):
     up_w, down_w, up_vec = params[2], params[3], params[6]
-    outer, inner = lax.axis_size("dp"), lax.axis_size("seq")
-    up_part = own_columns(up_w, outer, inner)
-    down_part = own_rows(down_w, outer, inner)
-    bias_part = own_columns(up_vec[None], outer, inner)[0]
-    upper_act = jnp.dot(normed_two, up_part, preferred_element_type=jnp.float32) + bias_part
-    hidden_f, gate_back = jax.vjp(smooth_gate, upper_act)
-    hidden = hidden_f.astype(jnp.bfloat16)
-    hidden_g = jnp.einsum("rd,fd->rf", incoming, down_part, preferred_element_type=jnp.float32)
-    upper_round = gate_back(hidden_g)[0].astype(jnp.bfloat16)
-    down_g = jnp.einsum("rf,rd->fd", hidden, incoming, preferred_element_type=jnp.float32)
-    up_g = jnp.einsum("rd,rf->df", normed_two, upper_round, preferred_element_type=jnp.float32)
-    return (up_g, down_g)
-
-
-def joined_columns(parts, outer_columns):
-    inner, rows, columns = parts.shape
-    ordered = parts.reshape(inner, rows, outer_columns, -1).transpose(1, 2, 0, 3)
-    return ordered.reshape(rows, inner * columns).astype(jnp.float32)
-
-
-def gathered_rows(values):
-    return lax.all_gather(values, "seq", axis=0, tiled=True)
-
-
-def by_owner(array, owners):
-    rows, columns = array.shape
-    return array.reshape(rows, owners, -1).transpose(1, 0, 2).reshape(owners, -1)
+    share = up_w.shape[0] // lax.axis_size("dp")
+    chip_columns = blocks_of(all_normed_two, (0, 1))
+    own, sent = [], []
+    for by in (0, 2):
+        up_part, down_part = blocks_of(up_w, (by,)), blocks_of(down_w, (by,), 0)
+        upper_act = jnp.dot(all_normed_two, up_part, preferred_element_type=jnp.float32)
+        upper_act = upper_act + blocks_of(up_vec[None], (by,))
+        hidden_f, gate_back = jax.vjp(smooth_gate, upper_act)
+        hidden_g = jnp.einsum(
+            "rd,fd->rf", all_incoming, down_part, preferred_element_type=jnp.float32
+        )
+        upper_round = gate_back(hidden_g)[0].astype(jnp.bfloat16)
+        if by == 0:
+            down_g = jnp.einsum(
+                "rf,rd->fd",
+                hidden_f.astype(jnp.bfloat16),
+                all_incoming,
+                preferred_element_type=jnp.float32,
+            )
+        up_g = jnp.einsum(
+            "rd,rf->df", chip_columns, upper_round, preferred_element_type=jnp.float32
+        )
+        own.append(up_g[:share])
+        sent.append(up_g[share:])
+    received = partner(jnp.concatenate(sent, axis=1), 1)
+    columns = own[0].shape[1]
+    index = lax.axis_index("dp")
+    total = jnp.zeros((share, up_w.shape[1]), jnp.float32)
+    for by, part in (
+        (0, own[0]),
+        (2, own[1]),
+        (1, received[:, :columns]),
+        (3, received[:, columns:]),
+    ):
+        total = lax.dynamic_update_slice_in_dim(total, part, (index ^ by) * columns, 1)
+    return (total, down_g)
+
+
+def summed_product(left, right):
+    line = gathered_rows(right)
+    other = partner(line, 1)
+    product = jnp.einsum("rd,re->de", left[0], line, preferred_element_type=jnp.float32)
+    product = product + jnp.einsum(
+        "rd,re->de", left[1], other, preferred_element_type=jnp.float32
+    )
+    share = product.shape[0] // 2
+    received = partner(product[share:].astype(jnp.bfloat16), 2)
+    return product[:share] + received.astype(jnp.float32)
 
 
 def piece_plan(shapes):
@@ -440,59 +452,36 @@
     entry_rows = jnp.where(leading, own_slot, received)
     last_output, saved = forward(entry_rows, params, bias)
     normed, query, own, halo, mixed, residual, normed_two, upper_act = saved
-    tokens_in = gathered_rows(jnp.concatenate([normed, normed_two, mixed], axis=1))
+    all_normed_two = gathered_tokens(normed_two)
+    mine = jnp.concatenate([blocks_of(normed, (0, 2)), blocks_of(mixed, (0, 2))], axis=1)
+    theirs = jnp.concatenate([blocks_of(normed, (1, 3)), blocks_of(mixed, (1, 3))], axis=1)
+    lefts = gathered_rows(jnp.stack([mine, partner(theirs, 1)]), 1)
+    normed_left, mixed_left = lefts[:, :, : width // 2], lefts[:, :, width // 2 :]
     early_entry = backward(own_slot, entry_rows, params, saved, bias)[0]
-    early_entry, tokens_in = lax.optimization_barrier((early_entry, tokens_in))
-    all_normed = tokens_in[:, :width]
-    all_normed_two = tokens_in[:, width : 2 * width]
-    all_mixed = tokens_in[:, 2 * width :]
     returned = passed_along(
         early_entry.astype(jnp.bfloat16).reshape(own_slot.shape), "section", -1
     )
     incoming = jnp.where(leading, returned, own_slot)
-    all_incoming = gathered_rows(incoming.reshape(-1, width))
-    up_g, down_g = feed_forward_grads(all_normed_two, all_incoming, params)
-    up_columns = up_g.shape[1]
-    gate_blocks = jnp.concatenate(
-        [rounded_blocks(up_g), rounded_blocks(down_g.reshape(width, -1))], axis=2
-    )
-    entry_g, residual_round, joined_heads, vector_grads, gate_blocks = backward(
-        incoming, entry_rows, params, saved, bias, gate_blocks
-    )
-    gate_own = summed_blocks(gate_blocks)
-    sent = jnp.concatenate(
+    all_incoming = gathered_tokens(incoming.reshape(-1, width))
+    entry_g, residual_round, query_g, own_g, vector_grads = backward(
+        incoming, entry_rows, params, saved, bias
+    )
+    out_total = summed_product(mixed_left, residual_round)
+    qkv_total = jnp.concatenate(
         [
-            joined_heads.reshape(-1, inner, 3 * width // inner),
-            residual_round.reshape(-1, inner, width // inner),
+            summed_product(normed_left, part)
+            for part in (query_g, own_g[:, :width], own_g[:, width:])
         ],
-        axis=2,
-    )
-    sent = lax.all_to_all(sent, "seq", split_axis=1, concat_axis=0, tiled=True)
-    sent = sent.reshape(-1, sent.shape[2])
-    joined_part, residual_part = sent[:, : 3 * width // inner], sent[:, 3 * width // inner :]
-    out_g = jnp.einsum("rd,re->de", all_mixed, residual_part, preferred_element_type=jnp.float32)
-    qkv_g = jnp.einsum("rd,re->de", all_normed, joined_part, preferred_element_type=jnp.float32)
-    matrix_part = jnp.concatenate([rounded_blocks(qkv_g), rounded_blocks(out_g)], axis=2)
-    vectors_g = jnp.concatenate([by_owner(part, outer) for part in vector_grads], axis=1)
-    columns, vector_size = matrix_part.shape[2], vectors_g.shape[1]
-    vector_rows = -(-vector_size // (16 * columns)) * 16
-    vectors_g = jnp.pad(vectors_g, ((0, 0), (0, vector_rows * columns - vector_size)))
-    vectors_g = rounded_blocks(vectors_g.reshape(-1, columns))
-    last_blocks = jnp.concatenate([matrix_part, vectors_g], axis=1)
-    last_blocks, gate_own = lax.optimization_barrier((last_blocks, gate_own))
-    gate_parts = gathered_parts(gate_own)
-    last_own, gate_parts = lax.optimization_barrier((summed_blocks(last_blocks), gate_parts))
-    up_total = joined_columns(gate_parts[:, :, :up_columns], outer)
-    down_total = gate_parts[:, :, up_columns:].reshape(-1, width).astype(jnp.float32)
-    parts = gathered_parts(last_own)
-    qkv_columns = qkv_g.shape[1]
-    qkv_total = joined_columns(parts[:, :share, :qkv_columns], 1)
-    out_total = joined_columns(parts[:, :share, qkv_columns:], 1)
-    own_vectors = jnp.sum(parts[:, share:].astype(jnp.float32), axis=0).reshape(-1)
-    gains_total = own_vectors[: gain_count * share].reshape(gain_count, share)
-    shifts_total = own_vectors[gain_count * share : (gain_count + shift_count) * share]
-    shifts_total = shifts_total.reshape(shift_count, share)
-    up_bias_total = own_vectors[(gain_count + shift_count) * share : vector_size]
+        axis=1,
+    )
+    up_total, down_total = feed_forward_grads(all_normed_two, all_incoming, params)
+    vectors_g = jnp.concatenate([part.reshape(-1) for part in vector_grads])
+    vectors_g = lax.psum(vectors_g, ("seq", "dp"))
+    gain_size, shift_size = gain_count * width, shift_count * width
+    gains_total = blocks_of(vectors_g[:gain_size].reshape(gain_count, width), (0,))
+    shifts_total = vectors_g[gain_size : gain_size + shift_size].reshape(shift_count, width)
+    shifts_total = blocks_of(shifts_total, (0,))
+    up_bias_total = blocks_of(vectors_g[gain_size + shift_size :][None], (0,))[0]
 
     ends_out = jnp.where(leading, entry_g, last_output).reshape(own_slot.shape)[None]
     return (

time: 588 us -> 644 us (1.095)
  matrix products: 108 us -> 180 us
  blocking collectives: 6.25 us -> 65.2 us
  local copies, waits for them, and re-layouts: 72.4 us -> 27.8 us
  waiting for transfers between devices: 200 us -> 171 us
  other arithmetic: 30.4 us -> 23.5 us
    psum x0 -> x1, blocking collectives: none -> 59.9 us  [shards(): vectors_g = lax.psum(vectors_g, ('seq', 'dp'))]
    dot_general x5 -> x13, matrix products: 20.7 us -> 78.7 us  [the longest x2 34 us: feed_forward_grads(): jnp.einsum('rd,rf->df', chip_columns, upper_round, preferred_element_type...]
    all_gather x4 -> x7, waiting for transfers between devices: 106 us -> 54.3 us  [gathered_rows(): return lax.all_gather(values, 'seq', axis=axis, tiled=True)]
    ppermute x0 -> x14, waiting for transfers between devices: none -> 48 us  [partner(): lax.ppermute(array, 'dp', [(i, i ^ by) for i in range(lax.axis_size('dp'))])]
    reduce_scatter x2 -> x0, waiting for transfers between devices: 30.6 us -> none  [summed_blocks(): lax.psum_scatter(blocks.reshape(-1, blocks.shape[2]), 'dp', scatter_dimen...]
    ppermute x7, waiting for transfers between devices: 38.9 us -> 67.4 us  [passed_along(): return lax.ppermute(array, axis, pairs)]
    all_to_all x1 -> x0, waiting for transfers between devices: 23.8 us -> none  [shards(): sent = lax.all_to_all(sent, 'seq', split_axis=1, concat_axis=0, tiled=True)]
    convert_element_type x5 -> x0, local copies, waits for them, and re-layouts: 22.2 us -> none  [joined_columns(): return ordered.reshape(rows, inner * columns).astype(jnp.float32)]
  transfers between devices with their start and end apart: 14 -> 28, of which waited for: 10 -> 14; matrix products, arithmetic and copies ran while one was open for 23% -> 17% of each run, Pallas kernels for 3% -> 15%
where the time goes in v2:
time: 644 us; the launch traced here: 634 us
  matrix products  180 us (28%)
  waiting for transfers between devices  171 us (27%)
  Pallas kernels  122 us (19%)
  blocking collectives  65.2 us (10%)
  starting transfers between devices  29.5 us (5%)
  local copies, waits for them, and re-layouts  27.8 us (4%)
  other arithmetic  23.5 us (4%)
  between operations  15.4 us (2%)
    pallas_call x1, Pallas kernels, gathered_weights(): pl.pallas_call(lambda *refs: gather_kernel(plan, count, *refs), out_shape...  89.3 us
    ppermute x7, waiting for transfers between devices, passed_along(): return lax.ppermute(array, axis, pairs)  67.4 us
    psum x1, blocking collectives, shards(): vectors_g = lax.psum(vectors_g, ('seq', 'dp'))  59.9 us
    all_gather x7, waiting for transfers between devices, gathered_rows(): return lax.all_gather(values, 'seq', axis=axis, tiled=True)  54.3 us
    ppermute x14, waiting for transfers between devices, partner(): lax.ppermute(array, 'dp', [(i, i ^ by) for i in range(lax.axis_size('dp'))])  48 us
    dot_general x2, matrix products, backward(): jnp.einsum('rf,df->rd', upper_g.astype(jnp.bfloat16), up_w, preferred_ele...  35.7 us
    dot_general x2, matrix products, feed_forward_grads(): jnp.einsum('rd,rf->df', chip_columns, upper_round, preferred_element_type...  34 us
    ppermute x7, starting transfers between devices, passed_along(): return lax.ppermute(array, axis, pairs)  21.4 us
  transfers between devices with their start and end apart: 28, of which 14 were waited for; matrix products, arithmetic and copies ran while one was open for 17% of the time, Pallas kernels for 15%

profile of v2, /device:TPU:0, one launch (start us, length us, event | category | flops | bytes accessed | tf_op | source)
XLA Modules:
  0.0 634.4 jit_solution(8382298123760600692)
XLA Ops:
  23.3 89.3 %gather_weights.1 = (bf16[4,256,3072]{2,1,0:T(8,128)(2,1)}, bf16[4,256,1024]{2,1,0:T(8,128)(2,1)}, bf16[4,256,4096]{2,1,0:T(8,128)(2,1)}, bf16[4,1024,1024]{2,1,0:T(8,128)(2,1)}) custom-call(bf16[256,3072]{1,0:T(8,128)(2,1)} %bitcast.199, bf16[256,1024]{1,0:T(8,128)(2,1)} %bitcast.200, bf16[256,4096]{1,0:T(8,128)(2,1)} %bitcast.197, bf16[1024,1024]{1,0:T(8,128)(2,1)} %bitcast.198), custom_call_target="tpu_custom_call" | custom-call | tf_op jit(solution)/shard_map/gather_weights/pallas_call | solution.py:411
  124.3 7.6 %collective-permute-done = bf16[128,2048]{1,0:T(8,128)(2,1)} collective-permute-done((bf16[128,2048]{1,0:T(8,128)(2,1)}, bf16[128,2048]{1,0:T(8,128)(2,1)}, u32[]{:S(2)}, u32[]{:S(2)}) %collective-permute-start) | collective-permute-done | bytes 524320 | tf_op jit(solution)/shard_map/ppermute | solution.py:18
  131.9 7.4 %attend.2 = bf16[128,1024]{1,0:T(8,128)(2,1)} custom-call(bf16[128,1024]{1,0:T(8,128)(2,1)} %fusion.99.query_ref, bf16[128,2048]{1,0:T(8,128)(2,1)} %fusion.38.own_ref, bf16[1,128,2048]{2,1,0:T(8,128)(2,1)} %bitcast.15.halo_ref, f32[2,64,128]{2,1,0:T(8,128)} %and_select_fusion.bias_ref), custom_call_target="tpu_custom_call" | custom-call | flops 1000000000 | bytes 10000000 | tf_op jit(solution)/shard_map/attend/pallas_call | solution.py:151
  141.0 10.5 %fusion.95 = bf16[128,1024]{1,0:T(8,128)(2,1)S(1)} fusion(f32[128,1024]{1,0:T(8,128)S(1)} %get-tuple-element.77, bf16[4096,1024]{1,0:T(8,128)(2,1)} %bitcast.185, bf16[1024,4096]{1,0:T(8,128)(2,1)} %bitcast.175, f32[4096]{0:T(1024)S(1)} %bitcast.215, f32[1024]{0:T(1024)S(1)} %bitcast.229, f32[1024]{0:T(1024)S(1)} %bitcast.231, f32[1024]{0:T(1024)S(1)} %bitcast.210, ...), kind=kOutput, calls=%fused_computation.98 | convolution fusion | flops 2153775104 | bytes 17593344 | tf_op jit(solution)/shard_map/dot_general | solution.py:192
  179.3 7.4 %attend.3.out_ref = bf16[128,1024]{1,0:T(8,128)(2,1)} custom-call(bf16[128,1024]{1,0:T(8,128)(2,1)} %fusion.96.query_ref, bf16[128,2048]{1,0:T(8,128)(2,1)} %copy-done.29, bf16[1,128,2048]{2,1,0:T(8,128)(2,1)} %bitcast.253, f32[2,64,128]{2,1,0:T(8,128)} %and_select_fusion.bias_ref), custom_call_target="tpu_custom_call" | custom-call | flops 1000000000 | bytes 10000000 | tf_op jit(solution)/shard_map/attend/pallas_call | solution.py:151
  188.6 8.0 %convolution_add_fusion = f32[128,4096]{0,1:T(8,128)} fusion(bf16[128,1024]{1,0:T(8,128)(2,1)S(1)} %add_convert_fusion.5, bf16[1024,4096]{1,0:T(8,128)(2,1)} %bitcast.176, f32[4096]{0:T(1024)S(1)} %bitcast.216), kind=kOutput, calls=%fused_computation.20 | convolution fusion | flops 1074266112 | bytes 10764288 | tf_op jit(solution)/shard_map/dot_general | solution.py:190
  196.5 29.1 %multiply_reduce_fusion.5 = (f32[128]{0:T(128)S(1)}, f32[128,1024]{1,0:T(8,128)}) fusion(f32[128,1024]{1,0:T(8,128)S(1)} %get-tuple-element.79, f32[128]{0:T(128)S(1)} %broadcast_multiply_fusion.2, f32[1024]{0:T(1024)S(1)} %bitcast.212, bf16[1024,4096]{1,0:T(8,128)(2,1)} %bitcast.177, f32[128,4096]{0,1:T(8,128)} %convolution_add_fusion, ...), kind=kOutput, calls=%fused_computation.166 | convolution fusion | flops 2158493696 | bytes 20190208 | tf_op jit(solution)/shard_map/rf,df->rd/dot_general | solution.py:206
  229.3 8.9 %attend_grad.2 = (bf16[128,1024]{1,0:T(8,128)(2,1)}, f32[128,2048]{1,0:T(8,128)}, bf16[1,128,2048]{2,1,0:T(8,128)(2,1)}) custom-call(bf16[128,1024]{1,0:T(8,128)(2,1)} %fusion.96.query_ref, bf16[128,2048]{1,0:T(8,128)(2,1)} %copy-done.29, bf16[1,128,2048]{2,1,0:T(8,128)(2,1)} %bitcast.254, f32[2,64,128]{2,1,0:T(8,128)} %and_select_fusion.bias_ref, ...), custom_call_target="tpu_custom_call" | custom-call | flops 1000000000 | bytes 10000000 | tf_op jit(solution)/shard_map/attend_grad/pallas_call | solution.py:162
  239.7 13.2 %collective-permute-done.4 = bf16[128,2048]{1,0:T(8,128)(2,1)S(1)} collective-permute-done((bf16[128,2048]{1,0:T(8,128)(2,1)}, bf16[128,2048]{1,0:T(8,128)(2,1)S(1)}, u32[]{:S(2)}, u32[]{:S(2)}) %collective-permute-start.4) | collective-permute-done | bytes 524320 | tf_op jit(solution)/shard_map/ppermute | solution.py:18
  269.6 7.3 %fusion.182 = (f32[4096]{0:T(1024)S(1)}, bf16[128,4096]{0,1:T(8,128)(2,1)S(1)}) fusion(f32[128,4096]{0,1:T(8,128)} %convolution_add_fusion, bf16[128,1024]{1,0:T(8,128)(2,1)S(1)} %bitcast.195, bf16[4096,1024]{1,0:T(8,128)(2,1)} %bitcast.187), kind=kOutput, calls=%fused_computation.277 | convolution fusion | flops 1084747776 | bytes 11812864 | tf_op jit(solution)/shard_map/rd,fd->rf/dot_general | solution.py:203
  287.2 9.0 %attend_grad.3 = (bf16[128,1024]{1,0:T(8,128)(2,1)}, f32[128,2048]{1,0:T(8,128)}, bf16[1,128,2048]{2,1,0:T(8,128)(2,1)}) custom-call(bf16[128,1024]{1,0:T(8,128)(2,1)} %fusion.96.query_ref, bf16[128,2048]{1,0:T(8,128)(2,1)} %copy-done.29, bf16[1,128,2048]{2,1,0:T(8,128)(2,1)} %bitcast.255, f32[2,64,128]{2,1,0:T(8,128)} %and_select_fusion.bias_ref, ...), custom_call_target="tpu_custom_call" | custom-call | flops 1000000000 | bytes 10000000 | tf_op jit(solution)/shard_map/attend_grad/pallas_call | solution.py:162
  298.8 27.3 %collective-permute-done.6 = bf16[128,2048]{1,0:T(8,128)(2,1)S(1)} collective-permute-done((bf16[128,2048]{1,0:T(8,128)(2,1)}, bf16[128,2048]{1,0:T(8,128)(2,1)S(1)}, u32[]{:S(2)}, u32[]{:S(2)}) %collective-permute-start.6) | collective-permute-done | bytes 524320 | tf_op jit(solution)/shard_map/ppermute | solution.py:18
  339.3 59.9 %psum.7 = f32[12288]{0:T(1024)S(1)} all-reduce(f32[12288]{0:T(1024)S(1)} %pad_maximum_fusion.8), channel_id=1, replica_groups=mesh['section'=2,'seq'=4,'dp'=4] {'seq','dp'}, use_global_device_ids=true, to_apply=%region_25.26 | all-reduce | flops 12288 | bytes 98304 | tf_op jit(solution)/shard_map/psum | solution.py:479
  414.9 14.0 %collective-permute-done.16 = bf16[512,1024]{1,0:T(8,128)(2,1)} collective-permute-done((bf16[512,1024]{1,0:T(8,128)(2,1)}, bf16[512,1024]{1,0:T(8,128)(2,1)}, u32[]{:S(2)}, u32[]{:S(2)}) %collective-permute-start.16) | collective-permute-done | bytes 1048608 | tf_op jit(solution)/shard_map/ppermute | solution.py:241
  434.4 7.1 %all-gather.13.cloned.1.call-done = bf16[512,1024]{1,0:T(8,128)(2,1)} async-done(((bf16[128,1024]{1,0:T(8,128)(2,1)}), bf16[512,1024]{1,0:T(8,128)(2,1)}) %all-gather.13.cloned.1.call-update) | async-done | bytes 1048592 | tf_op jit(solution)/shard_map/all_gather | solution.py:245
  441.5 47.2 %all-gather.9.cloned.1.call-done = bf16[2,512,1024]{2,1,0:T(8,128)(2,1)} async-done(((bf16[2,128,1024]{2,1,0:T(8,128)(2,1)}), bf16[2,512,1024]{2,1,0:T(8,128)(2,1)}) %all-gather.9.cloned.1.call-update) | async-done | bytes 2097168 | tf_op jit(solution)/shard_map/all_gather | solution.py:245
  510.4 9.6 %collective-permute-done.15 = bf16[256,1024]{1,0:T(8,128)(2,1)S(1)} collective-permute-done((bf16[256,1024]{1,0:T(8,128)(2,1)S(1)}, bf16[256,1024]{1,0:T(8,128)(2,1)S(1)}, u32[]{:S(2)}, u32[]{:S(2)}) %collective-permute-start.15) | collective-permute-done | bytes 524320 | tf_op jit(solution)/shard_map/ppermute | solution.py:241
  521.1 10.1 %collective-permute-done.13 = bf16[256,1024]{1,0:T(8,128)(2,1)S(1)} collective-permute-done((bf16[256,1024]{1,0:T(8,128)(2,1)S(1)}, bf16[256,1024]{1,0:T(8,128)(2,1)S(1)}, u32[]{:S(2)}, u32[]{:S(2)}) %collective-permute-start.13) | collective-permute-done | bytes 524320 | tf_op jit(solution)/shard_map/ppermute | solution.py:241
  531.4 9.8 %collective-permute-done.11 = bf16[256,1024]{1,0:T(8,128)(2,1)S(1)} collective-permute-done((bf16[256,1024]{1,0:T(8,128)(2,1)S(1)}, bf16[256,1024]{1,0:T(8,128)(2,1)S(1)}, u32[]{:S(2)}, u32[]{:S(2)}) %collective-permute-start.11) | collective-permute-done | bytes 524320 | tf_op jit(solution)/shard_map/ppermute | solution.py:241
  548.4 10.8 %fusion.58 = f32[2048,1024]{1,0:T(8,128)} fusion(bf16[2048,1024]{1,0:T(8,128)(2,1)} %constant_dynamic-update-slice_fusion, bf16[1024,4096]{1,0:T(8,128)(2,1)} %bitcast.179, s32[]{:T(128)S(6)} %select_n.83), kind=kOutput, calls=%fused_computation.62 | convolution fusion | flops 4294967296 | bytes 14680068 | tf_op jit(solution)/shard_map/dot_general | solution.py:270
  559.4 9.9 %fusion.56 = f32[2048,1024]{1,0:T(8,128)} fusion(bf16[2048,1024]{1,0:T(8,128)(2,1)S(1)} %constant_dynamic-update-slice_fusion.3, bf16[4096,1024]{1,0:T(8,128)(2,1)} %bitcast.189, s32[]{:T(128)S(6)} %select_n.84), kind=kOutput, calls=%fused_computation.60 | convolution fusion | flops 4294967296 | bytes 14680068 | tf_op jit(solution)/shard_map/rd,fd->rf/dot_general | solution.py:273
  569.4 17.0 %fusion.17 = f32[512,1024]{1,0:T(8,128)} fusion(f32[2048,1024]{1,0:T(8,128)} %fusion.58, f32[1024]{0:T(1024)S(1)} %bitcast.236, bf16[2048,1024]{1,0:T(8,128)(2,1)} %copy-done.26, bf16[4096,1024]{1,0:T(8,128)(2,1)} %bitcast.190, s32[]{:T(128)S(6)} %select_n.83, bf16[2048,256]{1,0:T(8,128)(2,1)} %get-tuple-element.53, bf16[2048,256]{1,0:T(8,128)(2,1)} %get-tuple-element.52), kind=kOutput, calls=%fused_computation.24 | convolution fusion | flops 6490685440 | bytes 18878468 | tf_op jit(solution)/shard_map/rd,rf->df/dot_general | solution.py:284
  588.7 17.0 %fusion.15 = f32[512,1024]{1,0:T(8,128)} fusion(f32[2048,1024]{1,0:T(8,128)} %fusion.56, f32[1024]{0:T(1024)S(1)} %bitcast.238, bf16[2048,1024]{1,0:T(8,128)(2,1)} %constant_dynamic-update-slice_fusion, bf16[1024,4096]{1,0:T(8,128)(2,1)} %bitcast.180, s32[]{:T(128)S(6)} %select_n.84, bf16[2048,256]{1,0:T(8,128)(2,1)} %get-tuple-element.53, ...), kind=kOutput, calls=%fused_computation.23 | convolution fusion | flops 6490685440 | bytes 18878468 | tf_op jit(solution)/shard_map/rd,rf->df/dot_general | solution.py:284
  613.4 11.5 %fusion.41 = f32[1,1024,1024]{2,1,0:T(8,128)} fusion(bf16[2048,1024]{1,0:T(8,128)(2,1)S(1)} %copy-done.27, f32[2048,1024]{1,0:T(8,128)} %fusion.58, f32[1024]{0:T(1024)S(1)} %bitcast.237), kind=kOutput, calls=%fused_computation.42 | convolution fusion | flops 4315938816 | bytes 16781312 | tf_op jit(solution)/shard_map/rf,rd->fd/dot_general | solution.py:278
  (249 shorter events, 170.0 us)
Async XLA Ops:
  7.2 395.4 %all-gather.19.cloned.1.call-start = ((), (), s32[]{:S(2)}) async-start(), calls=%async_computation.5 | async-start | bytes 1310720 | tf_op jit(solution)/shard_map/all_gather | solution.py:245
  7.2 116.3 %collective-permute-start.1 = (s32[2,64]{1,0:T(2,128)}, s32[2,64]{1,0:T(2,128)S(1)}, u32[]{:S(2)}, u32[]{:S(2)}) collective-permute-start(s32[2,64]{1,0:T(2,128)} %param.10), channel_id=1, source_target_pairs={{0,4},{4,8},{8,12},{1,5},{5,9},{9,13},{2,6},{6,10},{10,14},{3,7},{... | collective-permute-start | bytes 1544 | tf_op jit(solution)/shard_map/ppermute | solution.py:18
  116.3 15.6 %collective-permute-start = (bf16[128,2048]{1,0:T(8,128)(2,1)}, bf16[128,2048]{1,0:T(8,128)(2,1)}, u32[]{:S(2)}, u32[]{:S(2)}) collective-permute-start(bf16[128,2048]{1,0:T(8,128)(2,1)} %fusion.38.own_ref), channel_id=1, source_target_pairs={{0,4},{4,8},{8,12},{1,5},{5,9},{9,13},{2,6},{6,10},{10,14},{3,7},{... | collective-permute-start | bytes 1572872 | tf_op jit(solution)/shard_map/ppermute | solution.py:18
  238.3 14.6 %collective-permute-start.4 = (bf16[128,2048]{1,0:T(8,128)(2,1)}, bf16[128,2048]{1,0:T(8,128)(2,1)S(1)}, u32[]{:S(2)}, u32[]{:S(2)}) collective-permute-start(bf16[128,2048]{1,0:T(8,128)(2,1)} %bitcast.257), channel_id=1, source_target_pairs={{4,0},{8,4},{12,8},{5,1},{9,5},{13,9},{6,2},{10,6},{14,10},{7,3},{... | collective-permute-start | bytes 1572872 | tf_op jit(solution)/shard_map/ppermute | solution.py:18
  261.5 141.6 %all-gather.11.cloned.1.call-start = ((), (), s32[]{:S(2)}) async-start(), calls=%async_computation.1 | async-start | bytes 1310720 | tf_op jit(solution)/shard_map/all_gather | solution.py:245
  296.2 114.2 %all-gather.21.cloned.1.call-start = ((), (), s32[]{:S(2)}) async-start(), calls=%async_computation.6 | async-start | bytes 1310720 | tf_op jit(solution)/shard_map/all_gather | solution.py:245
  296.9 115.5 %all-gather.17.cloned.1.call-start = ((), (), s32[]{:S(2)}) async-start(), calls=%async_computation.4 | async-start | bytes 1310720 | tf_op jit(solution)/shard_map/all_gather | solution.py:245
  297.5 136.4 %all-gather.15.cloned.1.call-start = ((), (), s32[]{:S(2)}) async-start(), calls=%async_computation.3 | async-start | bytes 1310720 | tf_op jit(solution)/shard_map/all_gather | solution.py:245
  297.5 28.6 %collective-permute-start.6 = (bf16[128,2048]{1,0:T(8,128)(2,1)}, bf16[128,2048]{1,0:T(8,128)(2,1)S(1)}, u32[]{:S(2)}, u32[]{:S(2)}) collective-permute-start(bf16[128,2048]{1,0:T(8,128)(2,1)} %bitcast.256), channel_id=1, source_target_pairs={{4,0},{8,4},{12,8},{5,1},{9,5},{13,9},{6,2},{10,6},{14,10},{7,3},{... | collective-permute-start | bytes 1572872 | tf_op jit(solution)/shard_map/ppermute | solution.py:18
  328.4 113.0 %all-gather.13.cloned.1.call-start = ((), (), s32[]{:S(2)}) async-start(), calls=%async_computation.2 | async-start | bytes 1310720 | tf_op jit(solution)/shard_map/all_gather | solution.py:245
  329.0 159.7 %all-gather.9.cloned.1.call-start = ((), (), s32[]{:S(2)}) async-start(), calls=%async_computation | async-start | bytes 2621440 | tf_op jit(solution)/shard_map/all_gather | solution.py:245
  402.5 26.4 %collective-permute-start.16 = (bf16[512,1024]{1,0:T(8,128)(2,1)}, bf16[512,1024]{1,0:T(8,128)(2,1)}, u32[]{:S(2)}, u32[]{:S(2)}) collective-permute-start(bf16[512,1024]{1,0:T(8,128)(2,1)} %all-gather.19.cloned.1.call-done), channel_id=1, source_target_pairs={{0,2},{1,3},{2,0},{3,1},{4,6},{5,7},{6,4},{7,5},{8,10},{9,11},{10,... | collective-permute-start | bytes 3145736 | tf_op jit(solution)/shard_map/ppermute | solution.py:241
  403.1 38.3 %collective-permute-start.8 = (bf16[512,1024]{1,0:T(8,128)(2,1)}, bf16[512,1024]{1,0:T(8,128)(2,1)}, u32[]{:S(2)}, u32[]{:S(2)}) collective-permute-start(bf16[512,1024]{1,0:T(8,128)(2,1)} %all-gather.11.cloned.1.call-done), channel_id=1, source_target_pairs={{0,1},{1,0},{2,3},{3,2},{4,5},{5,4},{6,7},{7,6},{8,9},{9,8},{10,11... | collective-permute-start | bytes 3145736 | tf_op jit(solution)/shard_map/ppermute | solution.py:241
  410.4 88.6 %collective-permute-start.18 = (bf16[512,1024]{1,0:T(8,128)(2,1)}, bf16[512,1024]{1,0:T(8,128)(2,1)S(1)}, u32[]{:S(2)}, u32[]{:S(2)}) collective-permute-start(bf16[512,1024]{1,0:T(8,128)(2,1)} %all-gather.21.cloned.1.call-done), channel_id=1, source_target_pairs={{0,2},{1,3},{2,0},{3,1},{4,6},{5,7},{6,4},{7,5},{8,10},{9,11},{10,... | collective-permute-start | bytes 3145736 | tf_op jit(solution)/shard_map/ppermute | solution.py:241
  412.4 81.5 %collective-permute-start.14 = (bf16[512,1024]{1,0:T(8,128)(2,1)}, bf16[512,1024]{1,0:T(8,128)(2,1)}, u32[]{:S(2)}, u32[]{:S(2)}) collective-permute-start(bf16[512,1024]{1,0:T(8,128)(2,1)} %all-gather.17.cloned.1.call-done), channel_id=1, source_target_pairs={{0,1},{1,0},{2,3},{3,2},{4,5},{5,4},{6,7},{7,6},{8,9},{9,8},{10,11... | collective-permute-start | bytes 3145736 | tf_op jit(solution)/shard_map/ppermute | solution.py:241
  431.6 110.7 %collective-permute-start.17 = (bf16[1024,1024]{1,0:T(8,128)(2,1)}, bf16[1024,1024]{1,0:T(8,128)(2,1)}, u32[]{:S(2)}, u32[]{:S(2)}) collective-permute-start(bf16[1024,1024]{1,0:T(8,128)(2,1)} %pad_maximum_fusion), channel_id=1, source_target_pairs={{0,1},{1,0},{2,3},{3,2},{4,5},{5,4},{6,7},{7,6},{8,9},{9,8},{10,11... | collective-permute-start | bytes 6291464 | tf_op jit(solution)/shard_map/ppermute | solution.py:241
  433.9 66.4 %collective-permute-start.12 = (bf16[512,1024]{1,0:T(8,128)(2,1)}, bf16[512,1024]{1,0:T(8,128)(2,1)}, u32[]{:S(2)}, u32[]{:S(2)}) collective-permute-start(bf16[512,1024]{1,0:T(8,128)(2,1)} %all-gather.15.cloned.1.call-done), channel_id=1, source_target_pairs={{0,1},{1,0},{2,3},{3,2},{4,5},{5,4},{6,7},{7,6},{8,9},{9,8},{10,11... | collective-permute-start | bytes 3145736 | tf_op jit(solution)/shard_map/ppermute | solution.py:241
  441.4 61.0 %collective-permute-start.10 = (bf16[512,1024]{1,0:T(8,128)(2,1)}, bf16[512,1024]{1,0:T(8,128)(2,1)}, u32[]{:S(2)}, u32[]{:S(2)}) collective-permute-start(bf16[512,1024]{1,0:T(8,128)(2,1)} %all-gather.13.cloned.1.call-done), channel_id=1, source_target_pairs={{0,1},{1,0},{2,3},{3,2},{4,5},{5,4},{6,7},{7,6},{8,9},{9,8},{10,11... | collective-permute-start | bytes 3145736 | tf_op jit(solution)/shard_map/ppermute | solution.py:241
  493.9 14.9 %collective-permute-start.9 = (bf16[256,1024]{1,0:T(8,128)(2,1)S(1)}, bf16[256,1024]{1,0:T(8,128)(2,1)S(1)}, u32[]{:S(2)}, u32[]{:S(2)}) collective-permute-start(bf16[256,1024]{1,0:T(8,128)(2,1)S(1)} %slice.321), channel_id=1, source_target_pairs={{0,2},{1,3},{2,0},{3,1},{4,6},{5,7},{6,4},{7,5},{8,10},{9,11},{10,... | collective-permute-start | bytes 1572872 | tf_op jit(solution)/shard_map/ppermute | solution.py:241
  499.0 21.0 %collective-permute-start.15 = (bf16[256,1024]{1,0:T(8,128)(2,1)S(1)}, bf16[256,1024]{1,0:T(8,128)(2,1)S(1)}, u32[]{:S(2)}, u32[]{:S(2)}) collective-permute-start(bf16[256,1024]{1,0:T(8,128)(2,1)S(1)} %slice.318), channel_id=1, source_target_pairs={{0,2},{1,3},{2,0},{3,1},{4,6},{5,7},{6,4},{7,5},{8,10},{9,11},{10,... | collective-permute-start | bytes 1572872 | tf_op jit(solution)/shard_map/ppermute | solution.py:241
  500.3 59.0 %collective-permute-start.19 = (bf16[1024,1024]{1,0:T(8,128)(2,1)S(1)}, bf16[1024,1024]{1,0:T(8,128)(2,1)S(1)}, u32[]{:S(2)}, u32[]{:S(2)}) collective-permute-start(bf16[1024,1024]{1,0:T(8,128)(2,1)S(1)} %pad_maximum_fusion.2), channel_id=1, source_target_pairs={{0,1},{1,0},{2,3},{3,2},{4,5},{5,4},{6,7},{7,6},{8,9},{9,8},{10,11... | collective-permute-start | bytes 6291464 | tf_op jit(solution)/shard_map/ppermute | solution.py:241
  502.4 28.8 %collective-permute-start.13 = (bf16[256,1024]{1,0:T(8,128)(2,1)S(1)}, bf16[256,1024]{1,0:T(8,128)(2,1)S(1)}, u32[]{:S(2)}, u32[]{:S(2)}) collective-permute-start(bf16[256,1024]{1,0:T(8,128)(2,1)S(1)} %slice.319), channel_id=1, source_target_pairs={{0,2},{1,3},{2,0},{3,1},{4,6},{5,7},{6,4},{7,5},{8,10},{9,11},{10,... | collective-permute-start | bytes 1572872 | tf_op jit(solution)/shard_map/ppermute | solution.py:241
  508.8 32.4 %collective-permute-start.11 = (bf16[256,1024]{1,0:T(8,128)(2,1)S(1)}, bf16[256,1024]{1,0:T(8,128)(2,1)S(1)}, u32[]{:S(2)}, u32[]{:S(2)}) collective-permute-start(bf16[256,1024]{1,0:T(8,128)(2,1)S(1)} %slice.320), channel_id=1, source_target_pairs={{0,2},{1,3},{2,0},{3,1},{4,6},{5,7},{6,4},{7,5},{8,10},{9,11},{10,... | collective-permute-start | bytes 1572872 | tf_op jit(solution)/shard_map/ppermute | solution.py:241
  608.5 16.4 %collective-permute-start.20 = (f32[256,2048]{1,0:T(8,128)S(1)}, f32[256,2048]{1,0:T(8,128)S(1)}, u32[]{:S(2)}, u32[]{:S(2)}) collective-permute-start(f32[256,2048]{1,0:T(8,128)S(1)} %pad_maximum_fusion.3), channel_id=1, source_target_pairs={{0,1},{1,0},{2,3},{3,2},{4,5},{5,4},{6,7},{7,6},{8,9},{9,8},{10,11... | collective-permute-start | bytes 6291464 | tf_op jit(solution)/shard_map/ppermute | solution.py:241
  (36 other events, 482.5 us)
Sparse Core Ops, SparseCore 0:
  261.6 29.2 all-gather.18
  296.3 30.6 all-gather.10
  328.5 26.4 all-gather.20
  356.4 27.4 all-gather.16
  385.3 27.2 all-gather.14
  414.1 27.3 all-gather.12
  443.6 45.0 all-gather.8

commit v3 on v2

--- a/solution.py
+++ b/solution.py
@@ -245,8 +245,7 @@
     return lax.all_gather(values, "seq", axis=axis, tiled=True)
 
 
-def gathered_tokens(rows):
-    line = gathered_rows(rows)
+def gathered_tokens(line):
     both = jnp.concatenate([line, partner(line, 2)])
     return jnp.concatenate([both, partner(both, 1)])
 
@@ -260,56 +259,55 @@
     return blocks[0] if len(blocks) == 1 else jnp.concatenate(blocks, axis=axis)
 
 
-def feed_forward_grads(all_normed_two, all_incoming, params):
+def feed_forward_block(all_normed_two, all_incoming, params, by):
     up_w, down_w, up_vec = params[2], params[3], params[6]
-    share = up_w.shape[0] // lax.axis_size("dp")
+    up_part, down_part = blocks_of(up_w, (by,)), blocks_of(down_w, (by,), 0)
+    upper_act = jnp.dot(all_normed_two, up_part, preferred_element_type=jnp.float32)
+    upper_act = upper_act + blocks_of(up_vec[None], (by,))
+    hidden_f, gate_back = jax.vjp(smooth_gate, upper_act)
+    hidden_g = jnp.einsum("rd,fd->rf", all_incoming, down_part, preferred_element_type=jnp.float32)
+    upper_round = lax.optimization_barrier(gate_back(hidden_g)[0].astype(jnp.bfloat16))
     chip_columns = blocks_of(all_normed_two, (0, 1))
-    own, sent = [], []
-    for by in (0, 2):
-        up_part, down_part = blocks_of(up_w, (by,)), blocks_of(down_w, (by,), 0)
-        upper_act = jnp.dot(all_normed_two, up_part, preferred_element_type=jnp.float32)
-        upper_act = upper_act + blocks_of(up_vec[None], (by,))
-        hidden_f, gate_back = jax.vjp(smooth_gate, upper_act)
-        hidden_g = jnp.einsum(
-            "rd,fd->rf", all_incoming, down_part, preferred_element_type=jnp.float32
-        )
-        upper_round = gate_back(hidden_g)[0].astype(jnp.bfloat16)
-        if by == 0:
-            down_g = jnp.einsum(
-                "rf,rd->fd",
-                hidden_f.astype(jnp.bfloat16),
-                all_incoming,
-                preferred_element_type=jnp.float32,
-            )
-        up_g = jnp.einsum(
-            "rd,rf->df", chip_columns, upper_round, preferred_element_type=jnp.float32
-        )
-        own.append(up_g[:share])
-        sent.append(up_g[share:])
-    received = partner(jnp.concatenate(sent, axis=1), 1)
-    columns = own[0].shape[1]
-    index = lax.axis_index("dp")
-    total = jnp.zeros((share, up_w.shape[1]), jnp.float32)
+    up_g = jnp.einsum("rd,rf->df", chip_columns, upper_round, preferred_element_type=jnp.float32)
+    if by:
+        return up_g
+    hidden = hidden_f.astype(jnp.bfloat16)
+    down_g = jnp.einsum("rf,rd->fd", hidden, all_incoming, preferred_element_type=jnp.float32)
+    return (up_g, down_g)
+
+
+def up_blocks(own_first, own_second, received, share):
+    columns = own_first.shape[1]
+    index, count = lax.axis_index("dp"), lax.axis_size("dp")
+    total = jnp.zeros((share, count * columns), jnp.float32)
     for by, part in (
-        (0, own[0]),
-        (2, own[1]),
+        (0, own_first[:share]),
+        (2, own_second[:share]),
         (1, received[:, :columns]),
         (3, received[:, columns:]),
     ):
         total = lax.dynamic_update_slice_in_dim(total, part, (index ^ by) * columns, 1)
-    return (total, down_g)
-
-
-def summed_product(left, right):
-    line = gathered_rows(right)
-    other = partner(line, 1)
-    product = jnp.einsum("rd,re->de", left[0], line, preferred_element_type=jnp.float32)
-    product = product + jnp.einsum(
-        "rd,re->de", left[1], other, preferred_element_type=jnp.float32
-    )
-    share = product.shape[0] // 2
-    received = partner(product[share:].astype(jnp.bfloat16), 2)
-    return product[:share] + received.astype(jnp.float32)
+    return total
+
+
+def product(left, line, other):
+    total = jnp.einsum("rd,re->de", left[0], line, preferred_element_type=jnp.float32)
+    return total + jnp.einsum("rd,re->de", left[1], other, preferred_element_type=jnp.float32)
+
+
+def summed_shares(vector):
+    for by in (1, 2):
+        vector = vector + partner(vector, by)
+    by, count = 1, lax.axis_size("seq")
+    while by < count:
+        vector = vector + lax.ppermute(vector, "seq", [(i, i ^ by) for i in range(count)])
+        by *= 2
+    return vector
+
+
+def by_owner(array, owners):
+    rows, columns = array.shape
+    return array.reshape(rows, owners, -1).transpose(1, 0, 2).reshape(owners, -1)
 
 
 def piece_plan(shapes):
@@ -452,36 +450,56 @@
     entry_rows = jnp.where(leading, own_slot, received)
     last_output, saved = forward(entry_rows, params, bias)
     normed, query, own, halo, mixed, residual, normed_two, upper_act = saved
-    all_normed_two = gathered_tokens(normed_two)
+    normed_two_line = gathered_rows(normed_two)
     mine = jnp.concatenate([blocks_of(normed, (0, 2)), blocks_of(mixed, (0, 2))], axis=1)
     theirs = jnp.concatenate([blocks_of(normed, (1, 3)), blocks_of(mixed, (1, 3))], axis=1)
     lefts = gathered_rows(jnp.stack([mine, partner(theirs, 1)]), 1)
-    normed_left, mixed_left = lefts[:, :, : width // 2], lefts[:, :, width // 2 :]
     early_entry = backward(own_slot, entry_rows, params, saved, bias)[0]
     returned = passed_along(
         early_entry.astype(jnp.bfloat16).reshape(own_slot.shape), "section", -1
     )
     incoming = jnp.where(leading, returned, own_slot)
-    all_incoming = gathered_tokens(incoming.reshape(-1, width))
+    incoming_rows, normed_two_line, lefts = lax.optimization_barrier(
+        (incoming.reshape(-1, width), normed_two_line, lefts)
+    )
+    normed_left, mixed_left = lefts[:, :, : width // 2], lefts[:, :, width // 2 :]
+    incoming_line = gathered_rows(incoming_rows)
     entry_g, residual_round, query_g, own_g, vector_grads = backward(
         incoming, entry_rows, params, saved, bias
     )
-    out_total = summed_product(mixed_left, residual_round)
+    first_line = gathered_rows(jnp.concatenate([residual_round, query_g], axis=1))
+    second_line = gathered_rows(own_g)
+    all_normed_two = gathered_tokens(normed_two_line)
+    all_incoming = gathered_tokens(incoming_line)
+    up_first, down_total = feed_forward_block(all_normed_two, all_incoming, params, 0)
+    up_first, down_total, first_line = lax.optimization_barrier((up_first, down_total, first_line))
+    first_other = partner(first_line, 1)
+    up_second = feed_forward_block(all_normed_two, all_incoming, params, 2)
+    up_sent = partner(jnp.concatenate([up_first[share:], up_second[share:]], axis=1), 1)
+    out_g = product(mixed_left, first_line[:, :width], first_other[:, :width])
+    query_wg = product(normed_left, first_line[:, width:], first_other[:, width:])
+    first_sent = jnp.concatenate([out_g[share:], query_wg[share:]], axis=1).astype(jnp.bfloat16)
+    first_sent = partner(first_sent, 2)
+    up_second, second_line = lax.optimization_barrier((up_second, second_line))
+    second_other = partner(second_line, 1)
+    own_wg = product(normed_left, second_line, second_other)
+    second_sent = partner(own_wg[share:].astype(jnp.bfloat16), 2)
+    out_total = out_g[:share] + first_sent[:, :width].astype(jnp.float32)
     qkv_total = jnp.concatenate(
         [
-            summed_product(normed_left, part)
-            for part in (query_g, own_g[:, :width], own_g[:, width:])
+            query_wg[:share] + first_sent[:, width:].astype(jnp.float32),
+            own_wg[:share] + second_sent.astype(jnp.float32),
         ],
         axis=1,
     )
-    up_total, down_total = feed_forward_grads(all_normed_two, all_incoming, params)
-    vectors_g = jnp.concatenate([part.reshape(-1) for part in vector_grads])
-    vectors_g = lax.psum(vectors_g, ("seq", "dp"))
-    gain_size, shift_size = gain_count * width, shift_count * width
-    gains_total = blocks_of(vectors_g[:gain_size].reshape(gain_count, width), (0,))
-    shifts_total = vectors_g[gain_size : gain_size + shift_size].reshape(shift_count, width)
-    shifts_total = blocks_of(shifts_total, (0,))
-    up_bias_total = blocks_of(vectors_g[gain_size + shift_size :][None], (0,))[0]
+    up_total = up_blocks(up_first, up_second, up_sent, share)
+    vectors_g = jnp.concatenate([by_owner(part, outer) for part in vector_grads], axis=1)
+    summed = summed_shares(vectors_g.reshape(-1, 128)).reshape(outer, -1)
+    own_vectors = lax.dynamic_index_in_dim(summed, lax.axis_index("dp"), 0, keepdims=False)
+    gains_total = own_vectors[: gain_count * share].reshape(gain_count, share)
+    shifts_total = own_vectors[gain_count * share : (gain_count + shift_count) * share]
+    shifts_total = shifts_total.reshape(shift_count, share)
+    up_bias_total = own_vectors[(gain_count + shift_count) * share :]
 
     ends_out = jnp.where(leading, entry_g, last_output).reshape(own_slot.shape)[None]
     return (

time: 644 us -> 532 us (0.83)
  blocking collectives: 65.2 us -> 6.25 us
  matrix products: 180 us -> 149 us
  waiting for transfers between devices: 171 us -> 141 us
  starting transfers between devices: 29.5 us -> 41.9 us
  local copies, waits for them, and re-layouts: 27.8 us -> 18.9 us
    psum x1 -> x0, blocking collectives: 59.9 us -> none  [shards(): vectors_g = lax.psum(vectors_g, ('seq', 'dp'))]
    all_gather x7 -> x5, waiting for transfers between devices: 54.3 us -> 7.94 us  [gathered_rows(): return lax.all_gather(values, 'seq', axis=axis, tiled=True)]
    ppermute x14 -> x12, waiting for transfers between devices: 48 us -> 75.6 us  [partner(): lax.ppermute(array, 'dp', [(i, i ^ by) for i in range(lax.axis_size('dp'))])]
    dot_general x13, matrix products: 78.7 us -> 61.5 us  [the longest x2 25 us: feed_forward_block(): jnp.einsum('rd,fd->rf', all_incoming, down_part, preferred_element_type=j...]
    ppermute x7, waiting for transfers between devices: 67.4 us -> 51.3 us  [passed_along(): return lax.ppermute(array, axis, pairs)]
    dot_general x2, matrix products: 35.7 us -> 22.3 us  [backward(): jnp.einsum('rf,df->rd', upper_g.astype(jnp.bfloat16), up_w, preferred_ele...]
    ppermute x7, starting transfers between devices: 21.4 us -> 31.3 us  [passed_along(): return lax.ppermute(array, axis, pairs)]
  transfers between devices with their start and end apart: 28 -> 26, of which waited for: 14 -> 13; matrix products, arithmetic and copies ran while one was open for 17% -> 29% of each run, Pallas kernels for 15% -> 3%
where the time goes in v3:
time: 532 us; the launch traced here: 523 us
  matrix products  149 us (28%)
  waiting for transfers between devices  141 us (27%)
  Pallas kernels  122 us (23%)
  starting transfers between devices  41.9 us (8%)
  other arithmetic  28 us (5%)
  local copies, waits for them, and re-layouts  18.9 us (4%)
  between operations  15.1 us (3%)
  blocking collectives  6.25 us (1%)
    pallas_call x1, Pallas kernels, gathered_weights(): pl.pallas_call(lambda *refs: gather_kernel(plan, count, *refs), out_shape...  89.8 us
    ppermute x12, waiting for transfers between devices, partner(): lax.ppermute(array, 'dp', [(i, i ^ by) for i in range(lax.axis_size('dp'))])  75.6 us
    ppermute x7, waiting for transfers between devices, passed_along(): return lax.ppermute(array, axis, pairs)  51.3 us
    ppermute x7, starting transfers between devices, passed_along(): return lax.ppermute(array, axis, pairs)  31.3 us
    dot_general x2, matrix products, feed_forward_block(): jnp.einsum('rd,fd->rf', all_incoming, down_part, preferred_element_type=j...  25 us
    dot_general x2, matrix products, backward(): jnp.einsum('rf,df->rd', upper_g.astype(jnp.bfloat16), up_w, preferred_ele...  22.3 us
    pallas_call x2, Pallas kernels, attend_grad(): pl.pallas_call(attend_grad_kernel, out_shape=(jax.ShapeDtypeStruct(query....  18 us
    dot_general x2, matrix products, forward(): jnp.dot(hidden, down_w, preferred_element_type=jnp.float32)  16.6 us
  transfers between devices with their start and end apart: 26, of which 13 were waited for; matrix products, arithmetic and copies ran while one was open for 29% of the time, Pallas kernels for 3%

profile of v3, /device:TPU:0, one launch (start us, length us, event | category | flops | bytes accessed | tf_op | source)
XLA Modules:
  0.0 523.0 jit_solution(4598048390461468743)
XLA Ops:
  19.3 89.8 %gather_weights.1 = (bf16[4,256,3072]{2,1,0:T(8,128)(2,1)}, bf16[4,256,1024]{2,1,0:T(8,128)(2,1)}, bf16[4,256,4096]{2,1,0:T(8,128)(2,1)}, bf16[4,1024,1024]{2,1,0:T(8,128)(2,1)}) custom-call(bf16[256,3072]{1,0:T(8,128)(2,1)} %bitcast.192, bf16[256,1024]{1,0:T(8,128)(2,1)} %bitcast.193, bf16[256,4096]{1,0:T(8,128)(2,1)} %bitcast.190, bf16[1024,1024]{1,0:T(8,128)(2,1)} %bitcast.191), custom_call_target="tpu_custom_call" | custom-call | tf_op jit(solution)/shard_map/gather_weights/pallas_call | solution.py:409
  129.2 7.4 %attend.2 = bf16[128,1024]{1,0:T(8,128)(2,1)} custom-call(bf16[128,1024]{1,0:T(8,128)(2,1)} %fusion.94.query_ref, bf16[128,2048]{1,0:T(8,128)(2,1)} %fusion.32.own_ref, bf16[1,128,2048]{2,1,0:T(8,128)(2,1)} %bitcast.15.halo_ref, f32[2,64,128]{2,1,0:T(8,128)} %and_select_fusion.bias_ref), custom_call_target="tpu_custom_call" | custom-call | flops 1000000000 | bytes 10000000 | tf_op jit(solution)/shard_map/attend/pallas_call | solution.py:151
  138.3 10.5 %fusion.90 = bf16[128,1024]{1,0:T(8,128)(2,1)S(1)} fusion(f32[128,1024]{1,0:T(8,128)S(1)} %get-tuple-element.93, bf16[4096,1024]{1,0:T(8,128)(2,1)} %bitcast.178, bf16[1024,4096]{1,0:T(8,128)(2,1)} %bitcast.166, f32[4096]{0:T(1024)S(1)} %bitcast.210, f32[1024]{0:T(1024)S(1)} %bitcast.224, f32[1024]{0:T(1024)S(1)} %bitcast.226, f32[1024]{0:T(1024)S(1)} %bitcast.205, ...), kind=kOutput, calls=%fused_computation.98 | convolution fusion | flops 2153775104 | bytes 17593344 | tf_op jit(solution)/shard_map/dot_general | solution.py:192
  162.0 16.9 %collective-permute-start.3 = (bf16[128,2048]{1,0:T(8,128)(2,1)}, bf16[128,2048]{1,0:T(8,128)(2,1)}, u32[]{:S(2)}, u32[]{:S(2)}) collective-permute-start(bf16[128,2048]{1,0:T(8,128)(2,1)} %fusion.29.own_ref), channel_id=1, source_target_pairs={{0,4},{4,8},{8,12},{1,5},{5,9},{9,13},{2,6},{6,10},{10,14},{3,7},{... | collective-permute-start | bytes 1572872 | tf_op jit(solution)/shard_map/ppermute | solution.py:18
  182.4 7.4 %attend.3.out_ref = bf16[128,1024]{1,0:T(8,128)(2,1)} custom-call(bf16[128,1024]{1,0:T(8,128)(2,1)} %fusion.91.query_ref, bf16[128,2048]{1,0:T(8,128)(2,1)} %fusion.29.own_ref, bf16[1,128,2048]{2,1,0:T(8,128)(2,1)} %bitcast.24.halo_ref, f32[2,64,128]{2,1,0:T(8,128)} %and_select_fusion.bias_ref), custom_call_target="tpu_custom_call" | custom-call | flops 1000000000 | bytes 10000000 | tf_op jit(solution)/shard_map/attend/pallas_call | solution.py:151
  192.7 8.0 %convolution_add_fusion = f32[128,4096]{0,1:T(8,128)} fusion(bf16[128,1024]{1,0:T(8,128)(2,1)S(1)} %add_convert_fusion.5, bf16[1024,4096]{1,0:T(8,128)(2,1)} %bitcast.167, f32[4096]{0:T(1024)} %bitcast.211), kind=kOutput, calls=%fused_computation.20 | convolution fusion | flops 1074266112 | bytes 10764288 | tf_op jit(solution)/shard_map/dot_general | solution.py:190
  200.8 15.9 %multiply_reduce_fusion.5 = (f32[128]{0:T(128)S(1)}, f32[128,1024]{1,0:T(8,128)}) fusion(f32[128,1024]{1,0:T(8,128)S(1)} %get-tuple-element.95, f32[128]{0:T(128)S(1)} %copy-done.25, f32[1024]{0:T(1024)S(1)} %bitcast.207, bf16[1024,4096]{1,0:T(8,128)(2,1)} %bitcast.168, f32[128,4096]{0,1:T(8,128)} %convolution_add_fusion, ...), kind=kOutput, calls=%fused_computation.172 | convolution fusion | flops 2158493696 | bytes 20190208 | tf_op jit(solution)/shard_map/rf,df->rd/dot_general | solution.py:206
  220.9 9.0 %attend_grad.2 = (bf16[128,1024]{1,0:T(8,128)(2,1)}, f32[128,2048]{1,0:T(8,128)}, bf16[1,128,2048]{2,1,0:T(8,128)(2,1)}) custom-call(bf16[128,1024]{1,0:T(8,128)(2,1)} %fusion.91.query_ref, bf16[128,2048]{1,0:T(8,128)(2,1)} %fusion.29.own_ref, bf16[1,128,2048]{2,1,0:T(8,128)(2,1)} %bitcast.24.halo_ref, f32[2,64,128]{2,1,0:T(8,128)} %and_select_fusion.bias_ref, ...), custom_call_target="tpu_custom_call" | custom-call | flops 1000000000 | bytes 10000000 | tf_op jit(solution)/shard_map/attend_grad/pallas_call | solution.py:162
  235.0 9.3 %collective-permute-done.4 = bf16[128,2048]{1,0:T(8,128)(2,1)} collective-permute-done((bf16[128,2048]{1,0:T(8,128)(2,1)}, bf16[128,2048]{1,0:T(8,128)(2,1)}, u32[]{:S(2)}, u32[]{:S(2)}) %collective-permute-start.4) | collective-permute-done | bytes 524320 | tf_op jit(solution)/shard_map/ppermute | solution.py:18
  253.2 7.0 %collective-permute-done.5 = bf16[2,64,1024]{2,1,0:T(8,128)(2,1)S(1)} collective-permute-done((bf16[2,64,1024]{2,1,0:T(8,128)(2,1)S(1)}, bf16[2,64,1024]{2,1,0:T(8,128)(2,1)S(1)}, u32[]{:S(2)}, u32[]{:S(2)}) %collective-permute-start.5) | collective-permute-done | bytes 262176 | tf_op jit(solution)/shard_map/ppermute | solution.py:18
  260.3 7.2 %fusion.176 = (f32[4096]{0:T(1024)S(1)}, bf16[128,4096]{0,1:T(8,128)(2,1)S(1)}) fusion(f32[128,4096]{0,1:T(8,128)} %convolution_add_fusion, bf16[128,1024]{1,0:T(8,128)(2,1)S(1)} %bitcast.188, bf16[4096,1024]{1,0:T(8,128)(2,1)} %bitcast.180), kind=kOutput, calls=%fused_computation.270 | convolution fusion | flops 1084747776 | bytes 11812864 | tf_op jit(solution)/shard_map/rd,fd->rf/dot_general | solution.py:203
  267.6 6.5 %multiply_reduce_fusion = (f32[1024]{0:T(1024)S(1)}, f32[128]{0:T(128)S(1)}, f32[1024]{0:T(1024)S(1)}, f32[128,1024]{1,0:T(8,128)S(1)}) fusion(f32[128,1024]{1,0:T(8,128)S(1)} %get-tuple-element.95, f32[128]{0:T(128)S(1)} %copy-done.32, f32[128]{0:T(128)S(1)} %copy-done.25, f32[1024]{0:T(1024)S(1)} %bitcast.208, bf16[1024,4096]{1,0:T(8,128)(2,1)} %bitcast.169, ...), kind=kOutput, calls=%fused_computation.162 | convolution fusion | flops 1074788224 | bytes 10499584 | tf_op jit(solution)/shard_map/rf,df->rd/dot_general | solution.py:206
  275.1 7.9 %all-gather.9.cloned.1.call-done = bf16[2,512,1024]{2,1,0:T(8,128)(2,1)} async-done(((bf16[2,128,1024]{2,1,0:T(8,128)(2,1)}), bf16[2,512,1024]{2,1,0:T(8,128)(2,1)}) %all-gather.9.cloned.1.call-update) | async-done | bytes 2097168 | tf_op jit(solution)/shard_map/all_gather | solution.py:245
  286.5 9.0 %attend_grad.3 = (bf16[128,1024]{1,0:T(8,128)(2,1)}, f32[128,2048]{1,0:T(8,128)}, bf16[1,128,2048]{2,1,0:T(8,128)(2,1)}) custom-call(bf16[128,1024]{1,0:T(8,128)(2,1)} %fusion.91.query_ref, bf16[128,2048]{1,0:T(8,128)(2,1)} %fusion.29.own_ref, bf16[1,128,2048]{2,1,0:T(8,128)(2,1)} %bitcast.24.halo_ref, f32[2,64,128]{2,1,0:T(8,128)} %and_select_fusion.bias_ref, ...), custom_call_target="tpu_custom_call" | custom-call | flops 1000000000 | bytes 10000000 | tf_op jit(solution)/shard_map/attend_grad/pallas_call | solution.py:162
  296.8 24.8 %collective-permute-done.6 = bf16[128,2048]{1,0:T(8,128)(2,1)S(1)} collective-permute-done((bf16[128,2048]{1,0:T(8,128)(2,1)}, bf16[128,2048]{1,0:T(8,128)(2,1)S(1)}, u32[]{:S(2)}, u32[]{:S(2)}) %collective-permute-start.6) | collective-permute-done | bytes 524320 | tf_op jit(solution)/shard_map/ppermute | solution.py:18
  337.3 16.0 %collective-permute-done.8 = bf16[512,1024]{1,0:T(8,128)(2,1)} collective-permute-done((bf16[512,1024]{1,0:T(8,128)(2,1)}, bf16[512,1024]{1,0:T(8,128)(2,1)}, u32[]{:S(2)}, u32[]{:S(2)}) %collective-permute-start.8) | collective-permute-done | bytes 1048608 | tf_op jit(solution)/shard_map/ppermute | solution.py:241
  362.4 6.4 %collective-permute-done.19 = f32[96,128]{1,0:T(8,128)S(1)} collective-permute-done((f32[96,128]{1,0:T(8,128)S(1)}, f32[96,128]{1,0:T(8,128)S(1)}, u32[]{:S(2)}, u32[]{:S(2)}) %collective-permute-start.19) | collective-permute-done | bytes 49184 | tf_op jit(solution)/shard_map/ppermute | solution.py:303
  381.4 13.1 %collective-permute-done.10 = bf16[512,1024]{1,0:T(8,128)(2,1)} collective-permute-done((bf16[512,1024]{1,0:T(8,128)(2,1)}, bf16[512,1024]{1,0:T(8,128)(2,1)}, u32[]{:S(2)}, u32[]{:S(2)}) %collective-permute-start.10) | collective-permute-done | bytes 1048608 | tf_op jit(solution)/shard_map/ppermute | solution.py:241
  404.1 7.2 %fusion.53 = f32[2048,1024]{1,0:T(8,128)} fusion(bf16[2048,1024]{1,0:T(8,128)(2,1)S(1)} %constant_dynamic-update-slice_fusion, bf16[1024,4096]{1,0:T(8,128)(2,1)S(1)} %bitcast.173, s32[]{:T(128)S(6)} %select_n.86), kind=kOutput, calls=%fused_computation.62 | convolution fusion | flops 4294967296 | bytes 14680068 | tf_op jit(solution)/shard_map/dot_general | solution.py:265
  411.4 12.0 %fusion.13 = bf16[2048,1024]{1,0:T(8,128)(2,1)S(1)} fusion(f32[2048,1024]{1,0:T(8,128)S(1)} %fusion.47, f32[1024]{0:T(1024)S(1)} %bitcast.234, bf16[2048,1024]{1,0:T(8,128)(2,1)S(1)} %constant_dynamic-update-slice_fusion.3, bf16[4096,1024]{1,0:T(8,128)(2,1)} %bitcast.182, s32[]{:T(128)S(6)} %select_n.87), kind=kOutput, calls=%fused_computation.17 | convolution fusion | flops 4339007488 | bytes 18878468 | tf_op jit(solution)/shard_map/rd,fd->rf/dot_general | solution.py:268
  426.2 13.0 %fusion.6 = bf16[2048,1024]{1,0:T(8,128)(2,1)S(1)} fusion(f32[2048,1024]{1,0:T(8,128)} %fusion.53, f32[1024]{0:T(1024)S(1)} %bitcast.232, bf16[2048,1024]{1,0:T(8,128)(2,1)} %copy-done.20, bf16[4096,1024]{1,0:T(8,128)(2,1)} %bitcast.183, s32[]{:T(128)S(6)} %select_n.86), kind=kOutput, calls=%fused_computation.10 | convolution fusion | flops 4339007488 | bytes 18878468 | tf_op jit(solution)/shard_map/rd,fd->rf/dot_general | solution.py:268
  439.3 11.6 %fusion.14 = f32[1024,1024]{1,0:T(8,128)} fusion(bf16[2048,1024]{1,0:T(8,128)(2,1)S(1)} %copy-done.21, f32[2048,1024]{1,0:T(8,128)} %fusion.53, f32[1024]{0:T(1024)S(1)} %bitcast.233), kind=kOutput, calls=%fused_computation.22 | convolution fusion | flops 4315938816 | bytes 16781312 | tf_op jit(solution)/shard_map/rf,rd->fd/dot_general | solution.py:275
  469.3 21.9 %collective-permute-done.15 = bf16[256,2048]{1,0:T(8,128)(2,1)S(1)} collective-permute-done((bf16[256,2048]{1,0:T(8,128)(2,1)S(1)}, bf16[256,2048]{1,0:T(8,128)(2,1)S(1)}, u32[]{:S(2)}, u32[]{:S(2)}) %collective-permute-start.15) | collective-permute-done | bytes 1048608 | tf_op jit(solution)/shard_map/ppermute | solution.py:241
  491.6 21.5 %collective-permute-done.13 = bf16[256,2048]{1,0:T(8,128)(2,1)S(1)} collective-permute-done((bf16[256,2048]{1,0:T(8,128)(2,1)S(1)}, bf16[256,2048]{1,0:T(8,128)(2,1)S(1)}, u32[]{:S(2)}, u32[]{:S(2)}) %collective-permute-start.13) | collective-permute-done | bytes 1048608 | tf_op jit(solution)/shard_map/ppermute | solution.py:241
  (267 shorter events, 148.9 us)
Async XLA Ops:
  7.2 267.9 %all-gather.7.cloned.1.call-start = ((), (), s32[]{:S(2)}) async-start(), calls=%async_computation | async-start | bytes 1310720 | tf_op jit(solution)/shard_map/all_gather | solution.py:245
  112.8 16.4 %collective-permute-start = (bf16[128,2048]{1,0:T(8,128)(2,1)}, bf16[128,2048]{1,0:T(8,128)(2,1)}, u32[]{:S(2)}, u32[]{:S(2)}) collective-permute-start(bf16[128,2048]{1,0:T(8,128)(2,1)} %fusion.32.own_ref), channel_id=1, source_target_pairs={{0,4},{4,8},{8,12},{1,5},{5,9},{9,13},{2,6},{6,10},{10,14},{3,7},{... | collective-permute-start | bytes 1572872 | tf_op jit(solution)/shard_map/ppermute | solution.py:18
  117.2 11.2 %collective-permute-start.1 = (s32[2,64]{1,0:T(2,128)S(1)}, s32[2,64]{1,0:T(2,128)S(1)}, u32[]{:S(2)}, u32[]{:S(2)}) collective-permute-start(s32[2,64]{1,0:T(2,128)S(1)} %copy-done.33), channel_id=1, source_target_pairs={{0,4},{4,8},{8,12},{1,5},{5,9},{9,13},{2,6},{6,10},{10,14},{3,7},{... | collective-permute-start | bytes 1544 | tf_op jit(solution)/shard_map/ppermute | solution.py:18
  148.8 8.7 %collective-permute-start.2 = (bf16[2,64,1024]{2,1,0:T(8,128)(2,1)S(1)}, bf16[2,64,1024]{2,1,0:T(8,128)(2,1)S(1)}, u32[]{:S(2)}, u32[]{:S(2)}) collective-permute-start(bf16[2,64,1024]{2,1,0:T(8,128)(2,1)S(1)} %bitcast.250), channel_id=1, source_target_pairs={{0,16},{1,17},{2,18},{3,19},{4,20},{5,21},{6,22},{7,23},{8,24},{9,... | collective-permute-start | bytes 786440 | tf_op jit(solution)/shard_map/ppermute | solution.py:18
  162.0 20.4 %collective-permute-start.3 = (bf16[128,2048]{1,0:T(8,128)(2,1)}, bf16[128,2048]{1,0:T(8,128)(2,1)}, u32[]{:S(2)}, u32[]{:S(2)}) collective-permute-start(bf16[128,2048]{1,0:T(8,128)(2,1)} %fusion.29.own_ref), channel_id=1, source_target_pairs={{0,4},{4,8},{8,12},{1,5},{5,9},{9,13},{2,6},{6,10},{10,14},{3,7},{... | collective-permute-start | bytes 1572872 | tf_op jit(solution)/shard_map/ppermute | solution.py:18
  200.7 82.2 %all-gather.9.cloned.1.call-start = ((), (), s32[]{:S(2)}) async-start(), calls=%async_computation.1 | async-start | bytes 2621440 | tf_op jit(solution)/shard_map/all_gather | solution.py:245
  229.8 14.4 %collective-permute-start.4 = (bf16[128,2048]{1,0:T(8,128)(2,1)}, bf16[128,2048]{1,0:T(8,128)(2,1)}, u32[]{:S(2)}, u32[]{:S(2)}) collective-permute-start(bf16[128,2048]{1,0:T(8,128)(2,1)} %bitcast.248), channel_id=1, source_target_pairs={{4,0},{8,4},{12,8},{5,1},{9,5},{13,9},{6,2},{10,6},{14,10},{7,3},{... | collective-permute-start | bytes 1572872 | tf_op jit(solution)/shard_map/ppermute | solution.py:18
  234.6 134.3 %all-gather.11.cloned.1.call-start = ((), (), s32[]{:S(2)}) async-start(), calls=%async_computation.2 | async-start | bytes 1310720 | tf_op jit(solution)/shard_map/all_gather | solution.py:245
  251.9 8.3 %collective-permute-start.5 = (bf16[2,64,1024]{2,1,0:T(8,128)(2,1)S(1)}, bf16[2,64,1024]{2,1,0:T(8,128)(2,1)S(1)}, u32[]{:S(2)}, u32[]{:S(2)}) collective-permute-start(bf16[2,64,1024]{2,1,0:T(8,128)(2,1)S(1)} %bitcast.195), channel_id=1, source_target_pairs={{16,0},{17,1},{18,2},{19,3},{20,4},{21,5},{22,6},{23,7},{24,8},{25... | collective-permute-start | bytes 786440 | tf_op jit(solution)/shard_map/ppermute | solution.py:18
  283.0 142.9 %all-gather.15.cloned.1.call-start = ((), (), s32[]{:S(2)}) async-start(), calls=%async_computation.4 | async-start | bytes 2621440 | tf_op jit(solution)/shard_map/all_gather | solution.py:245
  295.5 26.1 %collective-permute-start.6 = (bf16[128,2048]{1,0:T(8,128)(2,1)}, bf16[128,2048]{1,0:T(8,128)(2,1)S(1)}, u32[]{:S(2)}, u32[]{:S(2)}) collective-permute-start(bf16[128,2048]{1,0:T(8,128)(2,1)} %bitcast.249), channel_id=1, source_target_pairs={{4,0},{8,4},{12,8},{5,1},{9,5},{13,9},{6,2},{10,6},{14,10},{7,3},{... | collective-permute-start | bytes 1572872 | tf_op jit(solution)/shard_map/ppermute | solution.py:18
  323.8 130.9 %all-gather.13.cloned.1.call-start = ((), (), s32[]{:S(2)}) async-start(), calls=%async_computation.3 | async-start | bytes 2621440 | tf_op jit(solution)/shard_map/all_gather | solution.py:245
  328.0 25.3 %collective-permute-start.8 = (bf16[512,1024]{1,0:T(8,128)(2,1)}, bf16[512,1024]{1,0:T(8,128)(2,1)}, u32[]{:S(2)}, u32[]{:S(2)}) collective-permute-start(bf16[512,1024]{1,0:T(8,128)(2,1)} %all-gather.7.cloned.1.call-done), channel_id=1, source_target_pairs={{0,2},{1,3},{2,0},{3,1},{4,6},{5,7},{6,4},{7,5},{8,10},{9,11},{10,... | collective-permute-start | bytes 3145736 | tf_op jit(solution)/shard_map/ppermute | solution.py:241
  337.2 19.2 %collective-permute-start.17 = (f32[96,128]{1,0:T(8,128)S(1)}, f32[96,128]{1,0:T(8,128)S(1)}, u32[]{:S(2)}, u32[]{:S(2)}) collective-permute-start(f32[96,128]{1,0:T(8,128)S(1)} %reshape.294), channel_id=1, source_target_pairs={{0,1},{1,0},{2,3},{3,2},{4,5},{5,4},{6,7},{7,6},{8,9},{9,8},{10,11... | collective-permute-start | bytes 147464 | tf_op jit(solution)/shard_map/ppermute | solution.py:241
  356.4 41.0 %collective-permute-start.9 = (bf16[1024,1024]{1,0:T(8,128)(2,1)}, bf16[1024,1024]{1,0:T(8,128)(2,1)}, u32[]{:S(2)}, u32[]{:S(2)}) collective-permute-start(bf16[1024,1024]{1,0:T(8,128)(2,1)} %pad_maximum_fusion), channel_id=1, source_target_pairs={{0,1},{1,0},{2,3},{3,2},{4,5},{5,4},{6,7},{7,6},{8,9},{9,8},{10,11... | collective-permute-start | bytes 6291464 | tf_op jit(solution)/shard_map/ppermute | solution.py:241
  360.6 8.1 %collective-permute-start.19 = (f32[96,128]{1,0:T(8,128)S(1)}, f32[96,128]{1,0:T(8,128)S(1)}, u32[]{:S(2)}, u32[]{:S(2)}) collective-permute-start(f32[96,128]{1,0:T(8,128)S(1)} %add.405), channel_id=1, source_target_pairs={{0,4},{4,0},{8,12},{12,8},{1,5},{5,1},{9,13},{13,9},{2,6},{6,2},{1... | collective-permute-start | bytes 147464 | tf_op jit(solution)/shard_map/ppermute | solution.py:303
  368.8 7.7 %collective-permute-start.20 = (f32[96,128]{1,0:T(8,128)S(1)}, f32[96,128]{1,0:T(8,128)S(1)}, u32[]{:S(2)}, u32[]{:S(2)}) collective-permute-start(f32[96,128]{1,0:T(8,128)S(1)} %add.406), channel_id=1, source_target_pairs={{0,8},{4,12},{8,0},{12,4},{1,9},{5,13},{9,1},{13,5},{2,10},{6,14},... | collective-permute-start | bytes 147464 | tf_op jit(solution)/shard_map/ppermute | solution.py:303
  368.9 25.6 %collective-permute-start.10 = (bf16[512,1024]{1,0:T(8,128)(2,1)}, bf16[512,1024]{1,0:T(8,128)(2,1)}, u32[]{:S(2)}, u32[]{:S(2)}) collective-permute-start(bf16[512,1024]{1,0:T(8,128)(2,1)} %all-gather.11.cloned.1.call-done), channel_id=1, source_target_pairs={{0,2},{1,3},{2,0},{3,1},{4,6},{5,7},{6,4},{7,5},{8,10},{9,11},{10,... | collective-permute-start | bytes 3145736 | tf_op jit(solution)/shard_map/ppermute | solution.py:241
  395.8 15.4 %collective-permute-start.11 = (bf16[1024,1024]{1,0:T(8,128)(2,1)S(1)}, bf16[1024,1024]{1,0:T(8,128)(2,1)S(1)}, u32[]{:S(2)}, u32[]{:S(2)}) collective-permute-start(bf16[1024,1024]{1,0:T(8,128)(2,1)S(1)} %pad_maximum_fusion.2), channel_id=1, source_target_pairs={{0,1},{1,0},{2,3},{3,2},{4,5},{5,4},{6,7},{7,6},{8,9},{9,8},{10,11... | collective-permute-start | bytes 6291464 | tf_op jit(solution)/shard_map/ppermute | solution.py:241
  425.9 36.2 %collective-permute-start.14 = (bf16[512,2048]{1,0:T(8,128)(2,1)}, bf16[512,2048]{1,0:T(8,128)(2,1)}, u32[]{:S(2)}, u32[]{:S(2)}) collective-permute-start(bf16[512,2048]{1,0:T(8,128)(2,1)} %all-gather.15.cloned.1.call-done), channel_id=1, source_target_pairs={{0,1},{1,0},{2,3},{3,2},{4,5},{5,4},{6,7},{7,6},{8,9},{9,8},{10,11... | collective-permute-start | bytes 6291464 | tf_op jit(solution)/shard_map/ppermute | solution.py:241
  454.7 12.0 %collective-permute-start.12 = (bf16[512,2048]{1,0:T(8,128)(2,1)}, bf16[512,2048]{1,0:T(8,128)(2,1)S(1)}, u32[]{:S(2)}, u32[]{:S(2)}) collective-permute-start(bf16[512,2048]{1,0:T(8,128)(2,1)} %all-gather.13.cloned.1.call-done), channel_id=1, source_target_pairs={{0,1},{1,0},{2,3},{3,2},{4,5},{5,4},{6,7},{7,6},{8,9},{9,8},{10,11... | collective-permute-start | bytes 6291464 | tf_op jit(solution)/shard_map/ppermute | solution.py:241
  456.4 12.6 %collective-permute-start.16 = (f32[256,2048]{1,0:T(8,128)S(1)}, f32[256,2048]{1,0:T(8,128)S(1)}, u32[]{:S(2)}, u32[]{:S(2)}) collective-permute-start(f32[256,2048]{1,0:T(8,128)S(1)} %pad_maximum_fusion.3), channel_id=1, source_target_pairs={{0,1},{1,0},{2,3},{3,2},{4,5},{5,4},{6,7},{7,6},{8,9},{9,8},{10,11... | collective-permute-start | bytes 6291464 | tf_op jit(solution)/shard_map/ppermute | solution.py:241
  465.1 26.1 %collective-permute-start.15 = (bf16[256,2048]{1,0:T(8,128)(2,1)S(1)}, bf16[256,2048]{1,0:T(8,128)(2,1)S(1)}, u32[]{:S(2)}, u32[]{:S(2)}) collective-permute-start(bf16[256,2048]{1,0:T(8,128)(2,1)S(1)} %slice.314), channel_id=1, source_target_pairs={{0,2},{1,3},{2,0},{3,1},{4,6},{5,7},{6,4},{7,5},{8,10},{9,11},{10,... | collective-permute-start | bytes 3145736 | tf_op jit(solution)/shard_map/ppermute | solution.py:241
  468.4 44.7 %collective-permute-start.13 = (bf16[256,2048]{1,0:T(8,128)(2,1)S(1)}, bf16[256,2048]{1,0:T(8,128)(2,1)S(1)}, u32[]{:S(2)}, u32[]{:S(2)}) collective-permute-start(bf16[256,2048]{1,0:T(8,128)(2,1)S(1)} %pad_maximum_fusion.6), channel_id=1, source_target_pairs={{0,2},{1,3},{2,0},{3,1},{4,6},{5,7},{6,4},{7,5},{8,10},{9,11},{10,... | collective-permute-start | bytes 3145736 | tf_op jit(solution)/shard_map/ppermute | solution.py:241
  (46 other events, 586.4 us)
Sparse Core Ops, SparseCore 0:
  200.8 27.6 all-gather.6
  234.7 48.2 all-gather.8
  284.5 32.4 all-gather.10
  323.9 45.5 all-gather.14
  370.9 46.0 all-gather.12

commit v4 on v3

--- a/solution.py
+++ b/solution.py
@@ -182,6 +182,8 @@
     own = jnp.dot(normed, qkv_w[:, width:], preferred_element_type=jnp.float32) + own_bias
     own = own.astype(jnp.bfloat16)
     halo = from_before(own)
+    normed_pair = own_left(normed)
+    halo, normed_pair = lax.optimization_barrier((halo, normed_pair))
     query = jnp.dot(normed, qkv_w[:, :width], preferred_element_type=jnp.float32) + vectors[1]
     query = query.astype(jnp.bfloat16)
     mixed = attend(query, own, halo, bias)
@@ -190,12 +192,13 @@
     upper_act = jnp.dot(normed_two, up_w, preferred_element_type=jnp.float32) + up_vec
     hidden = smooth_gate(upper_act).astype(jnp.bfloat16)
     output = residual + jnp.dot(hidden, down_w, preferred_element_type=jnp.float32) + vectors[5]
-    return (output, (normed, query, own, halo, mixed, residual, normed_two, upper_act))
-
-
-def backward(incoming, entry_rows, params, saved, bias):
+    saved = (normed_pair, query, own, halo, mixed, residual, normed_two, upper_act)
+    return (output, saved)
+
+
+def backward(incoming, entry_rows, params, saved, bias, beside=None):
     qkv_w, out_w, up_w, down_w, gain_vecs, vectors, up_vec = params
-    normed, query, own, halo, mixed, residual, normed_two, upper_act = saved
+    normed_pair, query, own, halo, mixed, residual, normed_two, upper_act = saved
     width = entry_rows.shape[-1]
     grad_rows = incoming.reshape(-1, width)
     upstream = grad_rows.astype(jnp.float32)
@@ -215,6 +218,8 @@
         "re,de->rd", residual_round, out_w, preferred_element_type=jnp.float32
     ).astype(jnp.bfloat16)
     query_g, own_g, halo_g = attend_grad(query, own, halo, bias, mixed, mixed_g)
+    if beside is not None:
+        query_g, halo_g, beside = lax.optimization_barrier((query_g, halo_g, beside))
     chunks = halo_g.shape[0]
     for chunk in range(chunks):
         own_g = own_g + passed_along(halo_g[chunk], "seq", chunk - chunks).astype(jnp.float32)
@@ -234,7 +239,7 @@
         ),
         up_bias_g[None],
     )
-    return (residual_g + entry_part, residual_round, query_g, own_g, vector_grads)
+    return (residual_g + entry_part, residual_round, query_g, own_g, vector_grads, beside)
 
 
 def partner(array, by):
@@ -259,21 +264,19 @@
     return blocks[0] if len(blocks) == 1 else jnp.concatenate(blocks, axis=axis)
 
 
-def feed_forward_block(all_normed_two, all_incoming, params, by):
+def feed_forward_back(all_normed_two, all_incoming, params, by):
     up_w, down_w, up_vec = params[2], params[3], params[6]
     up_part, down_part = blocks_of(up_w, (by,)), blocks_of(down_w, (by,), 0)
     upper_act = jnp.dot(all_normed_two, up_part, preferred_element_type=jnp.float32)
     upper_act = upper_act + blocks_of(up_vec[None], (by,))
     hidden_f, gate_back = jax.vjp(smooth_gate, upper_act)
     hidden_g = jnp.einsum("rd,fd->rf", all_incoming, down_part, preferred_element_type=jnp.float32)
-    upper_round = lax.optimization_barrier(gate_back(hidden_g)[0].astype(jnp.bfloat16))
-    chip_columns = blocks_of(all_normed_two, (0, 1))
-    up_g = jnp.einsum("rd,rf->df", chip_columns, upper_round, preferred_element_type=jnp.float32)
-    if by:
-        return up_g
-    hidden = hidden_f.astype(jnp.bfloat16)
-    down_g = jnp.einsum("rf,rd->fd", hidden, all_incoming, preferred_element_type=jnp.float32)
-    return (up_g, down_g)
+    return (hidden_f.astype(jnp.bfloat16), gate_back(hidden_g)[0].astype(jnp.bfloat16))
+
+
+def own_left(rows):
+    mine, theirs = blocks_of(rows, (0, 2)), blocks_of(rows, (1, 3))
+    return jnp.stack([mine, partner(theirs, 1)])
 
 
 def up_blocks(own_first, own_second, received, share):
@@ -449,41 +452,54 @@
     )
     entry_rows = jnp.where(leading, own_slot, received)
     last_output, saved = forward(entry_rows, params, bias)
-    normed, query, own, halo, mixed, residual, normed_two, upper_act = saved
-    normed_two_line = gathered_rows(normed_two)
-    mine = jnp.concatenate([blocks_of(normed, (0, 2)), blocks_of(mixed, (0, 2))], axis=1)
-    theirs = jnp.concatenate([blocks_of(normed, (1, 3)), blocks_of(mixed, (1, 3))], axis=1)
-    lefts = gathered_rows(jnp.stack([mine, partner(theirs, 1)]), 1)
+    normed_pair, query, own, halo, mixed, residual, normed_two, upper_act = saved
+    normed_left = gathered_rows(normed_pair, 1)
+    normed_two_sent, normed_left = lax.optimization_barrier((normed_two, normed_left))
+    all_normed_two = gathered_tokens(gathered_rows(normed_two_sent))
+    mixed_left = gathered_rows(own_left(mixed), 1)
     early_entry = backward(own_slot, entry_rows, params, saved, bias)[0]
     returned = passed_along(
         early_entry.astype(jnp.bfloat16).reshape(own_slot.shape), "section", -1
     )
     incoming = jnp.where(leading, returned, own_slot)
-    incoming_rows, normed_two_line, lefts = lax.optimization_barrier(
-        (incoming.reshape(-1, width), normed_two_line, lefts)
-    )
-    normed_left, mixed_left = lefts[:, :, : width // 2], lefts[:, :, width // 2 :]
-    incoming_line = gathered_rows(incoming_rows)
-    entry_g, residual_round, query_g, own_g, vector_grads = backward(
-        incoming, entry_rows, params, saved, bias
+    incoming, all_normed_two, normed_left, mixed_left = lax.optimization_barrier(
+        (incoming, all_normed_two, normed_left, mixed_left)
+    )
+    incoming_line = gathered_rows(incoming.reshape(-1, width))
+    entry_g, residual_round, query_g, own_g, vector_grads, incoming_line = backward(
+        incoming, entry_rows, params, saved, bias, incoming_line
     )
     first_line = gathered_rows(jnp.concatenate([residual_round, query_g], axis=1))
     second_line = gathered_rows(own_g)
-    all_normed_two = gathered_tokens(normed_two_line)
     all_incoming = gathered_tokens(incoming_line)
-    up_first, down_total = feed_forward_block(all_normed_two, all_incoming, params, 0)
-    up_first, down_total, first_line = lax.optimization_barrier((up_first, down_total, first_line))
+    hidden, upper_round = feed_forward_back(all_normed_two, all_incoming, params, 0)
+    upper_round, hidden, first_line = lax.optimization_barrier((upper_round, hidden, first_line))
     first_other = partner(first_line, 1)
-    up_second = feed_forward_block(all_normed_two, all_incoming, params, 2)
-    up_sent = partner(jnp.concatenate([up_first[share:], up_second[share:]], axis=1), 1)
+    chip_columns = blocks_of(all_normed_two, (0, 1))
+    down_total = jnp.einsum("rf,rd->fd", hidden, all_incoming, preferred_element_type=jnp.float32)
+    up_first = jnp.einsum(
+        "rd,rf->df", chip_columns, upper_round, preferred_element_type=jnp.float32
+    )
+    down_total, first_other = lax.optimization_barrier((down_total, first_other))
     out_g = product(mixed_left, first_line[:, :width], first_other[:, :width])
     query_wg = product(normed_left, first_line[:, width:], first_other[:, width:])
     first_sent = jnp.concatenate([out_g[share:], query_wg[share:]], axis=1).astype(jnp.bfloat16)
+    vectors_g = jnp.concatenate([by_owner(part, outer) for part in vector_grads], axis=1)
+    first_sent, later_incoming, vectors_g = lax.optimization_barrier(
+        (first_sent, all_incoming, vectors_g)
+    )
     first_sent = partner(first_sent, 2)
-    up_second, second_line = lax.optimization_barrier((up_second, second_line))
+    upper_round = feed_forward_back(all_normed_two, later_incoming, params, 2)[1]
+    upper_round, second_line, first_sent = lax.optimization_barrier(
+        (upper_round, second_line, first_sent)
+    )
     second_other = partner(second_line, 1)
+    up_second = jnp.einsum(
+        "rd,rf->df", chip_columns, upper_round, preferred_element_type=jnp.float32
+    )
     own_wg = product(normed_left, second_line, second_other)
     second_sent = partner(own_wg[share:].astype(jnp.bfloat16), 2)
+    up_sent = partner(jnp.concatenate([up_first[share:], up_second[share:]], axis=1), 1)
     out_total = out_g[:share] + first_sent[:, :width].astype(jnp.float32)
     qkv_total = jnp.concatenate(
         [
@@ -493,7 +509,6 @@
         axis=1,
     )
     up_total = up_blocks(up_first, up_second, up_sent, share)
-    vectors_g = jnp.concatenate([by_owner(part, outer) for part in vector_grads], axis=1)
     summed = summed_shares(vectors_g.reshape(-1, 128)).reshape(outer, -1)
     own_vectors = lax.dynamic_index_in_dim(summed, lax.axis_index("dp"), 0, keepdims=False)
     gains_total = own_vectors[: gain_count * share].reshape(gain_count, share)

time: 532 us -> 536 us (level)
  waiting for transfers between devices: 141 us -> 115 us
  matrix products: 149 us -> 168 us
  starting transfers between devices: 41.9 us -> 30.3 us
  Pallas kernels: 122 us -> 133 us
  local copies, waits for them, and re-layouts: 18.9 us -> 25.3 us
    ppermute x12 -> x13, waiting for transfers between devices: 75.6 us -> 36.4 us  [partner(): lax.ppermute(array, 'dp', [(i, i ^ by) for i in range(lax.axis_size('dp'))])]
    all_gather x5 -> x6, waiting for transfers between devices: 7.94 us -> 32 us  [gathered_rows(): return lax.all_gather(values, 'seq', axis=axis, tiled=True)]
    dot_general x7, matrix products: 54.4 us -> 67.9 us  [the longest x2 28.1 us: feed_forward_back(): jnp.einsum('rd,fd->rf', all_incoming, down_part, preferred_element_type=j...]
    ppermute x7, starting transfers between devices: 31.3 us -> 19.8 us  [passed_along(): return lax.ppermute(array, axis, pairs)]
    pallas_call x2, Pallas kernels: 18 us -> 28.3 us  [attend_grad(): pl.pallas_call(attend_grad_kernel, out_shape=(jax.ShapeDtypeStruct(query....]
    ppermute x7, waiting for transfers between devices: 51.3 us -> 44.7 us  [passed_along(): return lax.ppermute(array, axis, pairs)]
    dynamic_update_slice x4, local copies, waits for them, and re-layouts: 0.4 us -> 6.73 us  [up_blocks(): lax.dynamic_update_slice_in_dim(total, part, (index ^ by) * columns, 1)]
  transfers between devices with their start and end apart: 26 -> 28, of which waited for: 13 -> 15; matrix products, arithmetic and copies ran while one was open for 29% -> 35% of each run, Pallas kernels for 3% -> 7%
where the time goes in v4:
time: 536 us; the launch traced here: 527 us
  matrix products  168 us (31%)
  Pallas kernels  133 us (25%)
  waiting for transfers between devices  115 us (21%)
  other arithmetic  33 us (6%)
  starting transfers between devices  30.3 us (6%)
  local copies, waits for them, and re-layouts  25.3 us (5%)
  between operations  15.3 us (3%)
  blocking collectives  6.25 us (1%)
    pallas_call x1, Pallas kernels, gathered_weights(): pl.pallas_call(lambda *refs: gather_kernel(plan, count, *refs), out_shape...  89.8 us
    ppermute x7, waiting for transfers between devices, passed_along(): return lax.ppermute(array, axis, pairs)  44.7 us
    ppermute x13, waiting for transfers between devices, partner(): lax.ppermute(array, 'dp', [(i, i ^ by) for i in range(lax.axis_size('dp'))])  36.4 us
    all_gather x6, waiting for transfers between devices, gathered_rows(): return lax.all_gather(values, 'seq', axis=axis, tiled=True)  32 us
    pallas_call x2, Pallas kernels, attend_grad(): pl.pallas_call(attend_grad_kernel, out_shape=(jax.ShapeDtypeStruct(query....  28.3 us
    dot_general x2, matrix products, feed_forward_back(): jnp.einsum('rd,fd->rf', all_incoming, down_part, preferred_element_type=j...  28.1 us
    dot_general x2, matrix products, backward(): jnp.einsum('rf,df->rd', upper_g.astype(jnp.bfloat16), up_w, preferred_ele...  22.8 us
    dot_general x2, matrix products, feed_forward_back(): jnp.dot(all_normed_two, up_part, preferred_element_type=jnp.float32)  22.6 us
  transfers between devices with their start and end apart: 28, of which 15 were waited for; matrix products, arithmetic and copies ran while one was open for 35% of the time, Pallas kernels for 7%

profile of v4, /device:TPU:0, one launch (start us, length us, event | category | flops | bytes accessed | tf_op | source)
XLA Modules:
  0.0 526.6 jit_solution(360334828731498673)
XLA Ops:
  9.3 6.2 %all-gather = bf16[12288]{0:T(1024)(128)(2,1)S(1)} all-gather(bf16[3072]{0:T(1024)(128)(2,1)S(1)} %pad_maximum_fusion.14), channel_id=2, replica_groups=mesh['section'=2,'seq'=4,'dp'=4] {'dp'}, dimensions={0}, use_global_device_ids=true | all-gather | bytes 30720 | tf_op jit(solution)/shard_map/all_gather | solution.py:434
  19.3 89.8 %gather_weights.1 = (bf16[4,256,3072]{2,1,0:T(8,128)(2,1)}, bf16[4,256,1024]{2,1,0:T(8,128)(2,1)}, bf16[4,256,4096]{2,1,0:T(8,128)(2,1)}, bf16[4,1024,1024]{2,1,0:T(8,128)(2,1)}) custom-call(bf16[256,3072]{1,0:T(8,128)(2,1)} %bitcast.199, bf16[256,1024]{1,0:T(8,128)(2,1)} %bitcast.200, bf16[256,4096]{1,0:T(8,128)(2,1)} %bitcast.197, bf16[1024,1024]{1,0:T(8,128)(2,1)} %bitcast.198), custom_call_target="tpu_custom_call" | custom-call | tf_op jit(solution)/shard_map/gather_weights/pallas_call | solution.py:412
  129.2 7.4 %attend.2 = bf16[128,1024]{1,0:T(8,128)(2,1)} custom-call(bf16[128,1024]{1,0:T(8,128)(2,1)} %fusion.94.query_ref, bf16[128,2048]{1,0:T(8,128)(2,1)} %fusion.31.own_ref, bf16[1,128,2048]{2,1,0:T(8,128)(2,1)} %bitcast.15.halo_ref, f32[2,64,128]{2,1,0:T(8,128)} %and_select_fusion.bias_ref), custom_call_target="tpu_custom_call" | custom-call | flops 1000000000 | bytes 10000000 | tf_op jit(solution)/shard_map/attend/pallas_call | solution.py:151
  138.3 10.5 %fusion.90 = bf16[128,1024]{1,0:T(8,128)(2,1)S(1)} fusion(f32[128,1024]{1,0:T(8,128)S(1)} %get-tuple-element.119, bf16[4096,1024]{1,0:T(8,128)(2,1)} %bitcast.183, bf16[1024,4096]{1,0:T(8,128)(2,1)} %bitcast.173, f32[4096]{0:T(1024)S(1)} %bitcast.218, f32[1024]{0:T(1024)S(1)} %bitcast.232, f32[1024]{0:T(1024)S(1)} %bitcast.234, f32[1024]{0:T(1024)S(1)} %bitcast.213, ...), kind=kOutput, calls=%fused_computation.99 | convolution fusion | flops 2153775104 | bytes 17593344 | tf_op jit(solution)/shard_map/dot_general | solution.py:194
  169.4 7.4 %collective-permute-done.3 = bf16[128,2048]{1,0:T(8,128)(2,1)} collective-permute-done((bf16[128,2048]{1,0:T(8,128)(2,1)}, bf16[128,2048]{1,0:T(8,128)(2,1)}, u32[]{:S(2)}, u32[]{:S(2)}) %collective-permute-start.3) | collective-permute-done | bytes 524320 | tf_op jit(solution)/shard_map/ppermute | solution.py:18
  179.8 7.4 %attend.3.out_ref = bf16[128,1024]{1,0:T(8,128)(2,1)} custom-call(bf16[128,1024]{1,0:T(8,128)(2,1)} %fusion.91.query_ref, bf16[128,2048]{1,0:T(8,128)(2,1)} %fusion.28.own_ref, bf16[1,128,2048]{2,1,0:T(8,128)(2,1)} %bitcast.24.halo_ref, f32[2,64,128]{2,1,0:T(8,128)} %and_select_fusion.bias_ref), custom_call_target="tpu_custom_call" | custom-call | flops 1000000000 | bytes 10000000 | tf_op jit(solution)/shard_map/attend/pallas_call | solution.py:151
  189.8 17.4 %all-gather.8.cloned.1.call-done = bf16[2,512,512]{2,1,0:T(8,128)(2,1)} async-done(((bf16[2,128,512]{2,1,0:T(8,128)(2,1)}), bf16[2,512,512]{2,1,0:T(8,128)(2,1)}) %all-gather.8.cloned.1.call-update) | async-done | bytes 1048592 | tf_op jit(solution)/shard_map/all_gather | solution.py:250
  207.2 8.0 %convolution_add_fusion = f32[128,4096]{0,1:T(8,128)} fusion(bf16[128,1024]{1,0:T(8,128)(2,1)} %add_convert_fusion.5, bf16[1024,4096]{1,0:T(8,128)(2,1)} %bitcast.174, f32[4096]{0:T(1024)S(1)} %bitcast.219), kind=kOutput, calls=%fused_computation.20 | convolution fusion | flops 1074266112 | bytes 10764288 | tf_op jit(solution)/shard_map/dot_general | solution.py:192
  215.2 16.0 %multiply_reduce_fusion.5 = (f32[128]{0:T(128)S(1)}, f32[128,1024]{1,0:T(8,128)}) fusion(f32[128,1024]{1,0:T(8,128)S(1)} %get-tuple-element.121, f32[128]{0:T(128)S(1)} %broadcast_multiply_fusion.2, f32[1024]{0:T(1024)S(1)} %bitcast.215, bf16[1024,4096]{1,0:T(8,128)(2,1)} %bitcast.175, f32[128,4096]{0,1:T(8,128)} %convolution_add_fusion, ...), kind=kOutput, calls=%fused_computation.173 | convolution fusion | flops 2158493696 | bytes 20190208 | tf_op jit(solution)/shard_map/rf,df->rd/dot_general | solution.py:209
  241.9 19.3 %attend_grad.2 = (bf16[128,1024]{1,0:T(8,128)(2,1)}, f32[128,2048]{1,0:T(8,128)}, bf16[1,128,2048]{2,1,0:T(8,128)(2,1)}) custom-call(bf16[128,1024]{1,0:T(8,128)(2,1)} %fusion.91.query_ref, bf16[128,2048]{1,0:T(8,128)(2,1)} %fusion.28.own_ref, bf16[1,128,2048]{2,1,0:T(8,128)(2,1)} %bitcast.24.halo_ref, f32[2,64,128]{2,1,0:T(8,128)} %and_select_fusion.bias_ref, ...), custom_call_target="tpu_custom_call" | custom-call | flops 1000000000 | bytes 10000000 | tf_op jit(solution)/shard_map/attend_grad/pallas_call | solution.py:162
  270.4 6.0 %collective-permute-done.5 = bf16[128,2048]{1,0:T(8,128)(2,1)} collective-permute-done((bf16[128,2048]{1,0:T(8,128)(2,1)}, bf16[128,2048]{1,0:T(8,128)(2,1)}, u32[]{:S(2)}, u32[]{:S(2)}) %collective-permute-start.5) | collective-permute-done | bytes 524320 | tf_op jit(solution)/shard_map/ppermute | solution.py:18
  282.9 7.0 %collective-permute-done.6 = bf16[2,64,1024]{2,1,0:T(8,128)(2,1)} collective-permute-done((bf16[2,64,1024]{2,1,0:T(8,128)(2,1)S(1)}, bf16[2,64,1024]{2,1,0:T(8,128)(2,1)}, u32[]{:S(2)}, u32[]{:S(2)}) %collective-permute-start.6) | collective-permute-done | bytes 262176 | tf_op jit(solution)/shard_map/ppermute | solution.py:18
  299.8 8.0 %fusion.174 = (f32[4096]{0:T(1024)S(1)}, bf16[128,4096]{0,1:T(8,128)(2,1)}) fusion(f32[128,4096]{0,1:T(8,128)} %convolution_add_fusion, bf16[128,1024]{1,0:T(8,128)(2,1)S(1)} %bitcast.195, bf16[4096,1024]{1,0:T(8,128)(2,1)} %bitcast.185), kind=kOutput, calls=%fused_computation.268 | convolution fusion | flops 1084747776 | bytes 11812864 | tf_op jit(solution)/shard_map/rd,fd->rf/dot_general | solution.py:206
  307.9 6.8 %multiply_reduce_fusion = (f32[1024]{0:T(1024)S(1)}, f32[128]{0:T(128)S(1)}, f32[1024]{0:T(1024)S(1)}, f32[128,1024]{1,0:T(8,128)S(1)}) fusion(f32[128,1024]{1,0:T(8,128)S(1)} %get-tuple-element.121, f32[128]{0:T(128)S(1)} %fusion.155, f32[128]{0:T(128)S(1)} %broadcast_multiply_fusion.2, f32[1024]{0:T(1024)S(1)} %bitcast.216, ...), kind=kOutput, calls=%fused_computation.164 | convolution fusion | flops 1074788224 | bytes 10499584 | tf_op jit(solution)/shard_map/rf,df->rd/dot_general | solution.py:209
  318.3 9.0 %attend_grad.3 = (bf16[128,1024]{1,0:T(8,128)(2,1)}, f32[128,2048]{1,0:T(8,128)}, bf16[1,128,2048]{2,1,0:T(8,128)(2,1)}) custom-call(bf16[128,1024]{1,0:T(8,128)(2,1)} %fusion.91.query_ref, bf16[128,2048]{1,0:T(8,128)(2,1)} %fusion.28.own_ref, bf16[1,128,2048]{2,1,0:T(8,128)(2,1)} %bitcast.24.halo_ref, f32[2,64,128]{2,1,0:T(8,128)} %and_select_fusion.bias_ref, ...), custom_call_target="tpu_custom_call" | custom-call | flops 1000000000 | bytes 10000000 | tf_op jit(solution)/shard_map/attend_grad/pallas_call | solution.py:162
  336.7 14.3 %multiply_convert_fusion = (bf16[2048,1024]{1,0:T(8,128)(2,1)}, f32[2048,1024]{1,0:T(8,128)}) fusion(f32[1024]{0:T(1024)S(1)} %bitcast.243, bf16[2048,1024]{1,0:T(8,128)(2,1)} %pad_maximum_fusion, bf16[1024,4096]{1,0:T(8,128)(2,1)} %bitcast.177, s32[]{:T(128)S(6)} %select_n.88), kind=kOutput, calls=%fused_computation.18 | convolution fusion | flops 4315938816 | bytes 18878468 | tf_op jit(solution)/shard_map/dot_general | solution.py:270
  352.4 8.3 %fusion.46 = f32[2048,1024]{1,0:T(8,128)} fusion(bf16[2048,1024]{1,0:T(8,128)(2,1)S(1)} %copy-done.3, bf16[1024,4096]{1,0:T(8,128)(2,1)} %bitcast.178, s32[]{:T(128)S(6)} %select_n.89), kind=kOutput, calls=%fused_computation.58 | convolution fusion | flops 4294967296 | bytes 14680068 | tf_op jit(solution)/shard_map/dot_general | solution.py:270
  365.4 10.1 %collective-permute-done.11 = bf16[512,1024]{1,0:T(8,128)(2,1)S(1)} collective-permute-done((bf16[512,1024]{1,0:T(8,128)(2,1)S(1)}, bf16[512,1024]{1,0:T(8,128)(2,1)S(1)}, u32[]{:S(2)}, u32[]{:S(2)}) %collective-permute-start.11) | collective-permute-done | bytes 1048608 | tf_op jit(solution)/shard_map/ppermute | solution.py:246
  378.1 13.5 %collective-permute-done.10 = bf16[128,2048]{1,0:T(8,128)(2,1)S(1)} collective-permute-done((bf16[128,2048]{1,0:T(8,128)(2,1)S(1)}, bf16[128,2048]{1,0:T(8,128)(2,1)S(1)}, u32[]{:S(2)}, u32[]{:S(2)}) %collective-permute-start.10) | collective-permute-done | bytes 524320 | tf_op jit(solution)/shard_map/ppermute | solution.py:18
  402.7 13.8 %fusion.6 = bf16[2048,1024]{1,0:T(8,128)(2,1)} fusion(f32[2048,1024]{1,0:T(8,128)} %get-tuple-element.129, f32[1024]{0:T(1024)S(1)} %bitcast.244, bf16[2048,1024]{1,0:T(8,128)(2,1)S(1)} %constant_dynamic-update-slice_fusion, bf16[4096,1024]{1,0:T(8,128)(2,1)} %bitcast.186, s32[]{:T(128)S(6)} %select_n.88), kind=kOutput, calls=%fused_computation.10 | convolution fusion | flops 4339007488 | bytes 18878468 | tf_op jit(solution)/shard_map/rd,fd->rf/dot_general | solution.py:273
  418.6 10.2 %fusion.182 = f32[1024,1024]{1,0:T(8,128)} fusion(bf16[2048,1024]{1,0:T(8,128)(2,1)} %get-tuple-element.61, bf16[2048,1024]{1,0:T(8,128)(2,1)} %copy-done.29), kind=kOutput, calls=%fused_computation.276 | convolution fusion | flops 4294967296 | bytes 12582912 | tf_op jit(solution)/shard_map/rf,rd->fd/dot_general | solution.py:479
  438.5 14.3 %fusion.13 = bf16[2048,1024]{1,0:T(8,128)(2,1)} fusion(f32[2048,1024]{1,0:T(8,128)} %fusion.46, f32[1024]{0:T(1024)S(1)} %bitcast.240, bf16[2048,1024]{1,0:T(8,128)(2,1)} %copy-done.29, bf16[4096,1024]{1,0:T(8,128)(2,1)} %bitcast.187, s32[]{:T(128)S(6)} %select_n.89), kind=kOutput, calls=%fused_computation.17 | convolution fusion | flops 4339007488 | bytes 18878468 | tf_op jit(solution)/shard_map/rd,fd->rf/dot_general | solution.py:273
  453.5 9.6 %collective-permute-done.14 = bf16[256,2048]{1,0:T(8,128)(2,1)} collective-permute-done((bf16[256,2048]{1,0:T(8,128)(2,1)}, bf16[256,2048]{1,0:T(8,128)(2,1)}, u32[]{:S(2)}, u32[]{:S(2)}) %collective-permute-start.14) | collective-permute-done | bytes 1048608 | tf_op jit(solution)/shard_map/ppermute | solution.py:246
  501.7 15.4 %collective-permute-done.16 = bf16[256,2048]{1,0:T(8,128)(2,1)S(1)} collective-permute-done((bf16[256,2048]{1,0:T(8,128)(2,1)S(1)}, bf16[256,2048]{1,0:T(8,128)(2,1)S(1)}, u32[]{:S(2)}, u32[]{:S(2)}) %collective-permute-start.16) | collective-permute-done | bytes 1048608 | tf_op jit(solution)/shard_map/ppermute | solution.py:246
  (258 shorter events, 175.8 us)
Async XLA Ops:
  7.2 200.0 %all-gather.8.cloned.1.call-start = ((), (), s32[]{:S(2)}) async-start(), calls=%async_computation | async-start | bytes 1310720 | tf_op jit(solution)/shard_map/all_gather | solution.py:250
  112.8 16.4 %collective-permute-start = (bf16[128,2048]{1,0:T(8,128)(2,1)}, bf16[128,2048]{1,0:T(8,128)(2,1)}, u32[]{:S(2)}, u32[]{:S(2)}) collective-permute-start(bf16[128,2048]{1,0:T(8,128)(2,1)} %fusion.31.own_ref), channel_id=1, source_target_pairs={{0,4},{4,8},{8,12},{1,5},{5,9},{9,13},{2,6},{6,10},{10,14},{3,7},{... | collective-permute-start | bytes 1572872 | tf_op jit(solution)/shard_map/ppermute | solution.py:18
  117.1 11.3 %collective-permute-start.1 = (s32[2,64]{1,0:T(2,128)S(1)}, s32[2,64]{1,0:T(2,128)S(1)}, u32[]{:S(2)}, u32[]{:S(2)}) collective-permute-start(s32[2,64]{1,0:T(2,128)S(1)} %copy-done.30), channel_id=1, source_target_pairs={{0,4},{4,8},{8,12},{1,5},{5,9},{9,13},{2,6},{6,10},{10,14},{3,7},{... | collective-permute-start | bytes 1544 | tf_op jit(solution)/shard_map/ppermute | solution.py:18
  148.8 8.7 %collective-permute-start.2 = (bf16[2,64,1024]{2,1,0:T(8,128)(2,1)S(1)}, bf16[2,64,1024]{2,1,0:T(8,128)(2,1)S(1)}, u32[]{:S(2)}, u32[]{:S(2)}) collective-permute-start(bf16[2,64,1024]{2,1,0:T(8,128)(2,1)S(1)} %bitcast.258), channel_id=1, source_target_pairs={{0,16},{1,17},{2,18},{3,19},{4,20},{5,21},{6,22},{7,23},{8,24},{9,... | collective-permute-start | bytes 786440 | tf_op jit(solution)/shard_map/ppermute | solution.py:18
  162.0 14.8 %collective-permute-start.3 = (bf16[128,2048]{1,0:T(8,128)(2,1)}, bf16[128,2048]{1,0:T(8,128)(2,1)}, u32[]{:S(2)}, u32[]{:S(2)}) collective-permute-start(bf16[128,2048]{1,0:T(8,128)(2,1)} %fusion.28.own_ref), channel_id=1, source_target_pairs={{0,4},{4,8},{8,12},{1,5},{5,9},{9,13},{2,6},{6,10},{10,14},{3,7},{... | collective-permute-start | bytes 1572872 | tf_op jit(solution)/shard_map/ppermute | solution.py:18
  176.8 59.9 %all-gather.10.cloned.1.call-start = ((), (), s32[]{:S(2)}) async-start(), calls=%async_computation.1 | async-start | bytes 1310720 | tf_op jit(solution)/shard_map/all_gather | solution.py:250
  207.2 92.6 %all-gather.12.cloned.1.call-start = ((), (), s32[]{:S(2)}) async-start(), calls=%async_computation.2 | async-start | bytes 1310720 | tf_op jit(solution)/shard_map/all_gather | solution.py:250
  236.7 26.1 %collective-permute-start.7 = (bf16[512,1024]{1,0:T(8,128)(2,1)}, bf16[512,1024]{1,0:T(8,128)(2,1)}, u32[]{:S(2)}, u32[]{:S(2)}) collective-permute-start(bf16[512,1024]{1,0:T(8,128)(2,1)} %all-gather.10.cloned.1.call-done), channel_id=1, source_target_pairs={{0,2},{1,3},{2,0},{3,1},{4,6},{5,7},{6,4},{7,5},{8,10},{9,11},{10,... | collective-permute-start | bytes 3145736 | tf_op jit(solution)/shard_map/ppermute | solution.py:246
  261.2 15.2 %collective-permute-start.5 = (bf16[128,2048]{1,0:T(8,128)(2,1)}, bf16[128,2048]{1,0:T(8,128)(2,1)}, u32[]{:S(2)}, u32[]{:S(2)}) collective-permute-start(bf16[128,2048]{1,0:T(8,128)(2,1)} %bitcast.257), channel_id=1, source_target_pairs={{4,0},{8,4},{12,8},{5,1},{9,5},{13,9},{6,2},{10,6},{14,10},{7,3},{... | collective-permute-start | bytes 1572872 | tf_op jit(solution)/shard_map/ppermute | solution.py:18
  265.8 25.0 %collective-permute-start.8 = (bf16[1024,1024]{1,0:T(8,128)(2,1)}, bf16[1024,1024]{1,0:T(8,128)(2,1)}, u32[]{:S(2)}, u32[]{:S(2)}) collective-permute-start(bf16[1024,1024]{1,0:T(8,128)(2,1)} %pad_maximum_fusion.1), channel_id=1, source_target_pairs={{0,1},{1,0},{2,3},{3,2},{4,5},{5,4},{6,7},{7,6},{8,9},{9,8},{10,11... | collective-permute-start | bytes 6291464 | tf_op jit(solution)/shard_map/ppermute | solution.py:246
  270.3 65.0 %all-gather.14.cloned.1.call-start = ((), (), s32[]{:S(2)}) async-start(), calls=%async_computation.3 | async-start | bytes 1310720 | tf_op jit(solution)/shard_map/all_gather | solution.py:250
  307.8 108.7 %all-gather.16.cloned.1.call-start = ((), (), s32[]{:S(2)}) async-start(), calls=%async_computation.4 | async-start | bytes 2621440 | tf_op jit(solution)/shard_map/all_gather | solution.py:250
  336.2 117.3 %all-gather.18.cloned.1.call-start = ((), (), s32[]{:S(2)}) async-start(), calls=%async_computation.5 | async-start | bytes 2621440 | tf_op jit(solution)/shard_map/all_gather | solution.py:250
  351.0 24.4 %collective-permute-start.11 = (bf16[512,1024]{1,0:T(8,128)(2,1)S(1)}, bf16[512,1024]{1,0:T(8,128)(2,1)S(1)}, u32[]{:S(2)}, u32[]{:S(2)}) collective-permute-start(bf16[512,1024]{1,0:T(8,128)(2,1)S(1)} %copy-done.15), channel_id=1, source_target_pairs={{0,2},{1,3},{2,0},{3,1},{4,6},{5,7},{6,4},{7,5},{8,10},{9,11},{10,... | collective-permute-start | bytes 3145736 | tf_op jit(solution)/shard_map/ppermute | solution.py:246
  360.7 30.8 %collective-permute-start.10 = (bf16[128,2048]{1,0:T(8,128)(2,1)S(1)}, bf16[128,2048]{1,0:T(8,128)(2,1)S(1)}, u32[]{:S(2)}, u32[]{:S(2)}) collective-permute-start(bf16[128,2048]{1,0:T(8,128)(2,1)S(1)} %bitcast.256), channel_id=1, source_target_pairs={{4,0},{8,4},{12,8},{5,1},{9,5},{13,9},{6,2},{10,6},{14,10},{7,3},{... | collective-permute-start | bytes 1572872 | tf_op jit(solution)/shard_map/ppermute | solution.py:18
  377.0 21.9 %collective-permute-start.12 = (bf16[1024,1024]{1,0:T(8,128)(2,1)}, bf16[1024,1024]{1,0:T(8,128)(2,1)}, u32[]{:S(2)}, u32[]{:S(2)}) collective-permute-start(bf16[1024,1024]{1,0:T(8,128)(2,1)} %pad_maximum_fusion.2), channel_id=1, source_target_pairs={{0,1},{1,0},{2,3},{3,2},{4,5},{5,4},{6,7},{7,6},{8,9},{9,8},{10,11... | collective-permute-start | bytes 6291464 | tf_op jit(solution)/shard_map/ppermute | solution.py:246
  416.5 13.1 %collective-permute-start.13 = (bf16[512,2048]{1,0:T(8,128)(2,1)}, bf16[512,2048]{1,0:T(8,128)(2,1)}, u32[]{:S(2)}, u32[]{:S(2)}) collective-permute-start(bf16[512,2048]{1,0:T(8,128)(2,1)} %all-gather.16.cloned.1.call-done), channel_id=1, source_target_pairs={{0,1},{1,0},{2,3},{3,2},{4,5},{5,4},{6,7},{7,6},{8,9},{9,8},{10,11... | collective-permute-start | bytes 6291464 | tf_op jit(solution)/shard_map/ppermute | solution.py:246
  436.8 26.3 %collective-permute-start.14 = (bf16[256,2048]{1,0:T(8,128)(2,1)}, bf16[256,2048]{1,0:T(8,128)(2,1)}, u32[]{:S(2)}, u32[]{:S(2)}) collective-permute-start(bf16[256,2048]{1,0:T(8,128)(2,1)} %pad_maximum_fusion.7), channel_id=1, source_target_pairs={{0,2},{1,3},{2,0},{3,1},{4,6},{5,7},{6,4},{7,5},{8,10},{9,11},{10,... | collective-permute-start | bytes 3145736 | tf_op jit(solution)/shard_map/ppermute | solution.py:246
  438.2 14.6 %collective-permute-start.18 = (f32[96,128]{1,0:T(8,128)S(1)}, f32[96,128]{1,0:T(8,128)S(1)}, u32[]{:S(2)}, u32[]{:S(2)}) collective-permute-start(f32[96,128]{1,0:T(8,128)S(1)} %reshape.294), channel_id=1, source_target_pairs={{0,1},{1,0},{2,3},{3,2},{4,5},{5,4},{6,7},{7,6},{8,9},{9,8},{10,11... | collective-permute-start | bytes 147464 | tf_op jit(solution)/shard_map/ppermute | solution.py:246
  452.8 15.1 %collective-permute-start.19 = (f32[96,128]{1,0:T(8,128)S(1)}, f32[96,128]{1,0:T(8,128)S(1)}, u32[]{:S(2)}, u32[]{:S(2)}) collective-permute-start(f32[96,128]{1,0:T(8,128)S(1)} %add.406), channel_id=1, source_target_pairs={{0,2},{1,3},{2,0},{3,1},{4,6},{5,7},{6,4},{7,5},{8,10},{9,11},{10,... | collective-permute-start | bytes 147464 | tf_op jit(solution)/shard_map/ppermute | solution.py:246
  463.1 22.8 %collective-permute-start.15 = (bf16[512,2048]{1,0:T(8,128)(2,1)}, bf16[512,2048]{1,0:T(8,128)(2,1)}, u32[]{:S(2)}, u32[]{:S(2)}) collective-permute-start(bf16[512,2048]{1,0:T(8,128)(2,1)} %all-gather.18.cloned.1.call-done), channel_id=1, source_target_pairs={{0,1},{1,0},{2,3},{3,2},{4,5},{5,4},{6,7},{7,6},{8,9},{9,8},{10,11... | collective-permute-start | bytes 6291464 | tf_op jit(solution)/shard_map/ppermute | solution.py:246
  468.0 10.3 %collective-permute-start.20 = (f32[96,128]{1,0:T(8,128)S(1)}, f32[96,128]{1,0:T(8,128)S(1)}, u32[]{:S(2)}, u32[]{:S(2)}) collective-permute-start(f32[96,128]{1,0:T(8,128)S(1)} %add.407), channel_id=1, source_target_pairs={{0,4},{4,0},{8,12},{12,8},{1,5},{5,1},{9,13},{13,9},{2,6},{6,2},{1... | collective-permute-start | bytes 147464 | tf_op jit(solution)/shard_map/ppermute | solution.py:306
  474.4 22.8 %collective-permute-start.17 = (f32[256,2048]{1,0:T(8,128)}, f32[256,2048]{1,0:T(8,128)}, u32[]{:S(2)}, u32[]{:S(2)}) collective-permute-start(f32[256,2048]{1,0:T(8,128)} %pad_maximum_fusion.4), channel_id=1, source_target_pairs={{0,1},{1,0},{2,3},{3,2},{4,5},{5,4},{6,7},{7,6},{8,9},{9,8},{10,11... | collective-permute-start | bytes 6291464 | tf_op jit(solution)/shard_map/ppermute | solution.py:246
  492.0 25.1 %collective-permute-start.16 = (bf16[256,2048]{1,0:T(8,128)(2,1)S(1)}, bf16[256,2048]{1,0:T(8,128)(2,1)S(1)}, u32[]{:S(2)}, u32[]{:S(2)}) collective-permute-start(bf16[256,2048]{1,0:T(8,128)(2,1)S(1)} %slice.311), channel_id=1, source_target_pairs={{0,2},{1,3},{2,0},{3,1},{4,6},{5,7},{6,4},{7,5},{8,10},{9,11},{10,... | collective-permute-start | bytes 3145736 | tf_op jit(solution)/shard_map/ppermute | solution.py:246
  (40 other events, 401.3 us)
Sparse Core Ops, SparseCore 0:
  176.9 30.2 all-gather.7
  209.3 27.3 all-gather.9
  270.5 29.2 all-gather.11
  307.9 27.3 all-gather.13
  336.8 50.9 all-gather.15
  392.6 46.3 all-gather.17
